TPU v7x, 128 devices: a whole 4x4x4 slice. The times are simulated.
128 devices in a mesh: stem: 8 (over y_hi, z), leaf: 8 (over x, y_lo), slab: 2 (over core).
Axes of the slice: x: 4, y: 4 (y_hi: 2, y_lo: 2; y = y_hi * 2 + y_lo), z: 4, core: 2. Of those that a mesh axis runs over, the one named last changes fastest.
Arguments:
- branch_rows: bfloat16 [131072, 2, 256], P(('stem', 'leaf', 'slab')), may hold values from -6 to 6
- first_parent: int32 [131072, 1], P(('stem', 'leaf', 'slab')), may hold values from 0 to 15; in each aligned block of 1024 rows (0 to 1023, 1024 to 2047, ...) at most 160 rows name the same one
- second_parent: int32 [131072, 1], P(('stem', 'leaf', 'slab')), may hold values from 0 to 15; in each aligned block of 1024 rows (0 to 1023, 1024 to 2047, ...) at most 160 rows name the same one
- node_first: bfloat16 [16, 2, 256, 256], P(('leaf', 'slab')), may hold values from -1.25 to 1.25
- node_second: bfloat16 [16, 2, 256, 256], P(('leaf', 'slab')), may hold values from -1.25 to 1.25
- stem_tensors: bfloat16 [8, 2, 2, 256, 256], P('stem', None, None, 'slab'), may hold values from -1.25 to 1.25
Outputs:
- amplitudes: bfloat16 [131072, 2, 256], P(('stem', 'leaf', 'slab'))
Inputs may be any that keep to these rules, and one draw needn't show every extreme that they name: `first_parent`: within the rows of one device no node is named by more than 160 rows, a bound that some block reaches of them. `second_parent`: within the rows of one device no node is named by more than 160 rows, a bound that some block reaches of them.
All inputs are finite; a program needn't handle non-finite values.
Results may differ from a plain program's by a relative error of at most 0.012.
Values may be sent and summed in bfloat16 or wider, within the bound.
No kernel may reach another device: no remote copies, remote signals or barrier semaphores. Data moves between devices by JAX's collectives and lax.ppermute only.
A program may use at most 64 MiB of HBM per device.

v0:
```python
import jax
import jax.numpy as jnp
from jax import lax
from jax.sharding import PartitionSpec as P

CAP = 160


def shifted(value, axis, steps):
    count = lax.axis_size(axis)
    pairs = [(source, (source + steps) % count) for source in range(count)]
    return lax.ppermute(value, axis, pairs)


def complex_product(row_block, matrix):
    real_part = jnp.dot(row_block[:, 0], matrix[0], preferred_element_type=jnp.float32) - jnp.dot(
        row_block[:, 1], matrix[1], preferred_element_type=jnp.float32
    )
    imag_part = jnp.dot(row_block[:, 0], matrix[1], preferred_element_type=jnp.float32) + jnp.dot(
        row_block[:, 1], matrix[0], preferred_element_type=jnp.float32
    )
    return jnp.stack([real_part, imag_part], axis=1).astype(jnp.bfloat16)


def slot_matrix(parent, node_count):
    targets = parent[:, 0]
    row_total = targets.shape[0]
    matches = (targets[:, None] == jnp.arange(node_count, dtype=jnp.int32)[None, :]).astype(
        jnp.bfloat16
    )
    positions = jnp.arange(row_total, dtype=jnp.int32)
    triangle = (positions[:, None] > positions[None, :]).astype(jnp.bfloat16)
    earlier = jnp.dot(triangle, matches, preferred_element_type=jnp.float32)
    ranking = jnp.sum(earlier * matches.astype(jnp.float32), axis=1).astype(jnp.int32)
    slot_rows = targets * CAP + ranking
    slot_count = node_count * CAP
    return (jnp.arange(slot_count, dtype=jnp.int32)[:, None] == slot_rows[None, :]).astype(
        jnp.bfloat16
    )


def dispatch(row_block, selector, node_count):
    bond = row_block.shape[2]
    flat_rows = row_block.reshape(row_block.shape[0], 2 * bond)
    buffered = jnp.dot(selector, flat_rows, preferred_element_type=jnp.float32).astype(jnp.bfloat16)
    return buffered.reshape(node_count, CAP, 2, bond)


def collect(finished, selector):
    bond = finished.shape[-1]
    flat_slots = finished.reshape(selector.shape[0], 2 * bond)
    picked = lax.dot_general(
        selector, flat_slots, (((0,), (0,)), ((), ())), preferred_element_type=jnp.float32
    )
    return picked.astype(jnp.bfloat16).reshape(selector.shape[1], 2, bond)


def owner_level(row_block, parent, tensor, node_count):
    bond = row_block.shape[2]
    selector = slot_matrix(parent, node_count)
    outgoing = dispatch(row_block, selector, node_count)
    arrived = lax.all_to_all(outgoing, ("leaf", "slab"), split_axis=0, concat_axis=0, tiled=True)
    item_count = arrived.shape[1]
    finished = complex_product(arrived.reshape(node_count * item_count, 2, bond), tensor[0])
    finished = finished.reshape(node_count, item_count, 2, bond)
    returned = lax.all_to_all(finished, ("leaf", "slab"), split_axis=0, concat_axis=0, tiled=True)
    return collect(returned, selector)


def body(branch_rows, first_parent, second_parent, node_first, node_second, stem_tensors):
    node_count = lax.axis_size("leaf") * lax.axis_size("slab")
    first = owner_level(branch_rows, first_parent, node_first, node_count)
    second = owner_level(first, second_parent, node_second, node_count)
    stem_full = lax.all_gather(stem_tensors, "slab", axis=3, tiled=True)
    stem_held = stem_full[0]
    layers = stem_held.shape[0]
    groups = lax.axis_size("stem")
    current = second
    for visit in range(groups):
        for layer_index in range(layers):
            current = complex_product(current, stem_held[layer_index])
        current = shifted(current, "stem", 1)
    return current


def solution(mesh):
    return jax.shard_map(
        body,
        mesh=mesh,
        in_specs=(
            P(("stem", "leaf", "slab"), None, None),
            P(("stem", "leaf", "slab"), None),
            P(("stem", "leaf", "slab"), None),
            P(("leaf", "slab"), None, None, None),
            P(("leaf", "slab"), None, None, None),
            P("stem", None, None, "slab", None),
        ),
        out_specs=P(("stem", "leaf", "slab"), None, None),
        check_vma=False,
    )
```

profile of v0, /device:TPU:8, one launch (start us, length us, event | category | flops | bytes accessed | tf_op | source)
XLA Modules:
  0.0 437.6 jit_solution(14428524058748208709)
XLA Ops:
  2.9 4.1 fusion.9
  7.0 3.5 reshape.93
  10.6 37.3 %all_to_all.20 = bf16[16,160,2,256]{3,2,1,0:T(2,128)(2,1)S(1)} all-to-all(bf16[16,160,2,256]{3,2,1,0:T(2,128)(2,1)S(1)} %reshape.93), channel_id=1, replica_groups=mesh['stem'=8,'leaf'=8,'slab'=2] {'leaf','slab'}, dimensions={0} | all-to-all | bytes 5242880 | tf_op jit(solution)/shard_map/all_to_all | solution.py:62
  50.4 2.4 copy.10
  53.3 2.4 copy.9
  55.8 6.0 %pad_maximum_fusion = bf16[16,160,2,256]{3,2,1,0:T(2,128)(2,1)S(1)} fusion(bf16[16,160,1,256]{3,2,1,0:T(2,128)(2,1)S(1)} %copy.10, bf16[16,160,1,256]{3,2,1,0:T(2,128)(2,1)S(1)} %copy.9), kind=kLoop, calls=%fused_computation.23 | loop fusion | flops 5242880 | bytes 5242880 | tf_op jit(solution)/shard_map/stack | solution.py:22
  61.8 36.2 %all_to_all.21 = bf16[16,160,2,256]{3,2,1,0:T(2,128)(2,1)S(1)} all-to-all(bf16[16,160,2,256]{3,2,1,0:T(2,128)(2,1)S(1)} %pad_maximum_fusion), channel_id=1, replica_groups=mesh['stem'=8,'leaf'=8,'slab'=2] {'leaf','slab'}, dimensions={0} | all-to-all | bytes 5242880 | tf_op jit(solution)/shard_map/all_to_all | solution.py:66
  98.5 7.1 %fusion.8 = bf16[2560,512]{1,0:T(8,128)(2,1)} fusion(s32[1024]{0:T(1024)S(1)} %get-tuple-element.6, bf16[2560,512]{1,0:T(8,128)(2,1)S(1)} %bitcast.274, s32[1024]{0:T(1024)S(1)} %get-tuple-element.5), kind=kOutput, calls=%fused_computation.10 | convolution fusion | flops 5375787008 | bytes 5251072 | tf_op jit(solution)/shard_map/dot_general | solution.py:45
  105.6 3.5 reshape.96
  109.2 36.0 %all_to_all.22 = bf16[16,160,2,256]{3,2,1,0:T(2,128)(2,1)S(1)} all-to-all(bf16[16,160,2,256]{3,2,1,0:T(2,128)(2,1)S(1)} %reshape.96), channel_id=1, replica_groups=mesh['stem'=8,'leaf'=8,'slab'=2] {'leaf','slab'}, dimensions={0} | all-to-all | bytes 5242880 | tf_op jit(solution)/shard_map/all_to_all | solution.py:62
  147.6 2.4 copy.13
  153.0 6.8 %pad_maximum_fusion.1 = bf16[16,160,2,256]{3,2,1,0:T(2,128)(2,1)} fusion(bf16[16,160,1,256]{3,2,1,0:T(2,128)(2,1)S(1)} %copy.13, bf16[16,160,1,256]{3,2,1,0:T(2,128)(2,1)S(1)} %copy.12), kind=kLoop, calls=%fused_computation.24 | loop fusion | flops 5242880 | bytes 5242880 | tf_op jit(solution)/shard_map/stack | solution.py:22
  159.8 5.3 %all-to-all-start.3 = ((bf16[16,160,2,256]{3,2,1,0:T(2,128)(2,1)}), bf16[16,160,2,256]{3,2,1,0:T(2,128)(2,1)S(1)}, u32[]{:S(2)}, u32[]{:S(2)}) async-start(bf16[16,160,2,256]{3,2,1,0:T(2,128)(2,1)} %pad_maximum_fusion.1), calls=%async_computation.3 | async-start | bytes 5242880 | tf_op jit(solution)/shard_map/all_to_all | solution.py:66
  165.2 10.9 %all_gather.3 = bf16[1,2,2,256,256]{4,3,2,1,0:T(8,128)(2,1)S(1)} all-gather(bf16[1,2,2,128,256]{4,3,2,1,0:T(8,128)(2,1)S(1)} %copy-done.3), channel_id=1, replica_groups=mesh['stem'=8,'leaf'=8,'slab'=2] {'slab'}, dimensions={3}, use_global_device_ids=true | all-gather | bytes 786432 | tf_op jit(solution)/shard_map/all_gather | solution.py:74
  176.0 25.1 %all-to-all-done.3 = bf16[16,160,2,256]{3,2,1,0:T(2,128)(2,1)S(1)} async-done(((bf16[16,160,2,256]{3,2,1,0:T(2,128)(2,1)}), bf16[16,160,2,256]{3,2,1,0:T(2,128)(2,1)S(1)}, u32[]{:S(2)}, u32[]{:S(2)}) %all-to-all-start.3) | async-done | bytes 2621472 | tf_op jit(solution)/shard_map/all_to_all | solution.py:66
  201.6 3.1 fusion.16
  209.4 27.5 %collective-permute-done = bf16[1024,2,256]{2,0,1:T(8,128)(2,1)S(1)} collective-permute-done((bf16[1024,2,256]{2,0,1:T(8,128)(2,1)S(1)}, bf16[1024,2,256]{2,0,1:T(8,128)(2,1)S(1)}, u32[]{:S(2)}, u32[]{:S(2)}) %collective-permute-start) | collective-permute-done | bytes 1048608 | tf_op jit(solution)/shard_map/ppermute | solution.py:12
  239.5 28.5 %collective-permute-done.1 = bf16[1024,2,256]{2,0,1:T(8,128)(2,1)S(1)} collective-permute-done((bf16[1024,2,256]{2,0,1:T(8,128)(2,1)S(1)}, bf16[1024,2,256]{2,0,1:T(8,128)(2,1)S(1)}, u32[]{:S(2)}, u32[]{:S(2)}) %collective-permute-start.1) | collective-permute-done | bytes 1048608 | tf_op jit(solution)/shard_map/ppermute | solution.py:12
  270.6 27.6 %collective-permute-done.2 = bf16[1024,2,256]{2,0,1:T(8,128)(2,1)S(1)} collective-permute-done((bf16[1024,2,256]{2,0,1:T(8,128)(2,1)S(1)}, bf16[1024,2,256]{2,0,1:T(8,128)(2,1)S(1)}, u32[]{:S(2)}, u32[]{:S(2)}) %collective-permute-start.2) | collective-permute-done | bytes 1048608 | tf_op jit(solution)/shard_map/ppermute | solution.py:12
  301.0 26.6 %collective-permute-done.3 = bf16[1024,2,256]{2,0,1:T(8,128)(2,1)S(1)} collective-permute-done((bf16[1024,2,256]{2,0,1:T(8,128)(2,1)S(1)}, bf16[1024,2,256]{2,0,1:T(8,128)(2,1)S(1)}, u32[]{:S(2)}, u32[]{:S(2)}) %collective-permute-start.3) | collective-permute-done | bytes 1048608 | tf_op jit(solution)/shard_map/ppermute | solution.py:12
  330.2 25.7 %collective-permute-done.4 = bf16[1024,2,256]{2,0,1:T(8,128)(2,1)S(1)} collective-permute-done((bf16[1024,2,256]{2,0,1:T(8,128)(2,1)S(1)}, bf16[1024,2,256]{2,0,1:T(8,128)(2,1)S(1)}, u32[]{:S(2)}, u32[]{:S(2)}) %collective-permute-start.4) | collective-permute-done | bytes 1048608 | tf_op jit(solution)/shard_map/ppermute | solution.py:12
  358.5 24.8 %collective-permute-done.5 = bf16[1024,2,256]{2,0,1:T(8,128)(2,1)S(1)} collective-permute-done((bf16[1024,2,256]{2,0,1:T(8,128)(2,1)S(1)}, bf16[1024,2,256]{2,0,1:T(8,128)(2,1)S(1)}, u32[]{:S(2)}, u32[]{:S(2)}) %collective-permute-start.5) | collective-permute-done | bytes 1048608 | tf_op jit(solution)/shard_map/ppermute | solution.py:12
  385.9 23.9 %collective-permute-done.6 = bf16[1024,2,256]{2,0,1:T(8,128)(2,1)S(1)} collective-permute-done((bf16[1024,2,256]{2,0,1:T(8,128)(2,1)S(1)}, bf16[1024,2,256]{2,0,1:T(8,128)(2,1)S(1)}, u32[]{:S(2)}, u32[]{:S(2)}) %collective-permute-start.6) | collective-permute-done | bytes 1048608 | tf_op jit(solution)/shard_map/ppermute | solution.py:12
  412.4 22.9 %collective-permute-done.7 = bf16[1024,2,256]{2,0,1:T(8,128)(2,1)S(1)} collective-permute-done((bf16[1024,2,256]{2,0,1:T(8,128)(2,1)S(1)}, bf16[1024,2,256]{2,0,1:T(8,128)(2,1)S(1)}, u32[]{:S(2)}, u32[]{:S(2)}) %collective-permute-start.7) | collective-permute-done | bytes 1048608 | tf_op jit(solution)/shard_map/ppermute | solution.py:12
  (110 shorter events, 36.9 us)
Async XLA Ops:
  0.0 2.8 copy-start.4
  0.0 2.9 copy-start.5
  0.0 2.6 copy-start
  47.9 1.0 copy-start.1
  145.1 1.0 copy-start.2
  159.8 5.3 %copy-start.3 = (bf16[1,2,2,128,256]{4,3,2,1,0:T(8,128)(2,1)S(1)}, bf16[1,2,2,128,256]{4,3,2,1,0:T(8,128)(2,1)}, u32[]{:S(2)}) copy-start(bf16[1,2,2,128,256]{4,3,2,1,0:T(8,128)(2,1)} %param.11) | copy-start | bytes 786436
  159.8 41.3 %all-to-all-start.3 = ((bf16[16,160,2,256]{3,2,1,0:T(2,128)(2,1)}), bf16[16,160,2,256]{3,2,1,0:T(2,128)(2,1)S(1)}, u32[]{:S(2)}, u32[]{:S(2)}) async-start(bf16[16,160,2,256]{3,2,1,0:T(2,128)(2,1)} %pad_maximum_fusion.1), calls=%async_computation.3 | async-start | bytes 5242880 | tf_op jit(solution)/shard_map/all_to_all | solution.py:66
  207.4 29.5 %collective-permute-start = (bf16[1024,2,256]{2,0,1:T(8,128)(2,1)S(1)}, bf16[1024,2,256]{2,0,1:T(8,128)(2,1)S(1)}, u32[]{:S(2)}, u32[]{:S(2)}) collective-permute-start(bf16[1024,2,256]{2,0,1:T(8,128)(2,1)S(1)} %pad_maximum_fusion.2), channel_id=1, source_target_pairs={{0,16},{16,32},{32,48},{48,64},{64,80},{80,96},{96,112},{112,0},{1... | collective-permute-start | bytes 3145736 | tf_op jit(solution)/shard_map/ppermute | solution.py:12
  239.4 28.5 %collective-permute-start.1 = (bf16[1024,2,256]{2,0,1:T(8,128)(2,1)S(1)}, bf16[1024,2,256]{2,0,1:T(8,128)(2,1)S(1)}, u32[]{:S(2)}, u32[]{:S(2)}) collective-permute-start(bf16[1024,2,256]{2,0,1:T(8,128)(2,1)S(1)} %pad_maximum_fusion.3), channel_id=1, source_target_pairs={{0,16},{16,32},{32,48},{48,64},{64,80},{80,96},{96,112},{112,0},{1... | collective-permute-start | bytes 3145736 | tf_op jit(solution)/shard_map/ppermute | solution.py:12
  270.5 27.7 %collective-permute-start.2 = (bf16[1024,2,256]{2,0,1:T(8,128)(2,1)S(1)}, bf16[1024,2,256]{2,0,1:T(8,128)(2,1)S(1)}, u32[]{:S(2)}, u32[]{:S(2)}) collective-permute-start(bf16[1024,2,256]{2,0,1:T(8,128)(2,1)S(1)} %pad_maximum_fusion.4), channel_id=1, source_target_pairs={{0,16},{16,32},{32,48},{48,64},{64,80},{80,96},{96,112},{112,0},{1... | collective-permute-start | bytes 3145736 | tf_op jit(solution)/shard_map/ppermute | solution.py:12
  300.7 26.9 %collective-permute-start.3 = (bf16[1024,2,256]{2,0,1:T(8,128)(2,1)S(1)}, bf16[1024,2,256]{2,0,1:T(8,128)(2,1)S(1)}, u32[]{:S(2)}, u32[]{:S(2)}) collective-permute-start(bf16[1024,2,256]{2,0,1:T(8,128)(2,1)S(1)} %pad_maximum_fusion.5), channel_id=1, source_target_pairs={{0,16},{16,32},{32,48},{48,64},{64,80},{80,96},{96,112},{112,0},{1... | collective-permute-start | bytes 3145736 | tf_op jit(solution)/shard_map/ppermute | solution.py:12
  330.1 25.8 %collective-permute-start.4 = (bf16[1024,2,256]{2,0,1:T(8,128)(2,1)S(1)}, bf16[1024,2,256]{2,0,1:T(8,128)(2,1)S(1)}, u32[]{:S(2)}, u32[]{:S(2)}) collective-permute-start(bf16[1024,2,256]{2,0,1:T(8,128)(2,1)S(1)} %pad_maximum_fusion.6), channel_id=1, source_target_pairs={{0,16},{16,32},{32,48},{48,64},{64,80},{80,96},{96,112},{112,0},{1... | collective-permute-start | bytes 3145736 | tf_op jit(solution)/shard_map/ppermute | solution.py:12
  358.4 24.9 %collective-permute-start.5 = (bf16[1024,2,256]{2,0,1:T(8,128)(2,1)S(1)}, bf16[1024,2,256]{2,0,1:T(8,128)(2,1)S(1)}, u32[]{:S(2)}, u32[]{:S(2)}) collective-permute-start(bf16[1024,2,256]{2,0,1:T(8,128)(2,1)S(1)} %pad_maximum_fusion.7), channel_id=1, source_target_pairs={{0,16},{16,32},{32,48},{48,64},{64,80},{80,96},{96,112},{112,0},{1... | collective-permute-start | bytes 3145736 | tf_op jit(solution)/shard_map/ppermute | solution.py:12
  385.8 24.0 %collective-permute-start.6 = (bf16[1024,2,256]{2,0,1:T(8,128)(2,1)S(1)}, bf16[1024,2,256]{2,0,1:T(8,128)(2,1)S(1)}, u32[]{:S(2)}, u32[]{:S(2)}) collective-permute-start(bf16[1024,2,256]{2,0,1:T(8,128)(2,1)S(1)} %pad_maximum_fusion.8), channel_id=1, source_target_pairs={{0,16},{16,32},{32,48},{48,64},{64,80},{80,96},{96,112},{112,0},{1... | collective-permute-start | bytes 3145736 | tf_op jit(solution)/shard_map/ppermute | solution.py:12
  412.3 23.0 %collective-permute-start.7 = (bf16[1024,2,256]{2,0,1:T(8,128)(2,1)S(1)}, bf16[1024,2,256]{2,0,1:T(8,128)(2,1)S(1)}, u32[]{:S(2)}, u32[]{:S(2)}) collective-permute-start(bf16[1024,2,256]{2,0,1:T(8,128)(2,1)S(1)} %pad_maximum_fusion.9), channel_id=1, source_target_pairs={{0,16},{16,32},{32,48},{48,64},{64,80},{80,96},{96,112},{112,0},{1... | collective-permute-start | bytes 3145736 | tf_op jit(solution)/shard_map/ppermute | solution.py:12
where the time goes:
time: 446 us; the launch traced here: 438 us
  waiting for transfers between devices  233 us (52%)
  blocking collectives  120 us (27%)
  matrix products  40.2 us (9%)
  local copies, waits for them, and re-layouts  21.9 us (5%)
  other arithmetic  13.7 us (3%)
  starting transfers between devices  8.07 us (2%)
    ppermute x8, waiting for transfers between devices, shifted(): return lax.ppermute(value, axis, pairs)  207 us
    all_to_all x2, blocking collectives, owner_level(): lax.all_to_all(outgoing, ('leaf', 'slab'), split_axis=0, concat_axis=0, t...  73.3 us
    all_to_all x1, blocking collectives, owner_level(): lax.all_to_all(finished, ('leaf', 'slab'), split_axis=0, concat_axis=0, t...  36.2 us
    all_to_all x1, waiting for transfers between devices, owner_level(): lax.all_to_all(finished, ('leaf', 'slab'), split_axis=0, concat_axis=0, t...  25.1 us
    another operation x10, other arithmetic, complex_product(): return jnp.stack([real_part, imag_part], axis=1).astype(jnp.bfloat16)  13.7 us
    dot_general x2, matrix products, dispatch(): jnp.dot(selector, flat_rows, preferred_element_type=jnp.float32)  11.3 us
    all_gather x1, blocking collectives, body(): stem_full = lax.all_gather(stem_tensors, 'slab', axis=3, tiled=True)  10.9 us
    another operation x4, local copies, waits for them, and re-layouts, complex_product(): return jnp.stack([real_part, imag_part], axis=1).astype(jnp.bfloat16)  9.74 us
  transfers between devices with their start and end apart: 9, of which 9 were waited for; matrix products, arithmetic and copies ran while one was open for 0% of the time, Pallas kernels for 0%

commit v1 on v0

v1 whole, which is shorter than its diff:
```python
import jax
import jax.numpy as jnp
from jax import lax
from jax.experimental import pallas as pl
from jax.experimental.pallas import tpu as pltpu
from jax.sharding import PartitionSpec as P

AXES = ("stem", "leaf", "slab")
ROWS = 1024
BOND = 256
NODES = 16
PAD = 16
SORTED = 1280
WINDOW = 80
ROOM = SORTED + 2 * WINDOW
F32 = jnp.float32
BF16 = jnp.bfloat16


def device_index(x, y, z, c):
    return (((y // 2) * 4 + z) * 8 + (x * 2 + y % 2)) * 2 + c


def routed(value, move):
    pairs = []
    for x in range(4):
        for y in range(4):
            for z in range(4):
                for c in range(2):
                    tx, ty, tz, tc = move(x, y, z, c)
                    pairs.append((device_index(x, y, z, c), device_index(tx % 4, ty % 4, tz % 4, tc)))
    return lax.ppermute(value, AXES, pairs)


def swap(value):
    return routed(value, lambda x, y, z, c: (x, y, z, 1 - c))


def along_x(value):
    return routed(value, lambda x, y, z, c: (x + 1 - 2 * c, y, z, c))


def along_y(value):
    return routed(value, lambda x, y, z, c: (x, y + 1 - 2 * c, z, c))


def along_z(value):
    return routed(value, lambda x, y, z, c: (x, y, z + 1 - 2 * c, c))


def across_z(value):
    return routed(value, lambda x, y, z, c: (x, y, z + 2, c))


def across_y(value):
    return routed(value, lambda x, y, z, c: (x, y + 2, z, c))


def mm(a, b):
    return jnp.dot(a, b, preferred_element_type=F32)


def complex_mm(ar, ai, br, bi):
    return mm(ar, br) - mm(ai, bi), mm(ar, bi) + mm(ai, br)


def slot_of(parent, x, p, c):
    dx = (parent // 4 - x + 4) % 4
    dp = ((parent // 2) % 2 + p) % 2
    dc = (parent % 2 + c) % 2
    near = dx == 3 - 2 * c
    side = jnp.where(near, jnp.where(dc == 0, 2, 6), jnp.where(dc == 0, 7, 3))
    side = side + 6 * dp
    base = jnp.where(dx == 0, dc + 4 * dp, 10 + dc + 4 * dp)
    return jnp.where((dx == 1) | (dx == 3), side, base)


def positions(key, triangle):
    node = lax.broadcasted_iota(jnp.int32, (NODES, ROWS), 0)
    match = node == key
    match_f = match.astype(F32)
    before = mm(match.astype(BF16), triangle)
    count = jnp.sum(match_f, axis=1, keepdims=True)
    padded = jnp.floor((count + (PAD - 1)) * (1.0 / PAD)) * PAD
    lower = (
        lax.broadcasted_iota(jnp.int32, (NODES, NODES), 1) < lax.broadcasted_iota(jnp.int32, (NODES, NODES), 0)
    ).astype(BF16)
    start = mm(lower, jnp.broadcast_to(padded, (NODES, 128)).astype(BF16))
    place = jnp.sum(match_f * (start[:, :1] + before), axis=0, keepdims=True)
    return place, start, count


def prepare_kernel(key1_ref, key2_ref, rows_ref, x1_ref, q_ref, col_ref, table_ref, sel):
    lane = lax.broadcasted_iota(jnp.int32, (ROWS, ROWS), 1)
    sub = lax.broadcasted_iota(jnp.int32, (ROWS, ROWS), 0)
    triangle = (sub < lane).astype(BF16)
    place1, start1, count1 = positions(key1_ref[...], triangle)
    place2, start2, count2 = positions(key2_ref[...], triangle)
    table_ref[0] = start1.astype(jnp.int32)
    table_ref[1] = jnp.broadcast_to(count1, (NODES, 128)).astype(jnp.int32)
    table_ref[2] = start2.astype(jnp.int32)
    table_ref[3] = jnp.broadcast_to(count2, (NODES, 128)).astype(jnp.int32)
    place1_i = place1.astype(jnp.int32)
    step = 256
    for block in range(SORTED // step):
        spot = lax.broadcasted_iota(jnp.int32, (step, ROWS), 0) + block * step
        one_hot = (spot == place1_i).astype(BF16)
        sel[pl.ds(block * step, step), :] = one_hot
        x1_ref[pl.ds(block * step, step), :] = mm(one_hot, rows_ref[...]).astype(BF16)
    x1_ref[pl.ds(SORTED, ROOM - SORTED), :] = jnp.zeros((ROOM - SORTED, 2 * BOND), BF16)
    high = jnp.floor(place2 * (1.0 / 64.0))
    low = place2 - 64.0 * high
    which = lax.broadcasted_iota(jnp.int32, (8, ROWS), 0)
    parts = jnp.where(which == 0, high + 1.0, jnp.where(which == 1, low, 0.0)).astype(BF16)
    found = lax.dot_general(parts, sel[...], (((1,), (1,)), ((), ())), preferred_element_type=F32)
    q = (found[0:1] - 1.0) * 64.0 + found[1:2]
    q_ref[...] = jnp.broadcast_to(q, (8, SORTED)).astype(jnp.int32)
    col = jnp.transpose(jnp.broadcast_to(place2, (128, ROWS)))
    col_ref[...] = col.astype(jnp.int32)


def level(x_ref, out_ref, table_ref, row, slots, which):
    for k, slot in enumerate(slots):
        begin = pl.multiple_of(table_ref[row, k, 0], PAD)
        count = table_ref[row + 1, k, 0]
        for part in range(2):
            @pl.when(count > part * WINDOW)
            def _(begin=begin, part=part, slot=slot):
                spot = pl.ds(pl.multiple_of(begin + part * WINDOW, PAD), WINDOW)
                re, im = complex_mm(
                    x_ref[spot, :BOND], x_ref[spot, BOND:], slot[which, 0], slot[which, 1]
                )
                out_ref[spot, :BOND] = re.astype(BF16)
                out_ref[spot, BOND:] = im.astype(BF16)


def rows_kernel(*refs):
    table_ref, x1_ref, q_ref, col_ref, m_ref = refs[:5]
    slots = refs[5 : 5 + NODES]
    out_ref, first, x2, second = refs[5 + NODES :]
    first[...] = jnp.zeros_like(first)
    second[...] = jnp.zeros_like(second)
    x2[pl.ds(SORTED, ROOM - SORTED), :] = jnp.zeros((ROOM - SORTED, 2 * BOND), BF16)
    level(x1_ref, first, table_ref, 0, slots, 0)
    step = 256
    for block in range(SORTED // step):
        spot = lax.broadcasted_iota(jnp.int32, (step, SORTED), 0) + block * step
        one_hot = (spot == q_ref[0:1, :]).astype(BF16)
        x2[pl.ds(block * step, step), :] = mm(one_hot, first[pl.ds(0, SORTED), :]).astype(BF16)
    level(x2, second, table_ref, 2, slots, 1)
    for block in range(ROWS // step):
        spot = pl.ds(block * step, step)
        lane = lax.broadcasted_iota(jnp.int32, (step, SORTED), 1)
        one_hot = (lane == col_ref[spot, 0:1]).astype(BF16)
        picked = mm(one_hot, second[pl.ds(0, SORTED), :]).astype(BF16)
        re, im = complex_mm(picked[:, :BOND], picked[:, BOND:], m_ref[0], m_ref[1])
        out_ref[0, spot, :] = re.astype(BF16)
        out_ref[1, spot, :] = im.astype(BF16)


def pair_kernel(where_ref, own_ref, other_ref, p_ref, full):
    c = where_ref[1]
    for layer in range(2):
        for part in range(2):
            full[layer, part, pl.ds(pl.multiple_of(c * 128, 128), 128), :] = own_ref[layer, part]
            full[layer, part, pl.ds(pl.multiple_of((1 - c) * 128, 128), 128), :] = other_ref[layer, part]
    re, im = complex_mm(full[0, 0], full[0, 1], full[1, 0], full[1, 1])
    p_ref[0] = re.astype(BF16)
    p_ref[1] = im.astype(BF16)


def gather_ring(where_ref, refs, held):
    z, c = where_ref[0], where_ref[1]
    spots = (z, (z + 3 + 2 * c) % 4, (z + 1 + 2 - 2 * c + 2) % 4, (z + 2) % 4)
    for spot, ref in zip(spots, refs):
        held[spot] = ref[...]


def chain(held, order, out_ref):
    re, im = held[order[0], 0], held[order[0], 1]
    for spot in order[1:]:
        re, im = complex_mm(re, im, held[spot, 0], held[spot, 1])
        re, im = re.astype(BF16), im.astype(BF16)
    out_ref[0] = re
    out_ref[1] = im


def ring_kernel(where_ref, a_ref, b_ref, c_ref, d_ref, t_ref, held):
    gather_ring(where_ref, (a_ref, b_ref, c_ref, d_ref), held)
    chain(held, (0, 1, 2, 3), t_ref)


def loop_kernel(where_ref, a_ref, b_ref, c_ref, d_ref, far_ref, m_ref, held):
    gather_ring(where_ref, (a_ref, b_ref, c_ref, d_ref), held)
    held[4] = far_ref[...]
    z = where_ref[0]
    chain(held, tuple((z + i) % 5 for i in range(5)), m_ref)


def vmem():
    return pl.BlockSpec(memory_space=pltpu.VMEM)


def smem():
    return pl.BlockSpec(memory_space=pltpu.SMEM)


def call(kernel, out, ins, scratch, flops, moved):
    return pl.pallas_call(
        kernel,
        out_shape=out,
        in_specs=ins,
        out_specs=jax.tree.map(lambda _: vmem(), out),
        scratch_shapes=scratch,
        cost_estimate=pl.CostEstimate(flops=flops, bytes_accessed=moved, transcendentals=0),
        compiler_params=pltpu.CompilerParams(vmem_limit_bytes=40 * 2**20),
    )


def body(branch_rows, first_parent, second_parent, node_first, node_second, stem_tensors):
    stem, leaf, core = (lax.axis_index(name) for name in AXES)
    x, p, z = leaf // 2, leaf % 2, stem % 4
    where = jnp.stack([z, core]).astype(jnp.int32)
    matrix = jax.ShapeDtypeStruct((2, BOND, BOND), BF16)

    own = jnp.concatenate([node_first, node_second], axis=0)
    side = along_x(own)
    sibling = swap(own)
    stem_own = stem_tensors[0]
    stem_other = swap(stem_own)
    own_later, sibling, stem_other = lax.optimization_barrier((own, sibling, stem_other))
    side_far = along_x(sibling)
    turned = along_y(own_later)

    product = call(pair_kernel, matrix, [smem(), vmem(), vmem()],
                   [pltpu.VMEM((2, 2, BOND, BOND), BF16)], 2**28, 2**20)(where, stem_own, stem_other)

    rows = branch_rows.reshape(ROWS, 2 * BOND)
    key1 = slot_of(first_parent.reshape(1, ROWS), x, p, core)
    key2 = slot_of(second_parent.reshape(1, ROWS), x, p, core)
    x1, q, col, table = call(
        prepare_kernel,
        (
            jax.ShapeDtypeStruct((ROOM, 2 * BOND), BF16),
            jax.ShapeDtypeStruct((8, SORTED), jnp.int32),
            jax.ShapeDtypeStruct((ROWS, 128), jnp.int32),
            jax.ShapeDtypeStruct((4, NODES, 128), jnp.int32),
        ),
        [vmem(), vmem(), vmem()],
        [pltpu.VMEM((SORTED, ROWS), BF16)],
        2**31, 2**22,
    )(key1, key2, rows)

    near = along_z(product)
    opposite = across_z(product)
    near_other = swap(near)
    ring = (product, near, near_other, opposite)
    total = call(ring_kernel, matrix, [smem()] + [vmem()] * 4,
                 [pltpu.VMEM((4, 2, BOND, BOND), BF16)], 2**29, 2**20)(where, *ring)
    far = across_y(total)
    loop = call(loop_kernel, matrix, [smem()] + [vmem()] * 5,
                [pltpu.VMEM((5, 2, BOND, BOND), BF16)], 2**29, 2**20)(where, *ring, far)

    across = along_x(side)
    side_turned = along_y(side)
    side_far_turned = along_y(side_far)
    across_turned = along_y(across)
    slots = [own, sibling]
    for value in (side, turned, side_far, side_turned, across, side_far_turned, across_turned):
        slots += [value, swap(value)]

    out = call(
        rows_kernel,
        jax.ShapeDtypeStruct((2, ROWS, BOND), BF16),
        [smem()] + [vmem()] * (4 + NODES),
        [pltpu.VMEM((ROOM, 2 * BOND), BF16)] * 3,
        2**33, 2**24,
    )(table, x1, q, col, loop, *slots)
    return jnp.transpose(out, (1, 0, 2))


def solution(mesh):
    return jax.shard_map(
        body,
        mesh=mesh,
        in_specs=(
            P(AXES, None, None),
            P(AXES, None),
            P(AXES, None),
            P(("leaf", "slab"), None, None, None),
            P(("leaf", "slab"), None, None, None),
            P("stem", None, None, "slab", None),
        ),
        out_specs=P(AXES, None, None),
        check_vma=False,
    )
```

time: 446 us -> 80.2 us (0.18)
  the two profiles are of different devices: /device:TPU:8 before, /device:TPU:1 now
where the time goes in v1:
time: 80.2 us
  starting transfers between devices  37.2 us (46%)
  Pallas kernels  22.5 us (28%)
  waiting for transfers between devices  11.1 us (14%)
  local copies, waits for them, and re-layouts  8.73 us (11%)
    ppermute x20, starting transfers between devices, routed(): return lax.ppermute(value, AXES, pairs)  37.2 us
    pallas_call x1, Pallas kernels, body(): call(rows_kernel, jax.ShapeDtypeStruct((2, ROWS, BOND), BF16), [smem()] +...  16.1 us
    ppermute x20, waiting for transfers between devices, routed(): return lax.ppermute(value, AXES, pairs)  11.1 us
    unnamed x32, local copies, waits for them, and re-layouts  5.72 us
    pallas_call x1, Pallas kernels, body(): call(prepare_kernel, (jax.ShapeDtypeStruct((ROOM, 2 * BOND), BF16), jax.S...  2.64 us
    transpose x1, local copies, waits for them, and re-layouts, body(): return jnp.transpose(out, (1, 0, 2))  2.05 us
  transfers between devices with their start and end apart: 20, of which 5 were waited for; matrix products, arithmetic and copies ran while one was open for 2% of the time, Pallas kernels for 8%

profile of v1, /device:TPU:1, one launch (start us, length us, event | category | flops | bytes accessed | tf_op | source)
XLA Modules:
  0.0 80.2 jit_solution(6022971043025694748)
XLA Ops:
  0.0 1.0 %constant_dynamic-update-slice_fusion.1 = bf16[2,2,256,256]{3,2,1,0:T(8,128)(2,1)S(1)} fusion(bf16[1,2,256,256]{3,2,1,0:T(8,128)(2,1)} %param.9), kind=kLoop, calls=%fused_computation.41 | loop fusion | bytes 524288
  1.0 1.0 %constant_dynamic-update-slice_fusion.refs_5_ = bf16[2,2,256,256]{3,2,1,0:T(8,128)(2,1)S(1)} fusion(bf16[2,2,256,256]{3,2,1,0:T(8,128)(2,1)S(1)} %constant_dynamic-update-slice_fusion.1, bf16[1,2,256,256]{3,2,1,0:T(8,128)(2,1)} %param.10), kind=kLoop, calls=%fused_computation.40 | loop fusion | bytes 524288 | tf_op jit(solution)/shard_map/concatenate | solution.py:226
  1.9 1.5 %collective-permute-start = (bf16[2,2,256,256]{3,2,1,0:T(8,128)(2,1)S(1)}, bf16[2,2,256,256]{3,2,1,0:T(8,128)(2,1)S(1)}, u32[]{:S(2)}, u32[]{:S(2)}) collective-permute-start(bf16[2,2,256,256]{3,2,1,0:T(8,128)(2,1)S(1)} %constant_dynamic-update-slice_fusion.refs_5_), channel_id=1, source_target_pairs={{0,1},{1,0},{16,17},{17,16},{32,33},{33,32},{48,49},{49,48},{2,3},... | collective-permute-start | bytes 1572872 | tf_op jit(solution)/shard_map/ppermute | solution.py:32
  3.4 2.6 %collective-permute-start.6 = (bf16[2,2,256,256]{3,2,1,0:T(8,128)(2,1)S(1)}, bf16[2,2,256,256]{3,2,1,0:T(8,128)(2,1)S(1)}, u32[]{:S(2)}, u32[]{:S(2)}) collective-permute-start(bf16[2,2,256,256]{3,2,1,0:T(8,128)(2,1)S(1)} %constant_dynamic-update-slice_fusion.refs_5_), channel_id=1, source_target_pairs={{0,4},{1,13},{16,20},{17,29},{32,36},{33,45},{48,52},{49,61},{2,6}... | collective-permute-start | bytes 1572872 | tf_op jit(solution)/shard_map/ppermute | solution.py:32
  6.1 1.7 %collective-permute-done.1.other_ref = bf16[2,2,128,256]{3,2,1,0:T(8,128)(2,1)S(1)} collective-permute-done((bf16[2,2,128,256]{3,2,1,0:T(8,128)(2,1)}, bf16[2,2,128,256]{3,2,1,0:T(8,128)(2,1)S(1)}, u32[]{:S(2)}, u32[]{:S(2)}) %collective-permute-start.1) | collective-permute-done | bytes 262176 | tf_op jit(solution)/shard_map/ppermute | solution.py:32
  7.8 0.9 %copy-done.4 = bf16[1,2,2,128,256]{4,3,2,1,0:T(8,128)(2,1)S(1)} copy-done((bf16[1,2,2,128,256]{4,3,2,1,0:T(8,128)(2,1)S(1)}, bf16[1,2,2,128,256]{4,3,2,1,0:T(8,128)(2,1)}, u32[]{:S(2)}) %copy-start.4) | copy-done | bytes 262168
  9.6 3.8 %collective-permute-start.2 = (bf16[2,256,256]{2,1,0:T(8,128)(2,1)S(1)}, bf16[2,256,256]{2,1,0:T(8,128)(2,1)S(1)}, u32[]{:S(2)}, u32[]{:S(2)}) collective-permute-start(bf16[2,256,256]{2,1,0:T(8,128)(2,1)S(1)} %shard_map.65.a_ref), channel_id=1, source_target_pairs={{0,16},{1,49},{16,32},{17,1},{32,48},{33,17},{48,0},{49,33},{2,18}... | collective-permute-start | bytes 786440 | tf_op jit(solution)/shard_map/ppermute | solution.py:32
  14.0 2.7 %collective-permute-start.8 = (bf16[2,2,256,256]{3,2,1,0:T(8,128)(2,1)S(1)}, bf16[2,2,256,256]{3,2,1,0:T(8,128)(2,1)}, u32[]{:S(2)}, u32[]{:S(2)}) collective-permute-start(bf16[2,2,256,256]{3,2,1,0:T(8,128)(2,1)S(1)} %constant_dynamic-update-slice_fusion.refs_5_), channel_id=1, source_target_pairs={{0,2},{1,67},{16,18},{17,83},{32,34},{33,99},{48,50},{49,115},{2,6... | collective-permute-start | bytes 1572872 | tf_op jit(solution)/shard_map/ppermute | solution.py:32
  16.7 0.9 %collective-permute-start.14 = (bf16[2,2,256,256]{3,2,1,0:T(8,128)(2,1)S(1)}, bf16[2,2,256,256]{3,2,1,0:T(8,128)(2,1)}, u32[]{:S(2)}, u32[]{:S(2)}) collective-permute-start(bf16[2,2,256,256]{3,2,1,0:T(8,128)(2,1)S(1)} %collective-permute-done.6.refs_7_), channel_id=1, source_target_pairs={{0,4},{1,13},{16,20},{17,29},{32,36},{33,45},{48,52},{49,61},{2,6}... | collective-permute-start | bytes 1572872 | tf_op jit(solution)/shard_map/ppermute | solution.py:32
  17.6 4.7 %collective-permute-done.2.b_ref = bf16[2,256,256]{2,1,0:T(8,128)(2,1)S(1)} collective-permute-done((bf16[2,256,256]{2,1,0:T(8,128)(2,1)S(1)}, bf16[2,256,256]{2,1,0:T(8,128)(2,1)S(1)}, u32[]{:S(2)}, u32[]{:S(2)}) %collective-permute-start.2) | collective-permute-done | bytes 262176 | tf_op jit(solution)/shard_map/ppermute | solution.py:32
  22.4 0.9 %collective-permute-done.4.d_ref = bf16[2,256,256]{2,1,0:T(8,128)(2,1)S(1)} collective-permute-done((bf16[2,256,256]{2,1,0:T(8,128)(2,1)S(1)}, bf16[2,256,256]{2,1,0:T(8,128)(2,1)S(1)}, u32[]{:S(2)}, u32[]{:S(2)}) %collective-permute-start.4) | collective-permute-done | bytes 262176 | tf_op jit(solution)/shard_map/ppermute | solution.py:32
  23.3 2.7 %collective-permute-start.12 = (bf16[2,2,256,256]{3,2,1,0:T(8,128)(2,1)S(1)}, bf16[2,2,256,256]{3,2,1,0:T(8,128)(2,1)}, u32[]{:S(2)}, u32[]{:S(2)}) collective-permute-start(bf16[2,2,256,256]{3,2,1,0:T(8,128)(2,1)S(1)} %collective-permute-done.6.refs_7_), channel_id=1, source_target_pairs={{0,2},{1,67},{16,18},{17,83},{32,34},{33,99},{48,50},{49,115},{2,6... | collective-permute-start | bytes 1572872 | tf_op jit(solution)/shard_map/ppermute | solution.py:32
  26.8 1.4 %collective-permute-start.16 = (bf16[2,2,256,256]{3,2,1,0:T(8,128)(2,1)S(1)}, bf16[2,2,256,256]{3,2,1,0:T(8,128)(2,1)}, u32[]{:S(2)}, u32[]{:S(2)}) collective-permute-start(bf16[2,2,256,256]{3,2,1,0:T(8,128)(2,1)S(1)} %collective-permute-done.10.refs_11_), channel_id=1, source_target_pairs={{0,2},{1,67},{16,18},{17,83},{32,34},{33,99},{48,50},{49,115},{2,6... | collective-permute-start | bytes 1572872 | tf_op jit(solution)/shard_map/ppermute | solution.py:32
  28.5 1.7 %collective-permute-start.18 = (bf16[2,2,256,256]{3,2,1,0:T(8,128)(2,1)}, bf16[2,2,256,256]{3,2,1,0:T(8,128)(2,1)}, u32[]{:S(2)}, u32[]{:S(2)}) collective-permute-start(bf16[2,2,256,256]{3,2,1,0:T(8,128)(2,1)} %collective-permute-done.14.refs_15_), channel_id=1, source_target_pairs={{0,2},{1,67},{16,18},{17,83},{32,34},{33,99},{48,50},{49,115},{2,6... | collective-permute-start | bytes 1572872 | tf_op jit(solution)/shard_map/ppermute | solution.py:32
  30.2 1.4 %shard_map.66 = bf16[2,256,256]{2,1,0:T(8,128)(2,1)S(1)} custom-call(s32[2]{0:T(128)S(1)} %pad_add_fusion.where_ref, bf16[2,256,256]{2,1,0:T(8,128)(2,1)S(1)} %shard_map.65.a_ref, bf16[2,256,256]{2,1,0:T(8,128)(2,1)S(1)} %collective-permute-done.2.b_ref, bf16[2,256,256]{2,1,0:T(8,128)(2,1)S(1)} %collective-permute-done.3.c_ref, ...), custom_call_target="tpu_custom_call" | custom-call | flops 536870912 | bytes 1048576 | tf_op jit(solution)/shard_map/pallas_call | solution.py:258
  32.1 2.5 %collective-permute-start.5 = (bf16[2,256,256]{2,1,0:T(8,128)(2,1)S(1)}, bf16[2,256,256]{2,1,0:T(8,128)(2,1)S(1)}, u32[]{:S(2)}, u32[]{:S(2)}) collective-permute-start(bf16[2,256,256]{2,1,0:T(8,128)(2,1)S(1)} %shard_map.66), channel_id=1, source_target_pairs={{0,64},{1,65},{16,80},{17,81},{32,96},{33,97},{48,112},{49,113},{2... | collective-permute-start | bytes 786440 | tf_op jit(solution)/shard_map/ppermute | solution.py:32
  35.4 3.1 %collective-permute-start.15 = (bf16[2,2,256,256]{3,2,1,0:T(8,128)(2,1)}, bf16[2,2,256,256]{3,2,1,0:T(8,128)(2,1)}, u32[]{:S(2)}, u32[]{:S(2)}) collective-permute-start(bf16[2,2,256,256]{3,2,1,0:T(8,128)(2,1)} %collective-permute-done.14.refs_15_), channel_id=1, source_target_pairs={{0,1},{1,0},{16,17},{17,16},{32,33},{33,32},{48,49},{49,48},{2,3},... | collective-permute-start | bytes 1572872 | tf_op jit(solution)/shard_map/ppermute | solution.py:32
  38.5 3.2 %collective-permute-done.5.far_ref = bf16[2,256,256]{2,1,0:T(8,128)(2,1)S(1)} collective-permute-done((bf16[2,256,256]{2,1,0:T(8,128)(2,1)S(1)}, bf16[2,256,256]{2,1,0:T(8,128)(2,1)S(1)}, u32[]{:S(2)}, u32[]{:S(2)}) %collective-permute-start.5) | collective-permute-done | bytes 262176 | tf_op jit(solution)/shard_map/ppermute | solution.py:32
  42.4 12.0 %collective-permute-start.9 = (bf16[2,2,256,256]{3,2,1,0:T(8,128)(2,1)}, bf16[2,2,256,256]{3,2,1,0:T(8,128)(2,1)}, u32[]{:S(2)}, u32[]{:S(2)}) collective-permute-start(bf16[2,2,256,256]{3,2,1,0:T(8,128)(2,1)} %collective-permute-done.8.refs_9_), channel_id=1, source_target_pairs={{0,1},{1,0},{16,17},{17,16},{32,33},{33,32},{48,49},{49,48},{2,3},... | collective-permute-start | bytes 1572872 | tf_op jit(solution)/shard_map/ppermute | solution.py:32
  55.9 1.5 %copy.8 = bf16[128,8,2,256]{3,1,2,0:T(8,128)(2,1)S(1)} copy(bf16[128,8,2,256]{3,2,1,0:T(2,128)(2,1)} %bitcast.42) | data formatting | bytes 2097152
  57.7 2.6 %shard_map.64 = (bf16[1440,512]{1,0:T(8,128)(2,1)S(1)}, s32[8,1280]{1,0:T(8,128)S(1)}, s32[1024,128]{1,0:T(8,128)S(1)}, s32[4,16,128]{2,1,0:T(8,128)S(1)}) custom-call(s32[1,1024]{1,0:T(1,128)S(1)} %get-tuple-element.20.key1_ref, s32[1,1024]{1,0:T(1,128)S(1)} %get-tuple-element.19.key2_ref, bf16[1024,512]{1,0:T(8,128)(2,1)S(1)} %bitcast.38), custom_call_target="tpu_custom_call" | custom-call | flops 2147483648 | bytes 4194304 | tf_op jit(solution)/shard_map/pallas_call | solution.py:241
  60.4 1.6 %shard_map.67.refs_4_ = bf16[2,256,256]{2,1,0:T(8,128)(2,1)S(1)} custom-call(s32[2]{0:T(128)S(1)} %pad_add_fusion.where_ref, bf16[2,256,256]{2,1,0:T(8,128)(2,1)S(1)} %shard_map.65.a_ref, bf16[2,256,256]{2,1,0:T(8,128)(2,1)S(1)} %copy-done.6, bf16[2,256,256]{2,1,0:T(8,128)(2,1)S(1)} %copy-done.10, bf16[2,256,256]{2,1,0:T(8,128)(2,1)S(1)} %copy-done.8, ...), custom_call_target="tpu_custom_call" | custom-call | flops 536870912 | bytes 1048576 | tf_op jit(solution)/shard_map/pallas_call | solution.py:261
  62.0 16.1 %shard_map.68 = bf16[2,1024,256]{2,1,0:T(8,128)(2,1)S(1)} custom-call(s32[4,16,128]{2,1,0:T(8,128)S(1)} %get-tuple-element.12.refs_0_, bf16[1440,512]{1,0:T(8,128)(2,1)S(1)} %get-tuple-element.13.refs_1_, s32[8,1280]{1,0:T(8,128)S(1)} %get-tuple-element.14.refs_2_, s32[1024,128]{1,0:T(8,128)S(1)} %get-tuple-element.15.refs_3_, ...), custom_call_target="tpu_custom_call" | custom-call | flops 8589934592 | bytes 16777216 | tf_op jit(solution)/shard_map/pallas_call | solution.py:272
  78.1 2.0 %copy.7 = bf16[1024,2,256]{2,1,0:T(2,128)(2,1)} copy(bf16[1024,2,256]{2,0,1:T(8,128)(2,1)S(1)} %bitcast.39) | data formatting | bytes 2097152 | tf_op jit(solution)/shard_map/transpose | solution.py:279
  (57 shorter events, 6.4 us)
Async XLA Ops:
  1.9 5.8 %collective-permute-start = (bf16[2,2,256,256]{3,2,1,0:T(8,128)(2,1)S(1)}, bf16[2,2,256,256]{3,2,1,0:T(8,128)(2,1)S(1)}, u32[]{:S(2)}, u32[]{:S(2)}) collective-permute-start(bf16[2,2,256,256]{3,2,1,0:T(8,128)(2,1)S(1)} %constant_dynamic-update-slice_fusion.refs_5_), channel_id=1, source_target_pairs={{0,1},{1,0},{16,17},{17,16},{32,33},{33,32},{48,49},{49,48},{2,3},... | collective-permute-start | bytes 1572872 | tf_op jit(solution)/shard_map/ppermute | solution.py:32
  3.4 13.3 %collective-permute-start.6 = (bf16[2,2,256,256]{3,2,1,0:T(8,128)(2,1)S(1)}, bf16[2,2,256,256]{3,2,1,0:T(8,128)(2,1)S(1)}, u32[]{:S(2)}, u32[]{:S(2)}) collective-permute-start(bf16[2,2,256,256]{3,2,1,0:T(8,128)(2,1)S(1)} %constant_dynamic-update-slice_fusion.refs_5_), channel_id=1, source_target_pairs={{0,4},{1,13},{16,20},{17,29},{32,36},{33,45},{48,52},{49,61},{2,6}... | collective-permute-start | bytes 1572872 | tf_op jit(solution)/shard_map/ppermute | solution.py:32
  6.0 1.7 %collective-permute-start.1 = (bf16[2,2,128,256]{3,2,1,0:T(8,128)(2,1)}, bf16[2,2,128,256]{3,2,1,0:T(8,128)(2,1)S(1)}, u32[]{:S(2)}, u32[]{:S(2)}) collective-permute-start(bf16[2,2,128,256]{3,2,1,0:T(8,128)(2,1)} %bitcast.40), channel_id=1, source_target_pairs={{0,1},{1,0},{16,17},{17,16},{32,33},{33,32},{48,49},{49,48},{2,3},... | collective-permute-start | bytes 786440 | tf_op jit(solution)/shard_map/ppermute | solution.py:32
  9.6 12.8 %collective-permute-start.2 = (bf16[2,256,256]{2,1,0:T(8,128)(2,1)S(1)}, bf16[2,256,256]{2,1,0:T(8,128)(2,1)S(1)}, u32[]{:S(2)}, u32[]{:S(2)}) collective-permute-start(bf16[2,256,256]{2,1,0:T(8,128)(2,1)S(1)} %shard_map.65.a_ref), channel_id=1, source_target_pairs={{0,16},{1,49},{16,32},{17,1},{32,48},{33,17},{48,0},{49,33},{2,18}... | collective-permute-start | bytes 786440 | tf_op jit(solution)/shard_map/ppermute | solution.py:32
  13.4 9.9 %collective-permute-start.4 = (bf16[2,256,256]{2,1,0:T(8,128)(2,1)S(1)}, bf16[2,256,256]{2,1,0:T(8,128)(2,1)S(1)}, u32[]{:S(2)}, u32[]{:S(2)}) collective-permute-start(bf16[2,256,256]{2,1,0:T(8,128)(2,1)S(1)} %shard_map.65.a_ref), channel_id=1, source_target_pairs={{0,32},{1,33},{16,48},{17,49},{32,0},{33,1},{48,16},{49,17},{2,34}... | collective-permute-start | bytes 786440 | tf_op jit(solution)/shard_map/ppermute | solution.py:32
  13.4 13.4 %collective-permute-start.10 = (bf16[2,2,256,256]{3,2,1,0:T(8,128)(2,1)S(1)}, bf16[2,2,256,256]{3,2,1,0:T(8,128)(2,1)S(1)}, u32[]{:S(2)}, u32[]{:S(2)}) collective-permute-start(bf16[2,2,256,256]{3,2,1,0:T(8,128)(2,1)S(1)} %collective-permute-done.refs_6_), channel_id=1, source_target_pairs={{0,4},{1,13},{16,20},{17,29},{32,36},{33,45},{48,52},{49,61},{2,6}... | collective-permute-start | bytes 1572872 | tf_op jit(solution)/shard_map/ppermute | solution.py:32
  14.0 14.3 %collective-permute-start.8 = (bf16[2,2,256,256]{3,2,1,0:T(8,128)(2,1)S(1)}, bf16[2,2,256,256]{3,2,1,0:T(8,128)(2,1)}, u32[]{:S(2)}, u32[]{:S(2)}) collective-permute-start(bf16[2,2,256,256]{3,2,1,0:T(8,128)(2,1)S(1)} %constant_dynamic-update-slice_fusion.refs_5_), channel_id=1, source_target_pairs={{0,2},{1,67},{16,18},{17,83},{32,34},{33,99},{48,50},{49,115},{2,6... | collective-permute-start | bytes 1572872 | tf_op jit(solution)/shard_map/ppermute | solution.py:32
  16.7 11.8 %collective-permute-start.14 = (bf16[2,2,256,256]{3,2,1,0:T(8,128)(2,1)S(1)}, bf16[2,2,256,256]{3,2,1,0:T(8,128)(2,1)}, u32[]{:S(2)}, u32[]{:S(2)}) collective-permute-start(bf16[2,2,256,256]{3,2,1,0:T(8,128)(2,1)S(1)} %collective-permute-done.6.refs_7_), channel_id=1, source_target_pairs={{0,4},{1,13},{16,20},{17,29},{32,36},{33,45},{48,52},{49,61},{2,6}... | collective-permute-start | bytes 1572872 | tf_op jit(solution)/shard_map/ppermute | solution.py:32
  22.4 32.1 %copy-start.5 = (bf16[2,256,256]{2,1,0:T(8,128)(2,1)}, bf16[2,256,256]{2,1,0:T(8,128)(2,1)S(1)}, u32[]{:S(2)}) copy-start(bf16[2,256,256]{2,1,0:T(8,128)(2,1)S(1)} %collective-permute-done.2.b_ref) | copy-start | bytes 786436
  22.4 3.7 %collective-permute-start.3 = (bf16[2,256,256]{2,1,0:T(8,128)(2,1)S(1)}, bf16[2,256,256]{2,1,0:T(8,128)(2,1)S(1)}, u32[]{:S(2)}, u32[]{:S(2)}) collective-permute-start(bf16[2,256,256]{2,1,0:T(8,128)(2,1)S(1)} %collective-permute-done.2.b_ref), channel_id=1, source_target_pairs={{0,1},{1,0},{16,17},{17,16},{32,33},{33,32},{48,49},{49,48},{2,3},... | collective-permute-start | bytes 786440 | tf_op jit(solution)/shard_map/ppermute | solution.py:32
  23.3 32.5 %copy-start.7 = (bf16[2,256,256]{2,1,0:T(8,128)(2,1)}, bf16[2,256,256]{2,1,0:T(8,128)(2,1)S(1)}, u32[]{:S(2)}) copy-start(bf16[2,256,256]{2,1,0:T(8,128)(2,1)S(1)} %collective-permute-done.4.d_ref) | copy-start | bytes 786436
  23.3 8.9 %collective-permute-start.12 = (bf16[2,2,256,256]{3,2,1,0:T(8,128)(2,1)S(1)}, bf16[2,2,256,256]{3,2,1,0:T(8,128)(2,1)}, u32[]{:S(2)}, u32[]{:S(2)}) collective-permute-start(bf16[2,2,256,256]{3,2,1,0:T(8,128)(2,1)S(1)} %collective-permute-done.6.refs_7_), channel_id=1, source_target_pairs={{0,2},{1,67},{16,18},{17,83},{32,34},{33,99},{48,50},{49,115},{2,6... | collective-permute-start | bytes 1572872 | tf_op jit(solution)/shard_map/ppermute | solution.py:32
  26.0 29.8 %copy-start.9 = (bf16[2,256,256]{2,1,0:T(8,128)(2,1)}, bf16[2,256,256]{2,1,0:T(8,128)(2,1)S(1)}, u32[]{:S(2)}) copy-start(bf16[2,256,256]{2,1,0:T(8,128)(2,1)S(1)} %collective-permute-done.3.c_ref) | copy-start | bytes 786436
  26.0 8.6 %collective-permute-start.7 = (bf16[2,2,256,256]{3,2,1,0:T(8,128)(2,1)S(1)}, bf16[2,2,256,256]{3,2,1,0:T(8,128)(2,1)S(1)}, u32[]{:S(2)}, u32[]{:S(2)}) collective-permute-start(bf16[2,2,256,256]{3,2,1,0:T(8,128)(2,1)S(1)} %collective-permute-done.6.refs_7_), channel_id=1, source_target_pairs={{0,1},{1,0},{16,17},{17,16},{32,33},{33,32},{48,49},{49,48},{2,3},... | collective-permute-start | bytes 1572872 | tf_op jit(solution)/shard_map/ppermute | solution.py:32
  26.8 27.6 %collective-permute-start.16 = (bf16[2,2,256,256]{3,2,1,0:T(8,128)(2,1)S(1)}, bf16[2,2,256,256]{3,2,1,0:T(8,128)(2,1)}, u32[]{:S(2)}, u32[]{:S(2)}) collective-permute-start(bf16[2,2,256,256]{3,2,1,0:T(8,128)(2,1)S(1)} %collective-permute-done.10.refs_11_), channel_id=1, source_target_pairs={{0,2},{1,67},{16,18},{17,83},{32,34},{33,99},{48,50},{49,115},{2,6... | collective-permute-start | bytes 1572872 | tf_op jit(solution)/shard_map/ppermute | solution.py:32
  28.2 26.2 %collective-permute-start.11 = (bf16[2,2,256,256]{3,2,1,0:T(8,128)(2,1)S(1)}, bf16[2,2,256,256]{3,2,1,0:T(8,128)(2,1)S(1)}, u32[]{:S(2)}, u32[]{:S(2)}) collective-permute-start(bf16[2,2,256,256]{3,2,1,0:T(8,128)(2,1)S(1)} %collective-permute-done.10.refs_11_), channel_id=1, source_target_pairs={{0,1},{1,0},{16,17},{17,16},{32,33},{33,32},{48,49},{49,48},{2,3},... | collective-permute-start | bytes 1572872 | tf_op jit(solution)/shard_map/ppermute | solution.py:32
  28.5 27.3 %collective-permute-start.18 = (bf16[2,2,256,256]{3,2,1,0:T(8,128)(2,1)}, bf16[2,2,256,256]{3,2,1,0:T(8,128)(2,1)}, u32[]{:S(2)}, u32[]{:S(2)}) collective-permute-start(bf16[2,2,256,256]{3,2,1,0:T(8,128)(2,1)} %collective-permute-done.14.refs_15_), channel_id=1, source_target_pairs={{0,2},{1,67},{16,18},{17,83},{32,34},{33,99},{48,50},{49,115},{2,6... | collective-permute-start | bytes 1572872 | tf_op jit(solution)/shard_map/ppermute | solution.py:32
  31.6 25.8 %copy-start.13 = (s32[1024,1]{0,1:T(1,128)S(1)}, s32[1024,1]{0,1:T(1,128)}, u32[]{:S(2)}) copy-start(s32[1024,1]{0,1:T(1,128)} %param.8) | copy-start | bytes 12292
  32.1 9.6 %collective-permute-start.5 = (bf16[2,256,256]{2,1,0:T(8,128)(2,1)S(1)}, bf16[2,256,256]{2,1,0:T(8,128)(2,1)S(1)}, u32[]{:S(2)}, u32[]{:S(2)}) collective-permute-start(bf16[2,256,256]{2,1,0:T(8,128)(2,1)S(1)} %shard_map.66), channel_id=1, source_target_pairs={{0,64},{1,65},{16,80},{17,81},{32,96},{33,97},{48,112},{49,113},{2... | collective-permute-start | bytes 786440 | tf_op jit(solution)/shard_map/ppermute | solution.py:32
  35.4 26.6 %collective-permute-start.15 = (bf16[2,2,256,256]{3,2,1,0:T(8,128)(2,1)}, bf16[2,2,256,256]{3,2,1,0:T(8,128)(2,1)}, u32[]{:S(2)}, u32[]{:S(2)}) collective-permute-start(bf16[2,2,256,256]{3,2,1,0:T(8,128)(2,1)} %collective-permute-done.14.refs_15_), channel_id=1, source_target_pairs={{0,1},{1,0},{16,17},{17,16},{32,33},{33,32},{48,49},{49,48},{2,3},... | collective-permute-start | bytes 1572872 | tf_op jit(solution)/shard_map/ppermute | solution.py:32
  42.4 19.5 %collective-permute-start.9 = (bf16[2,2,256,256]{3,2,1,0:T(8,128)(2,1)}, bf16[2,2,256,256]{3,2,1,0:T(8,128)(2,1)}, u32[]{:S(2)}, u32[]{:S(2)}) collective-permute-start(bf16[2,2,256,256]{3,2,1,0:T(8,128)(2,1)} %collective-permute-done.8.refs_9_), channel_id=1, source_target_pairs={{0,1},{1,0},{16,17},{17,16},{32,33},{33,32},{48,49},{49,48},{2,3},... | collective-permute-start | bytes 1572872 | tf_op jit(solution)/shard_map/ppermute | solution.py:32
  54.5 7.5 %collective-permute-start.13 = (bf16[2,2,256,256]{3,2,1,0:T(8,128)(2,1)}, bf16[2,2,256,256]{3,2,1,0:T(8,128)(2,1)}, u32[]{:S(2)}, u32[]{:S(2)}) collective-permute-start(bf16[2,2,256,256]{3,2,1,0:T(8,128)(2,1)} %collective-permute-done.12.refs_13_), channel_id=1, source_target_pairs={{0,1},{1,0},{16,17},{17,16},{32,33},{33,32},{48,49},{49,48},{2,3},... | collective-permute-start | bytes 1572872 | tf_op jit(solution)/shard_map/ppermute | solution.py:32
  55.3 6.7 %collective-permute-start.17 = (bf16[2,2,256,256]{3,2,1,0:T(8,128)(2,1)}, bf16[2,2,256,256]{3,2,1,0:T(8,128)(2,1)}, u32[]{:S(2)}, u32[]{:S(2)}) collective-permute-start(bf16[2,2,256,256]{3,2,1,0:T(8,128)(2,1)} %collective-permute-done.16.refs_17_), channel_id=1, source_target_pairs={{0,1},{1,0},{16,17},{17,16},{32,33},{33,32},{48,49},{49,48},{2,3},... | collective-permute-start | bytes 1572872 | tf_op jit(solution)/shard_map/ppermute | solution.py:32
  55.8 6.2 %collective-permute-start.19 = (bf16[2,2,256,256]{3,2,1,0:T(8,128)(2,1)}, bf16[2,2,256,256]{3,2,1,0:T(8,128)(2,1)}, u32[]{:S(2)}, u32[]{:S(2)}) collective-permute-start(bf16[2,2,256,256]{3,2,1,0:T(8,128)(2,1)} %collective-permute-done.18.refs_19_), channel_id=1, source_target_pairs={{0,1},{1,0},{16,17},{17,16},{32,33},{33,32},{48,49},{49,48},{2,3},... | collective-permute-start | bytes 1572872 | tf_op jit(solution)/shard_map/ppermute | solution.py:32
  (11 other events, 43.1 us)

commit v2 on v1

v2 whole, which is shorter than its diff:
```python
import jax
import jax.numpy as jnp
from jax import lax
from jax.experimental import pallas as pl
from jax.experimental.pallas import tpu as pltpu
from jax.sharding import PartitionSpec as P

AXES = ("stem", "leaf", "slab")
ROWS = 1024
BOND = 256
NODES = 16
PAD = 16
SORTED = 1280
WINDOW = 80
ROOM = SORTED + 2 * WINDOW
TAIL = ROOM - 928
F32 = jnp.float32
BF16 = jnp.bfloat16


def device_index(x, y, z, c):
    return (((y // 2) * 4 + z) * 8 + (x * 2 + y % 2)) * 2 + c


def routed(value, move):
    pairs = []
    for x in range(4):
        for y in range(4):
            for z in range(4):
                for c in range(2):
                    tx, ty, tz, tc = move(x, y, z, c)
                    pairs.append((device_index(x, y, z, c), device_index(tx % 4, ty % 4, tz % 4, tc)))
    return lax.ppermute(value, AXES, pairs)


def swap(value):
    return routed(value, lambda x, y, z, c: (x, y, z, 1 - c))


def along_x(value):
    return routed(value, lambda x, y, z, c: (x + 1 - 2 * c, y, z, c))


def along_y(value):
    return routed(value, lambda x, y, z, c: (x, y + 1 - 2 * c, z, c))


def along_z(value):
    return routed(value, lambda x, y, z, c: (x, y, z + 1 - 2 * c, c))


def across_z(value):
    return routed(value, lambda x, y, z, c: (x, y, z + 2, c))


def across_y(value):
    return routed(value, lambda x, y, z, c: (x, y + 2, z, c))


def mm(a, b):
    return jnp.dot(a, b, preferred_element_type=F32)


def complex_mm(ar, ai, br, bi):
    return mm(ar, br) - mm(ai, bi), mm(ar, bi) + mm(ai, br)


def slot_of(parent, x, p, c):
    dx = (parent // 4 - x + 4) % 4
    dp = ((parent // 2) % 2 + p) % 2
    dc = (parent % 2 + c) % 2
    near = dx == 3 - 2 * c
    side = jnp.where(near, jnp.where(dc == 0, 2, 6), jnp.where(dc == 0, 7, 3))
    side = side + 6 * dp
    base = jnp.where(dx == 0, dc + 4 * dp, 10 + dc + 4 * dp)
    return jnp.where((dx == 1) | (dx == 3), side, base)


def round_up(count):
    return jnp.floor((count + (PAD - 1)) * (1.0 / PAD)) * PAD


def iota(shape, axis):
    return lax.broadcasted_iota(jnp.int32, shape, axis)


def prepare_kernel(
    where_ref, parents_ref, rows_hbm, x1_ref, goes_ref, place_ref, table_ref, sel, rows_ref, sem
):
    copy = pltpu.make_async_copy(rows_hbm, rows_ref, sem)
    copy.start()
    x, p, c = where_ref[2], where_ref[3], where_ref[1]
    triangle = (iota((ROWS, ROWS), 0) < iota((ROWS, ROWS), 1)).astype(BF16)
    node = iota((NODES, ROWS), 0)
    match = jnp.concatenate(
        [
            (node == slot_of(parents_ref[0:1, :], x, p, c)).astype(F32),
            (node == slot_of(parents_ref[1:2, :], x, p, c)).astype(F32),
        ],
        axis=0,
    )
    before = mm(match.astype(BF16), triangle)
    total = round_up(jnp.sum(match, axis=1, keepdims=True))
    lower = (iota((NODES, NODES), 1) < iota((NODES, NODES), 0)).astype(BF16)
    upper = (iota((NODES, NODES), 0) < iota((NODES, NODES), 1)).astype(BF16)
    places, rows_of_table = [], []
    for way in range(2):
        own = match[way * NODES : (way + 1) * NODES]
        padded = jnp.broadcast_to(total[way * NODES : (way + 1) * NODES], (NODES, 128)).astype(BF16)
        start = mm(lower, padded)[:, :1]
        places.append(
            jnp.sum(own * (start + before[way * NODES : (way + 1) * NODES]), axis=0, keepdims=True)
        )
        count = lax.dot_general(
            jnp.ones((8, ROWS), BF16), own.astype(BF16), (((1,), (1,)), ((), ())), preferred_element_type=F32
        )
        rows_of_table += [mm(round_up(count).astype(BF16), upper), count]
    row = iota((8, NODES), 0)
    table = jnp.where(row == 0, rows_of_table[0], 0.0)
    for k in range(1, 4):
        table = jnp.where(row == k, rows_of_table[k], table)
    table_ref[...] = table.astype(jnp.int32)

    place1 = places[0].astype(jnp.int32)
    copy.wait()
    flat = rows_ref[...].reshape(ROWS, 2 * BOND)
    step = 256
    for block in range(SORTED // step):
        spot = pl.ds(block * step, step)
        one_hot = (iota((step, ROWS), 0) + block * step == place1).astype(BF16)
        sel[spot, :] = one_hot
        sorted_rows = mm(one_hot, flat).astype(BF16)
        x1_ref[0, spot, :] = sorted_rows[:, :BOND]
        x1_ref[1, spot, :] = sorted_rows[:, BOND:]
    x1_ref[:, pl.ds(SORTED, ROOM - SORTED), :] = jnp.zeros((2, ROOM - SORTED, BOND), BF16)

    high = jnp.floor(places[1] * (1.0 / 64.0))
    low = places[1] - 64.0 * high
    which = iota((8, ROWS), 0)
    parts = jnp.where(which == 0, high + 1.0, jnp.where(which == 1, low, 0.0)).astype(BF16)
    found = lax.dot_general(parts, sel[...], (((1,), (1,)), ((), ())), preferred_element_type=F32)
    goes_ref[...] = jnp.broadcast_to((found[0:1] - 1.0) * 64.0 + found[1:2], (8, SORTED)).astype(jnp.int32)
    place_ref[...] = jnp.broadcast_to(places[1], (8, ROWS))


def select_kernel(goes_ref, place_ref, to2_ref, back_ref):
    step = 256
    for block in range(SORTED // step):
        to2_ref[pl.ds(block * step, step), :] = (
            iota((step, SORTED), 0) + block * step == goes_ref[0:1, :]
        ).astype(BF16)
    column = jnp.transpose(jnp.broadcast_to(place_ref[0:1, :], (128, ROWS))).astype(jnp.int32)[:, :1]
    for block in range(ROWS // step):
        back_ref[pl.ds(block * step, step), :] = (
            iota((step, SORTED), 1) == column[block * step : (block + 1) * step]
        ).astype(BF16)


def window(x_ref, out_ref, slot, which, begin):
    spot = pl.ds(pl.multiple_of(begin, PAD), WINDOW)
    pair = x_ref[:, spot, :].reshape(2 * WINDOW, BOND)
    by_re, by_im = mm(pair, slot[which, 0]), mm(pair, slot[which, 1])
    out_ref[0, spot, :] = (by_re[:WINDOW] - by_im[WINDOW:]).astype(BF16)
    out_ref[1, spot, :] = (by_im[:WINDOW] + by_re[WINDOW:]).astype(BF16)


def level(x_ref, out_ref, table_ref, row, slots, which):
    out_ref[:, pl.ds(ROOM - TAIL, TAIL), :] = jnp.zeros((2, TAIL, BOND), BF16)
    for k, slot in enumerate(slots):
        @pl.when(table_ref[row + 1, k] > WINDOW)
        def _(k=k, slot=slot):
            window(x_ref, out_ref, slot, which, table_ref[row, k] + WINDOW)
    for k, slot in enumerate(slots):
        window(x_ref, out_ref, slot, which, table_ref[row, k])


def rows_kernel(*refs):
    table_ref, x1_ref, to2_ref, back_ref, m_ref = refs[:5]
    slots = refs[5 : 5 + NODES]
    out_ref, first, x2, second = refs[5 + NODES :]
    level(x1_ref, first, table_ref, 0, slots, 0)
    x2[:, pl.ds(SORTED, ROOM - SORTED), :] = jnp.zeros((2, ROOM - SORTED, BOND), BF16)
    step = 256
    for block in range(SORTED // step):
        spot = pl.ds(block * step, step)
        for part in range(2):
            x2[part, spot, :] = mm(to2_ref[spot, :], first[part, pl.ds(0, SORTED), :]).astype(BF16)
    level(x2, second, table_ref, 2, slots, 1)
    spread = iota((2 * step, 2 * step), 0)
    interleave = (iota((2 * step, 2 * step), 1) == spread // 2 + step * (spread % 2)).astype(BF16)
    for block in range(ROWS // step):
        spot = pl.ds(block * step, step)
        pair = jnp.concatenate(
            [mm(back_ref[spot, :], second[part, pl.ds(0, SORTED), :]).astype(BF16) for part in range(2)], axis=0
        )
        by_re, by_im = mm(pair, m_ref[0]), mm(pair, m_ref[1])
        pair = jnp.concatenate([by_re[:step] - by_im[step:], by_im[:step] + by_re[step:]], axis=0)
        out_ref[spot] = mm(interleave, pair.astype(BF16)).astype(BF16).reshape(step, 2, BOND)


def pair_kernel(where_ref, own_ref, other_ref, p_ref, full):
    c = where_ref[1]
    for layer in range(2):
        for part in range(2):
            full[layer, part, pl.ds(pl.multiple_of(c * 128, 128), 128), :] = own_ref[layer, part]
            full[layer, part, pl.ds(pl.multiple_of((1 - c) * 128, 128), 128), :] = other_ref[layer, part]
    re, im = complex_mm(full[0, 0], full[0, 1], full[1, 0], full[1, 1])
    p_ref[0] = re.astype(BF16)
    p_ref[1] = im.astype(BF16)


def gather_ring(where_ref, refs, held):
    z, c = where_ref[0], where_ref[1]
    spots = (z, (z + 3 + 2 * c) % 4, (z + 1 + 2 - 2 * c + 2) % 4, (z + 2) % 4)
    for spot, ref in zip(spots, refs):
        held[spot] = ref[...]


def half_of(core):
    return pl.ds(pl.multiple_of(core * (BOND // 2), BOND // 2), BOND // 2)


def ring_kernel(where_ref, a_ref, b_ref, c_ref, d_ref, t_ref, held):
    gather_ring(where_ref, (a_ref, b_ref, c_ref, d_ref), held)
    rows = half_of(where_ref[1])
    re, im = held[0, 0, rows, :], held[0, 1, rows, :]
    for spot in (1, 2, 3):
        re, im = complex_mm(re, im, held[spot, 0], held[spot, 1])
        re, im = re.astype(BF16), im.astype(BF16)
    t_ref[0] = re
    t_ref[1] = im


def loop_kernel(where_ref, a_ref, b_ref, c_ref, d_ref, far_ref, far_other_ref, m_ref, held):
    gather_ring(where_ref, (a_ref, b_ref, c_ref, d_ref), held)
    z, core = where_ref[0], where_ref[1]
    for part in range(2):
        held[4, part, half_of(core), :] = far_ref[part]
        held[4, part, half_of(1 - core), :] = far_other_ref[part]
    re, im = held[z, 0], held[z, 1]
    for i in range(1, 5):
        re, im = complex_mm(re, im, held[(z + i) % 5, 0], held[(z + i) % 5, 1])
        re, im = re.astype(BF16), im.astype(BF16)
    m_ref[0] = re
    m_ref[1] = im


def vmem():
    return pl.BlockSpec(memory_space=pltpu.VMEM)


def smem():
    return pl.BlockSpec(memory_space=pltpu.SMEM)


def call(kernel, out, ins, scratch, flops, moved, room=20):
    return pl.pallas_call(
        kernel,
        out_shape=out,
        in_specs=ins,
        out_specs=jax.tree.map(lambda _: vmem(), out),
        scratch_shapes=scratch,
        cost_estimate=pl.CostEstimate(flops=flops, bytes_accessed=moved, transcendentals=0),
        compiler_params=pltpu.CompilerParams(vmem_limit_bytes=room * 2**20),
    )


def after(value, *others):
    return lax.optimization_barrier((value, *others))[0]


def body(branch_rows, first_parent, second_parent, node_first, node_second, stem_tensors):
    stem, leaf, core = (lax.axis_index(name) for name in AXES)
    where = jnp.stack([stem % 4, core, leaf // 2, leaf % 2]).astype(jnp.int32)
    matrix = jax.ShapeDtypeStruct((2, BOND, BOND), BF16)
    half = jax.ShapeDtypeStruct((2, BOND // 2, BOND), BF16)

    own = lax.optimization_barrier(jnp.concatenate([node_first, node_second], axis=0))
    with jax.named_scope("sibling"):
        sibling = swap(own)
    with jax.named_scope("side"):
        side = along_x(own)
    stem_own = stem_tensors[0]
    with jax.named_scope("stem_other"):
        stem_other = swap(stem_own)
    own_later, sibling = lax.optimization_barrier((own, sibling))
    with jax.named_scope("side_far"):
        side_far = along_x(sibling)
    with jax.named_scope("turned"):
        turned = along_y(own_later)

    product = call(pair_kernel, matrix, [smem(), vmem(), vmem()],
                   [pltpu.VMEM((2, 2, BOND, BOND), BF16)], 2**28, 2**20)(after(where, sibling), stem_own, stem_other)
    with jax.named_scope("near"):
        near = along_z(product)
    with jax.named_scope("opposite"):
        opposite = across_z(product)

    hbm = pl.BlockSpec(memory_space=pltpu.HBM)
    parents = jnp.concatenate([first_parent.reshape(1, ROWS), second_parent.reshape(1, ROWS)], axis=0)
    side_later = after(side, product, turned)
    with jax.named_scope("side_turned"):
        side_turned = along_y(side_later)
    with jax.named_scope("across"):
        across = along_x(side_later)
    with jax.named_scope("near_other"):
        near_other = swap(near)
    with jax.named_scope("side_far_turned"):
        side_far_turned = along_y(after(side_far, product))
    ring = (product, near, near_other, opposite)
    total = call(ring_kernel, half, [smem()] + [vmem()] * 4,
                 [pltpu.VMEM((4, 2, BOND, BOND), BF16)], 2**29, 2**20)(where, *ring)
    with jax.named_scope("far"):
        far = across_y(total)
    with jax.named_scope("across_turned"):
        across_turned = along_y(after(across, total))
    x1, goes, place, table = call(
        prepare_kernel,
        (
            jax.ShapeDtypeStruct((2, ROOM, BOND), BF16),
            jax.ShapeDtypeStruct((8, SORTED), jnp.int32),
            jax.ShapeDtypeStruct((8, ROWS), F32),
            jax.ShapeDtypeStruct((8, NODES), jnp.int32),
        ),
        [smem(), vmem(), hbm],
        [
            pltpu.VMEM((SORTED, ROWS), BF16),
            pltpu.VMEM((ROWS, 2, BOND), BF16),
            pltpu.SemaphoreType.DMA,
        ],
        2**31, 2**22,
    )(after(where, across, total), parents, branch_rows)
    to2, back = call(
        select_kernel,
        (jax.ShapeDtypeStruct((SORTED, SORTED), BF16), jax.ShapeDtypeStruct((ROWS, SORTED), BF16)),
        [vmem(), vmem()], [], 2**30, 2**22,
    )(after(goes, side_turned), place)
    with jax.named_scope("far_other"):
        far_other = swap(far)
    loop = call(loop_kernel, matrix, [smem()] + [vmem()] * 6,
                [pltpu.VMEM((5, 2, BOND, BOND), BF16)], 2**29, 2**20)(where, *ring, far, far_other)

    slots = [own, sibling]
    for value in (side, turned, side_far, side_turned, across, side_far_turned, across_turned):
        with jax.named_scope("shared"):
            slots += [value, swap(after(value, to2))]

    return call(
        rows_kernel,
        jax.ShapeDtypeStruct((ROWS, 2, BOND), BF16),
        [smem()] + [vmem()] * (4 + NODES),
        [pltpu.VMEM((2, ROOM, BOND), BF16)] * 3,
        2**33, 2**24,
    )(table, x1, to2, back, loop, *slots)


def solution(mesh):
    return jax.shard_map(
        body,
        mesh=mesh,
        in_specs=(
            P(AXES, None, None),
            P(AXES, None),
            P(AXES, None),
            P(("leaf", "slab"), None, None, None),
            P(("leaf", "slab"), None, None, None),
            P("stem", None, None, "slab", None),
        ),
        out_specs=P(AXES, None, None),
        check_vma=False,
    )
```

time: 80.2 us -> 60 us (0.75)
  starting transfers between devices: 37.2 us -> 26.9 us
  local copies, waits for them, and re-layouts: 8.73 us -> 0.95 us
  Pallas kernels: 22.5 us -> 20.3 us
  waiting for transfers between devices: 11.1 us -> 9.14 us
  other arithmetic: 0.3 us -> 1.96 us
    ppermute x20 -> x21, starting transfers between devices: 37.2 us -> 26.9 us  [routed(): return lax.ppermute(value, AXES, pairs)]
    unnamed x32 -> x4, local copies, waits for them, and re-layouts: 5.72 us -> 0.95 us
    pallas_call x4 -> x5, Pallas kernels: 21.7 us -> 19.4 us  [the longest x1 11.2 us: body(): call(rows_kernel, jax.ShapeDtypeStruct((ROWS, 2, BOND), BF16), [smem()] +...]
    transpose x1 -> x0, local copies, waits for them, and re-layouts: 2.05 us -> none  [body(): return jnp.transpose(out, (1, 0, 2))]
    ppermute x20 -> x21, waiting for transfers between devices: 11.1 us -> 9.14 us  [routed(): return lax.ppermute(value, AXES, pairs)]
    concatenate x0 -> x2, other arithmetic: none -> 1.88 us  [the longest x1 1.17 us: body(): jnp.concatenate([node_first, node_second], axis=0)]
    concatenate x1 -> x0, local copies, waits for them, and re-layouts: 0.97 us -> none  [body(): own = jnp.concatenate([node_first, node_second], axis=0)]
  transfers between devices with their start and end apart: 20 -> 21, of which waited for: 5 -> 6; matrix products, arithmetic and copies ran while one was open for 2% -> 1% of each run, Pallas kernels for 8% -> 15%
where the time goes in v2:
time: 60 us; the launch traced here: 59.4 us
  starting transfers between devices  26.9 us (45%)
  Pallas kernels  20.3 us (34%)
  waiting for transfers between devices  9.14 us (15%)
  other arithmetic  1.96 us (3%)
  local copies, waits for them, and re-layouts  0.95 us (2%)
    ppermute x21, starting transfers between devices, routed(): return lax.ppermute(value, AXES, pairs)  26.9 us
    pallas_call x1, Pallas kernels, body(): call(rows_kernel, jax.ShapeDtypeStruct((ROWS, 2, BOND), BF16), [smem()] +...  11.2 us
    ppermute x21, waiting for transfers between devices, routed(): return lax.ppermute(value, AXES, pairs)  9.14 us
    pallas_call x1, Pallas kernels, body(): call(prepare_kernel, (jax.ShapeDtypeStruct((2, ROOM, BOND), BF16), jax.Sh...  3.77 us
    pallas_call x1, Pallas kernels, body(): call(select_kernel, (jax.ShapeDtypeStruct((SORTED, SORTED), BF16), jax.Sh...  1.65 us
    pallas_call x1, Pallas kernels, body(): call(loop_kernel, matrix, [smem()] + [vmem()] * 6, [pltpu.VMEM((5, 2, BON...  1.57 us
  transfers between devices with their start and end apart: 21, of which 6 were waited for; matrix products, arithmetic and copies ran while one was open for 1% of the time, Pallas kernels for 15%

profile of v2, /device:TPU:1, one launch (start us, length us, event | category | flops | bytes accessed | tf_op | source)
XLA Modules:
  0.0 59.4 jit_solution(14080777080796465861)
XLA Ops:
  0.0 1.2 %pad_maximum_fusion.refs_5_ = bf16[2,2,256,256]{3,2,1,0:T(8,128)(2,1)S(1)} fusion(bf16[1,2,256,256]{3,2,1,0:T(8,128)(2,1)} %param.10, bf16[1,2,256,256]{3,2,1,0:T(8,128)(2,1)} %param.9), kind=kLoop, calls=%fused_computation | loop fusion | flops 262144 | bytes 1048576 | tf_op jit(solution)/shard_map/concatenate | solution.py:278
  1.2 1.5 %collective-permute-start.1 = (bf16[2,2,256,256]{3,2,1,0:T(8,128)(2,1)S(1)}, bf16[2,2,256,256]{3,2,1,0:T(8,128)(2,1)S(1)}, u32[]{:S(2)}, u32[]{:S(2)}) collective-permute-start(bf16[2,2,256,256]{3,2,1,0:T(8,128)(2,1)S(1)} %pad_maximum_fusion.refs_5_), channel_id=1, source_target_pairs={{0,1},{1,0},{16,17},{17,16},{32,33},{33,32},{48,49},{49,48},{2,3},... | collective-permute-start | bytes 1572872 | tf_op jit(solution)/shard_map/sibling/ppermute | solution.py:33
  2.7 2.6 %collective-permute-start = (bf16[2,2,256,256]{3,2,1,0:T(8,128)(2,1)S(1)}, bf16[2,2,256,256]{3,2,1,0:T(8,128)(2,1)S(1)}, u32[]{:S(2)}, u32[]{:S(2)}) collective-permute-start(bf16[2,2,256,256]{3,2,1,0:T(8,128)(2,1)S(1)} %pad_maximum_fusion.refs_5_), channel_id=1, source_target_pairs={{0,4},{1,13},{16,20},{17,29},{32,36},{33,45},{48,52},{49,61},{2,6}... | collective-permute-start | bytes 1572872 | tf_op jit(solution)/shard_map/side/ppermute | solution.py:33
  5.2 2.7 %collective-permute-start.3 = (bf16[2,2,256,256]{3,2,1,0:T(8,128)(2,1)S(1)}, bf16[2,2,256,256]{3,2,1,0:T(8,128)(2,1)S(1)}, u32[]{:S(2)}, u32[]{:S(2)}) collective-permute-start(bf16[2,2,256,256]{3,2,1,0:T(8,128)(2,1)S(1)} %pad_maximum_fusion.refs_5_), channel_id=1, source_target_pairs={{0,2},{1,67},{16,18},{17,83},{32,34},{33,99},{48,50},{49,115},{2,6... | collective-permute-start | bytes 1572872 | tf_op jit(solution)/shard_map/turned/ppermute | solution.py:33
  8.1 1.5 %collective-permute-start.13 = (bf16[2,2,256,256]{3,2,1,0:T(8,128)(2,1)S(1)}, bf16[2,2,256,256]{3,2,1,0:T(8,128)(2,1)S(1)}, u32[]{:S(2)}, u32[]{:S(2)}) collective-permute-start(bf16[2,2,256,256]{3,2,1,0:T(8,128)(2,1)S(1)} %collective-permute-done.1.refs_6_), channel_id=1, source_target_pairs={{0,4},{1,13},{16,20},{17,29},{32,36},{33,45},{48,52},{49,61},{2,6}... | collective-permute-start | bytes 1572872 | tf_op jit(solution)/shard_map/side_far/ppermute | solution.py:33
  9.7 0.9 %copy-done.1 = bf16[1,2,2,128,256]{4,3,2,1,0:T(8,128)(2,1)S(1)} copy-done((bf16[1,2,2,128,256]{4,3,2,1,0:T(8,128)(2,1)S(1)}, bf16[1,2,2,128,256]{4,3,2,1,0:T(8,128)(2,1)}, u32[]{:S(2)}) %copy-start.1) | copy-done | bytes 262168
  10.7 0.9 %shard_map.64.a_ref = bf16[2,256,256]{2,1,0:T(8,128)(2,1)S(1)} custom-call(s32[4]{0:T(128)S(1)} %pad_add_fusion.1.where_ref, bf16[2,2,128,256]{3,2,1,0:T(8,128)(2,1)S(1)} %bitcast.8, bf16[2,2,128,256]{3,2,1,0:T(8,128)(2,1)S(1)} %collective-permute-done.2.other_ref), custom_call_target="tpu_custom_call" | custom-call | flops 268435456 | bytes 1048576 | tf_op jit(solution)/shard_map/pallas_call | solution.py:292
  11.6 3.8 %collective-permute-start.5 = (bf16[2,256,256]{2,1,0:T(8,128)(2,1)S(1)}, bf16[2,256,256]{2,1,0:T(8,128)(2,1)S(1)}, u32[]{:S(2)}, u32[]{:S(2)}) collective-permute-start(bf16[2,256,256]{2,1,0:T(8,128)(2,1)S(1)} %shard_map.64.a_ref), channel_id=1, source_target_pairs={{0,16},{1,49},{16,32},{17,1},{32,48},{33,17},{48,0},{49,33},{2,18}... | collective-permute-start | bytes 786440 | tf_op jit(solution)/shard_map/near/ppermute | solution.py:33
  15.4 1.5 %collective-permute-start.4 = (bf16[2,2,256,256]{3,2,1,0:T(8,128)(2,1)S(1)}, bf16[2,2,256,256]{3,2,1,0:T(8,128)(2,1)S(1)}, u32[]{:S(2)}, u32[]{:S(2)}) collective-permute-start(bf16[2,2,256,256]{3,2,1,0:T(8,128)(2,1)S(1)} %collective-permute-done.refs_7_), channel_id=1, source_target_pairs={{0,4},{1,13},{16,20},{17,29},{32,36},{33,45},{48,52},{49,61},{2,6}... | collective-permute-start | bytes 1572872 | tf_op jit(solution)/shard_map/across/ppermute | solution.py:33
  16.9 1.8 %collective-permute-start.8 = (bf16[2,2,256,256]{3,2,1,0:T(8,128)(2,1)S(1)}, bf16[2,2,256,256]{3,2,1,0:T(8,128)(2,1)S(1)}, u32[]{:S(2)}, u32[]{:S(2)}) collective-permute-start(bf16[2,2,256,256]{3,2,1,0:T(8,128)(2,1)S(1)} %collective-permute-done.refs_7_), channel_id=1, source_target_pairs={{0,2},{1,67},{16,18},{17,83},{32,34},{33,99},{48,50},{49,115},{2,6... | collective-permute-start | bytes 1572872 | tf_op jit(solution)/shard_map/side_turned/ppermute | solution.py:33
  18.8 3.6 %collective-permute-start.7 = (bf16[2,256,256]{2,1,0:T(8,128)(2,1)S(1)}, bf16[2,256,256]{2,1,0:T(8,128)(2,1)S(1)}, u32[]{:S(2)}, u32[]{:S(2)}) collective-permute-start(bf16[2,256,256]{2,1,0:T(8,128)(2,1)S(1)} %shard_map.64.a_ref), channel_id=1, source_target_pairs={{0,32},{1,33},{16,48},{17,49},{32,0},{33,1},{48,16},{49,17},{2,34}... | collective-permute-start | bytes 786440 | tf_op jit(solution)/shard_map/opposite/ppermute | solution.py:33
  22.4 0.7 %pad_add_fusion.parents_ref = s32[2,1024]{1,0:T(2,128)S(1)} fusion(s32[1,1024]{1,0:T(1,128)} %bitcast.9, s32[1,1024]{1,0:T(1,128)} %bitcast.10), kind=kLoop, calls=%fused_computation.1 | loop fusion | flops 2048 | bytes 16384 | tf_op jit(solution)/shard_map/concatenate | solution.py:300
  23.1 1.1 %collective-permute-start.17 = (bf16[2,2,256,256]{3,2,1,0:T(8,128)(2,1)S(1)}, bf16[2,2,256,256]{3,2,1,0:T(8,128)(2,1)S(1)}, u32[]{:S(2)}, u32[]{:S(2)}) collective-permute-start(bf16[2,2,256,256]{3,2,1,0:T(8,128)(2,1)S(1)} %collective-permute-done.13.refs_11_), channel_id=1, source_target_pairs={{0,2},{1,67},{16,18},{17,83},{32,34},{33,99},{48,50},{49,115},{2,6... | collective-permute-start | bytes 1572872 | tf_op jit(solution)/shard_map/side_far_turned/ppermute | solution.py:33
  24.2 3.1 %collective-permute-done.7.d_ref = bf16[2,256,256]{2,1,0:T(8,128)(2,1)S(1)} collective-permute-done((bf16[2,256,256]{2,1,0:T(8,128)(2,1)S(1)}, bf16[2,256,256]{2,1,0:T(8,128)(2,1)S(1)}, u32[]{:S(2)}, u32[]{:S(2)}) %collective-permute-start.7) | collective-permute-done | bytes 262176 | tf_op jit(solution)/shard_map/opposite/ppermute | solution.py:33
  27.3 1.2 %shard_map.65 = bf16[2,128,256]{2,1,0:T(8,128)(2,1)S(1)} custom-call(s32[4]{0:T(128)S(1)} %pad_add_fusion.1.where_ref, bf16[2,256,256]{2,1,0:T(8,128)(2,1)S(1)} %shard_map.64.a_ref, bf16[2,256,256]{2,1,0:T(8,128)(2,1)S(1)} %collective-permute-done.5.b_ref, bf16[2,256,256]{2,1,0:T(8,128)(2,1)S(1)} %collective-permute-done.6.c_ref, ...), custom_call_target="tpu_custom_call" | custom-call | flops 536870912 | bytes 1048576 | tf_op jit(solution)/shard_map/pallas_call | solution.py:311
  28.5 1.1 %collective-permute-start.19 = (bf16[2,2,256,256]{3,2,1,0:T(8,128)(2,1)S(1)}, bf16[2,2,256,256]{3,2,1,0:T(8,128)(2,1)S(1)}, u32[]{:S(2)}, u32[]{:S(2)}) collective-permute-start(bf16[2,2,256,256]{3,2,1,0:T(8,128)(2,1)S(1)} %collective-permute-done.4.refs_15_), channel_id=1, source_target_pairs={{0,2},{1,67},{16,18},{17,83},{32,34},{33,99},{48,50},{49,115},{2,6... | collective-permute-start | bytes 1572872 | tf_op jit(solution)/shard_map/across_turned/ppermute | solution.py:33
  29.6 3.8 %shard_map.66 = (bf16[2,1440,256]{2,1,0:T(8,128)(2,1)S(1)}, s32[8,1280]{1,0:T(8,128)S(1)}, f32[8,1024]{1,0:T(8,128)S(1)}, s32[8,16]{1,0:T(8,128)S(1)}) custom-call(s32[4]{0:T(128)S(1)} %pad_add_fusion.1.where_ref, s32[2,1024]{1,0:T(2,128)S(1)} %pad_add_fusion.parents_ref, bf16[1024,2,256]{2,1,0:T(2,128)(2,1)S(1)} %copy-done), custom_call_target="tpu_custom_call" | custom-call | flops 2147483648 | bytes 4194304 | tf_op jit(solution)/shard_map/pallas_call | solution.py:317
  33.4 1.7 %shard_map.67 = (bf16[1280,1280]{1,0:T(8,128)(2,1)S(1)}, bf16[1024,1280]{1,0:T(8,128)(2,1)S(1)}) custom-call(s32[8,1280]{1,0:T(8,128)S(1)} %get-tuple-element.34.goes_ref, f32[8,1024]{1,0:T(8,128)S(1)} %get-tuple-element.35.place_ref), custom_call_target="tpu_custom_call" | custom-call | flops 1073741824 | bytes 4194304 | tf_op jit(solution)/shard_map/pallas_call | solution.py:333
  35.8 2.2 %collective-permute-start.9 = (bf16[2,128,256]{2,1,0:T(8,128)(2,1)S(1)}, bf16[2,128,256]{2,1,0:T(8,128)(2,1)S(1)}, u32[]{:S(2)}, u32[]{:S(2)}) collective-permute-start(bf16[2,128,256]{2,1,0:T(8,128)(2,1)S(1)} %shard_map.65), channel_id=1, source_target_pairs={{0,64},{1,65},{16,80},{17,81},{32,96},{33,97},{48,112},{49,113},{2... | collective-permute-start | bytes 393224 | tf_op jit(solution)/shard_map/far/ppermute | solution.py:33
  38.0 4.0 %collective-permute-done.9.far_ref = bf16[2,128,256]{2,1,0:T(8,128)(2,1)S(1)} collective-permute-done((bf16[2,128,256]{2,1,0:T(8,128)(2,1)S(1)}, bf16[2,128,256]{2,1,0:T(8,128)(2,1)S(1)}, u32[]{:S(2)}, u32[]{:S(2)}) %collective-permute-start.9) | collective-permute-done | bytes 131104 | tf_op jit(solution)/shard_map/far/ppermute | solution.py:33
  42.0 1.3 %collective-permute-start.10 = (bf16[2,128,256]{2,1,0:T(8,128)(2,1)S(1)}, bf16[2,128,256]{2,1,0:T(8,128)(2,1)S(1)}, u32[]{:S(2)}, u32[]{:S(2)}) collective-permute-start(bf16[2,128,256]{2,1,0:T(8,128)(2,1)S(1)} %collective-permute-done.9.far_ref), channel_id=1, source_target_pairs={{0,1},{1,0},{16,17},{17,16},{32,33},{33,32},{48,49},{49,48},{2,3},... | collective-permute-start | bytes 393224 | tf_op jit(solution)/shard_map/far_other/ppermute | solution.py:33
  45.1 1.6 %shard_map.68.refs_4_ = bf16[2,256,256]{2,1,0:T(8,128)(2,1)S(1)} custom-call(s32[4]{0:T(128)S(1)} %pad_add_fusion.1.where_ref, bf16[2,256,256]{2,1,0:T(8,128)(2,1)S(1)} %shard_map.64.a_ref, bf16[2,256,256]{2,1,0:T(8,128)(2,1)S(1)} %collective-permute-done.5.b_ref, bf16[2,256,256]{2,1,0:T(8,128)(2,1)S(1)} %collective-permute-done.6.c_ref, ...), custom_call_target="tpu_custom_call" | custom-call | flops 536870912 | bytes 1048576 | tf_op jit(solution)/shard_map/pallas_call | solution.py:340
  47.4 0.7 %collective-permute-done.20.refs_20_ = bf16[2,2,256,256]{3,2,1,0:T(8,128)(2,1)S(1)} collective-permute-done((bf16[2,2,256,256]{3,2,1,0:T(8,128)(2,1)S(1)}, bf16[2,2,256,256]{3,2,1,0:T(8,128)(2,1)S(1)}, u32[]{:S(2)}, u32[]{:S(2)}) %collective-permute-start.20) | collective-permute-done | bytes 524320 | tf_op jit(solution)/shard_map/shared/ppermute | solution.py:33
  48.1 11.2 %shard_map.69 = bf16[1024,2,256]{2,1,0:T(2,128)(2,1)} custom-call(s32[8,16]{1,0:T(8,128)S(1)} %get-tuple-element.31.refs_0_, bf16[2,1440,256]{2,1,0:T(8,128)(2,1)S(1)} %get-tuple-element.32.refs_1_, bf16[1280,1280]{1,0:T(8,128)(2,1)S(1)} %get-tuple-element.36.refs_2_, bf16[1024,1280]{1,0:T(8,128)(2,1)S(1)} %get-tuple-element.37.refs_3_, ...), custom_call_target="tpu_custom_call" | custom-call | flops 8589934592 | bytes 16777216 | tf_op jit(solution)/shard_map/pallas_call | solution.py:348
  (31 shorter events, 3.6 us)
Async XLA Ops:
  0.0 29.6 %copy-start = (bf16[1024,2,256]{2,1,0:T(2,128)(2,1)S(1)}, bf16[1024,2,256]{2,1,0:T(2,128)(2,1)}, u32[]{:S(2)}) copy-start(bf16[1024,2,256]{2,1,0:T(2,128)(2,1)} %rows_hbm.1) | copy-start | bytes 3145732
  1.2 4.1 %collective-permute-start.1 = (bf16[2,2,256,256]{3,2,1,0:T(8,128)(2,1)S(1)}, bf16[2,2,256,256]{3,2,1,0:T(8,128)(2,1)S(1)}, u32[]{:S(2)}, u32[]{:S(2)}) collective-permute-start(bf16[2,2,256,256]{3,2,1,0:T(8,128)(2,1)S(1)} %pad_maximum_fusion.refs_5_), channel_id=1, source_target_pairs={{0,1},{1,0},{16,17},{17,16},{32,33},{33,32},{48,49},{49,48},{2,3},... | collective-permute-start | bytes 1572872 | tf_op jit(solution)/shard_map/sibling/ppermute | solution.py:33
  2.7 12.7 %collective-permute-start = (bf16[2,2,256,256]{3,2,1,0:T(8,128)(2,1)S(1)}, bf16[2,2,256,256]{3,2,1,0:T(8,128)(2,1)S(1)}, u32[]{:S(2)}, u32[]{:S(2)}) collective-permute-start(bf16[2,2,256,256]{3,2,1,0:T(8,128)(2,1)S(1)} %pad_maximum_fusion.refs_5_), channel_id=1, source_target_pairs={{0,4},{1,13},{16,20},{17,29},{32,36},{33,45},{48,52},{49,61},{2,6}... | collective-permute-start | bytes 1572872 | tf_op jit(solution)/shard_map/side/ppermute | solution.py:33
  5.2 10.1 %collective-permute-start.3 = (bf16[2,2,256,256]{3,2,1,0:T(8,128)(2,1)S(1)}, bf16[2,2,256,256]{3,2,1,0:T(8,128)(2,1)S(1)}, u32[]{:S(2)}, u32[]{:S(2)}) collective-permute-start(bf16[2,2,256,256]{3,2,1,0:T(8,128)(2,1)S(1)} %pad_maximum_fusion.refs_5_), channel_id=1, source_target_pairs={{0,2},{1,67},{16,18},{17,83},{32,34},{33,99},{48,50},{49,115},{2,6... | collective-permute-start | bytes 1572872 | tf_op jit(solution)/shard_map/turned/ppermute | solution.py:33
  8.0 1.7 %collective-permute-start.2 = (bf16[2,2,128,256]{3,2,1,0:T(8,128)(2,1)}, bf16[2,2,128,256]{3,2,1,0:T(8,128)(2,1)S(1)}, u32[]{:S(2)}, u32[]{:S(2)}) collective-permute-start(bf16[2,2,128,256]{3,2,1,0:T(8,128)(2,1)} %bitcast.7), channel_id=1, source_target_pairs={{0,1},{1,0},{16,17},{17,16},{32,33},{33,32},{48,49},{49,48},{2,3},... | collective-permute-start | bytes 786440 | tf_op jit(solution)/shard_map/stem_other/ppermute | solution.py:33
  8.1 15.0 %collective-permute-start.13 = (bf16[2,2,256,256]{3,2,1,0:T(8,128)(2,1)S(1)}, bf16[2,2,256,256]{3,2,1,0:T(8,128)(2,1)S(1)}, u32[]{:S(2)}, u32[]{:S(2)}) collective-permute-start(bf16[2,2,256,256]{3,2,1,0:T(8,128)(2,1)S(1)} %collective-permute-done.1.refs_6_), channel_id=1, source_target_pairs={{0,4},{1,13},{16,20},{17,29},{32,36},{33,45},{48,52},{49,61},{2,6}... | collective-permute-start | bytes 1572872 | tf_op jit(solution)/shard_map/side_far/ppermute | solution.py:33
  9.7 1.0 %copy-start.1 = (bf16[1,2,2,128,256]{4,3,2,1,0:T(8,128)(2,1)S(1)}, bf16[1,2,2,128,256]{4,3,2,1,0:T(8,128)(2,1)}, u32[]{:S(2)}) copy-start(bf16[1,2,2,128,256]{4,3,2,1,0:T(8,128)(2,1)} %param.11) | copy-start | bytes 786436
  11.6 10.8 %collective-permute-start.5 = (bf16[2,256,256]{2,1,0:T(8,128)(2,1)S(1)}, bf16[2,256,256]{2,1,0:T(8,128)(2,1)S(1)}, u32[]{:S(2)}, u32[]{:S(2)}) collective-permute-start(bf16[2,256,256]{2,1,0:T(8,128)(2,1)S(1)} %shard_map.64.a_ref), channel_id=1, source_target_pairs={{0,16},{1,49},{16,32},{17,1},{32,48},{33,17},{48,0},{49,33},{2,18}... | collective-permute-start | bytes 786440 | tf_op jit(solution)/shard_map/near/ppermute | solution.py:33
  15.4 13.1 %collective-permute-start.4 = (bf16[2,2,256,256]{3,2,1,0:T(8,128)(2,1)S(1)}, bf16[2,2,256,256]{3,2,1,0:T(8,128)(2,1)S(1)}, u32[]{:S(2)}, u32[]{:S(2)}) collective-permute-start(bf16[2,2,256,256]{3,2,1,0:T(8,128)(2,1)S(1)} %collective-permute-done.refs_7_), channel_id=1, source_target_pairs={{0,4},{1,13},{16,20},{17,29},{32,36},{33,45},{48,52},{49,61},{2,6}... | collective-permute-start | bytes 1572872 | tf_op jit(solution)/shard_map/across/ppermute | solution.py:33
  16.9 16.4 %collective-permute-start.8 = (bf16[2,2,256,256]{3,2,1,0:T(8,128)(2,1)S(1)}, bf16[2,2,256,256]{3,2,1,0:T(8,128)(2,1)S(1)}, u32[]{:S(2)}, u32[]{:S(2)}) collective-permute-start(bf16[2,2,256,256]{3,2,1,0:T(8,128)(2,1)S(1)} %collective-permute-done.refs_7_), channel_id=1, source_target_pairs={{0,2},{1,67},{16,18},{17,83},{32,34},{33,99},{48,50},{49,115},{2,6... | collective-permute-start | bytes 1572872 | tf_op jit(solution)/shard_map/side_turned/ppermute | solution.py:33
  18.8 8.5 %collective-permute-start.7 = (bf16[2,256,256]{2,1,0:T(8,128)(2,1)S(1)}, bf16[2,256,256]{2,1,0:T(8,128)(2,1)S(1)}, u32[]{:S(2)}, u32[]{:S(2)}) collective-permute-start(bf16[2,256,256]{2,1,0:T(8,128)(2,1)S(1)} %shard_map.64.a_ref), channel_id=1, source_target_pairs={{0,32},{1,33},{16,48},{17,49},{32,0},{33,1},{48,16},{49,17},{2,34}... | collective-permute-start | bytes 786440 | tf_op jit(solution)/shard_map/opposite/ppermute | solution.py:33
  22.4 4.9 %collective-permute-start.6 = (bf16[2,256,256]{2,1,0:T(8,128)(2,1)S(1)}, bf16[2,256,256]{2,1,0:T(8,128)(2,1)S(1)}, u32[]{:S(2)}, u32[]{:S(2)}) collective-permute-start(bf16[2,256,256]{2,1,0:T(8,128)(2,1)S(1)} %collective-permute-done.5.b_ref), channel_id=1, source_target_pairs={{0,1},{1,0},{16,17},{17,16},{32,33},{33,32},{48,49},{49,48},{2,3},... | collective-permute-start | bytes 786440 | tf_op jit(solution)/shard_map/near_other/ppermute | solution.py:33
  23.1 20.1 %collective-permute-start.17 = (bf16[2,2,256,256]{3,2,1,0:T(8,128)(2,1)S(1)}, bf16[2,2,256,256]{3,2,1,0:T(8,128)(2,1)S(1)}, u32[]{:S(2)}, u32[]{:S(2)}) collective-permute-start(bf16[2,2,256,256]{3,2,1,0:T(8,128)(2,1)S(1)} %collective-permute-done.13.refs_11_), channel_id=1, source_target_pairs={{0,2},{1,67},{16,18},{17,83},{32,34},{33,99},{48,50},{49,115},{2,6... | collective-permute-start | bytes 1572872 | tf_op jit(solution)/shard_map/side_far_turned/ppermute | solution.py:33
  28.5 14.8 %collective-permute-start.19 = (bf16[2,2,256,256]{3,2,1,0:T(8,128)(2,1)S(1)}, bf16[2,2,256,256]{3,2,1,0:T(8,128)(2,1)S(1)}, u32[]{:S(2)}, u32[]{:S(2)}) collective-permute-start(bf16[2,2,256,256]{3,2,1,0:T(8,128)(2,1)S(1)} %collective-permute-done.4.refs_15_), channel_id=1, source_target_pairs={{0,2},{1,67},{16,18},{17,83},{32,34},{33,99},{48,50},{49,115},{2,6... | collective-permute-start | bytes 1572872 | tf_op jit(solution)/shard_map/across_turned/ppermute | solution.py:33
  35.0 9.6 %collective-permute-start.11 = (bf16[2,2,256,256]{3,2,1,0:T(8,128)(2,1)S(1)}, bf16[2,2,256,256]{3,2,1,0:T(8,128)(2,1)S(1)}, u32[]{:S(2)}, u32[]{:S(2)}) collective-permute-start(bf16[2,2,256,256]{3,2,1,0:T(8,128)(2,1)S(1)} %collective-permute-done.refs_7_), channel_id=1, source_target_pairs={{0,1},{1,0},{16,17},{17,16},{32,33},{33,32},{48,49},{49,48},{2,3},... | collective-permute-start | bytes 1572872 | tf_op jit(solution)/shard_map/shared/ppermute | solution.py:33
  35.7 9.0 %collective-permute-start.12 = (bf16[2,2,256,256]{3,2,1,0:T(8,128)(2,1)S(1)}, bf16[2,2,256,256]{3,2,1,0:T(8,128)(2,1)S(1)}, u32[]{:S(2)}, u32[]{:S(2)}) collective-permute-start(bf16[2,2,256,256]{3,2,1,0:T(8,128)(2,1)S(1)} %collective-permute-done.3.refs_9_), channel_id=1, source_target_pairs={{0,1},{1,0},{16,17},{17,16},{32,33},{33,32},{48,49},{49,48},{2,3},... | collective-permute-start | bytes 1572872 | tf_op jit(solution)/shard_map/shared/ppermute | solution.py:33
  35.8 6.2 %collective-permute-start.9 = (bf16[2,128,256]{2,1,0:T(8,128)(2,1)S(1)}, bf16[2,128,256]{2,1,0:T(8,128)(2,1)S(1)}, u32[]{:S(2)}, u32[]{:S(2)}) collective-permute-start(bf16[2,128,256]{2,1,0:T(8,128)(2,1)S(1)} %shard_map.65), channel_id=1, source_target_pairs={{0,64},{1,65},{16,80},{17,81},{32,96},{33,97},{48,112},{49,113},{2... | collective-permute-start | bytes 393224 | tf_op jit(solution)/shard_map/far/ppermute | solution.py:33
  42.0 2.2 %collective-permute-start.10 = (bf16[2,128,256]{2,1,0:T(8,128)(2,1)S(1)}, bf16[2,128,256]{2,1,0:T(8,128)(2,1)S(1)}, u32[]{:S(2)}, u32[]{:S(2)}) collective-permute-start(bf16[2,128,256]{2,1,0:T(8,128)(2,1)S(1)} %collective-permute-done.9.far_ref), channel_id=1, source_target_pairs={{0,1},{1,0},{16,17},{17,16},{32,33},{33,32},{48,49},{49,48},{2,3},... | collective-permute-start | bytes 393224 | tf_op jit(solution)/shard_map/far_other/ppermute | solution.py:33
  43.2 3.4 %collective-permute-start.14 = (bf16[2,2,256,256]{3,2,1,0:T(8,128)(2,1)S(1)}, bf16[2,2,256,256]{3,2,1,0:T(8,128)(2,1)S(1)}, u32[]{:S(2)}, u32[]{:S(2)}) collective-permute-start(bf16[2,2,256,256]{3,2,1,0:T(8,128)(2,1)S(1)} %collective-permute-done.13.refs_11_), channel_id=1, source_target_pairs={{0,1},{1,0},{16,17},{17,16},{32,33},{33,32},{48,49},{49,48},{2,3},... | collective-permute-start | bytes 1572872 | tf_op jit(solution)/shard_map/shared/ppermute | solution.py:33
  43.2 3.4 %collective-permute-start.15 = (bf16[2,2,256,256]{3,2,1,0:T(8,128)(2,1)S(1)}, bf16[2,2,256,256]{3,2,1,0:T(8,128)(2,1)S(1)}, u32[]{:S(2)}, u32[]{:S(2)}) collective-permute-start(bf16[2,2,256,256]{3,2,1,0:T(8,128)(2,1)S(1)} %collective-permute-done.8.refs_13_), channel_id=1, source_target_pairs={{0,1},{1,0},{16,17},{17,16},{32,33},{33,32},{48,49},{49,48},{2,3},... | collective-permute-start | bytes 1572872 | tf_op jit(solution)/shard_map/shared/ppermute | solution.py:33
  44.2 2.5 %collective-permute-start.16 = (bf16[2,2,256,256]{3,2,1,0:T(8,128)(2,1)S(1)}, bf16[2,2,256,256]{3,2,1,0:T(8,128)(2,1)S(1)}, u32[]{:S(2)}, u32[]{:S(2)}) collective-permute-start(bf16[2,2,256,256]{3,2,1,0:T(8,128)(2,1)S(1)} %collective-permute-done.4.refs_15_), channel_id=1, source_target_pairs={{0,1},{1,0},{16,17},{17,16},{32,33},{33,32},{48,49},{49,48},{2,3},... | collective-permute-start | bytes 1572872 | tf_op jit(solution)/shard_map/shared/ppermute | solution.py:33
  44.6 2.8 %collective-permute-start.18 = (bf16[2,2,256,256]{3,2,1,0:T(8,128)(2,1)S(1)}, bf16[2,2,256,256]{3,2,1,0:T(8,128)(2,1)S(1)}, u32[]{:S(2)}, u32[]{:S(2)}) collective-permute-start(bf16[2,2,256,256]{3,2,1,0:T(8,128)(2,1)S(1)} %collective-permute-done.17.refs_17_), channel_id=1, source_target_pairs={{0,1},{1,0},{16,17},{17,16},{32,33},{33,32},{48,49},{49,48},{2,3},... | collective-permute-start | bytes 1572872 | tf_op jit(solution)/shard_map/shared/ppermute | solution.py:33
  44.7 3.4 %collective-permute-start.20 = (bf16[2,2,256,256]{3,2,1,0:T(8,128)(2,1)S(1)}, bf16[2,2,256,256]{3,2,1,0:T(8,128)(2,1)S(1)}, u32[]{:S(2)}, u32[]{:S(2)}) collective-permute-start(bf16[2,2,256,256]{3,2,1,0:T(8,128)(2,1)S(1)} %collective-permute-done.19.refs_19_), channel_id=1, source_target_pairs={{0,1},{1,0},{16,17},{17,16},{32,33},{33,32},{48,49},{49,48},{2,3},... | collective-permute-start | bytes 1572872 | tf_op jit(solution)/shard_map/shared/ppermute | solution.py:33

commit v3 on v2

--- a/solution.py
+++ b/solution.py
@@ -63,6 +63,10 @@
 
 def complex_mm(ar, ai, br, bi):
     return mm(ar, br) - mm(ai, bi), mm(ar, bi) + mm(ai, br)
+
+
+def rounded(pair):
+    return pair[0].astype(BF16), pair[1].astype(BF16)
 
 
 def slot_of(parent, x, p, c):
@@ -174,10 +178,10 @@
         window(x_ref, out_ref, slot, which, table_ref[row, k])
 
 
-def rows_kernel(*refs):
-    table_ref, x1_ref, to2_ref, back_ref, m_ref = refs[:5]
-    slots = refs[5 : 5 + NODES]
-    out_ref, first, x2, second = refs[5 + NODES :]
+def nodes_kernel(*refs):
+    table_ref, x1_ref, to2_ref = refs[:3]
+    slots = refs[3 : 3 + NODES]
+    second, first, x2 = refs[3 + NODES :]
     level(x1_ref, first, table_ref, 0, slots, 0)
     x2[:, pl.ds(SORTED, ROOM - SORTED), :] = jnp.zeros((2, ROOM - SORTED, BOND), BF16)
     step = 256
@@ -186,6 +190,12 @@
         for part in range(2):
             x2[part, spot, :] = mm(to2_ref[spot, :], first[part, pl.ds(0, SORTED), :]).astype(BF16)
     level(x2, second, table_ref, 2, slots, 1)
+
+
+def stem_kernel(second, back_ref, ends_ref, far_ref, out_ref):
+    left = rounded(complex_mm(ends_ref[0, 0], ends_ref[0, 1], far_ref[0], far_ref[1]))
+    loop_re, loop_im = rounded(complex_mm(*left, ends_ref[1, 0], ends_ref[1, 1]))
+    step = 256
     spread = iota((2 * step, 2 * step), 0)
     interleave = (iota((2 * step, 2 * step), 1) == spread // 2 + step * (spread % 2)).astype(BF16)
     for block in range(ROWS // step):
@@ -193,7 +203,7 @@
         pair = jnp.concatenate(
             [mm(back_ref[spot, :], second[part, pl.ds(0, SORTED), :]).astype(BF16) for part in range(2)], axis=0
         )
-        by_re, by_im = mm(pair, m_ref[0]), mm(pair, m_ref[1])
+        by_re, by_im = mm(pair, loop_re), mm(pair, loop_im)
         pair = jnp.concatenate([by_re[:step] - by_im[step:], by_im[:step] + by_re[step:]], axis=0)
         out_ref[spot] = mm(interleave, pair.astype(BF16)).astype(BF16).reshape(step, 2, BOND)
 
@@ -216,33 +226,27 @@
         held[spot] = ref[...]
 
 
-def half_of(core):
-    return pl.ds(pl.multiple_of(core * (BOND // 2), BOND // 2), BOND // 2)
-
-
 def ring_kernel(where_ref, a_ref, b_ref, c_ref, d_ref, t_ref, held):
     gather_ring(where_ref, (a_ref, b_ref, c_ref, d_ref), held)
-    rows = half_of(where_ref[1])
-    re, im = held[0, 0, rows, :], held[0, 1, rows, :]
+    re, im = held[0, 0], held[0, 1]
     for spot in (1, 2, 3):
-        re, im = complex_mm(re, im, held[spot, 0], held[spot, 1])
-        re, im = re.astype(BF16), im.astype(BF16)
+        re, im = rounded(complex_mm(re, im, held[spot, 0], held[spot, 1]))
     t_ref[0] = re
     t_ref[1] = im
 
 
-def loop_kernel(where_ref, a_ref, b_ref, c_ref, d_ref, far_ref, far_other_ref, m_ref, held):
+def ends_kernel(where_ref, a_ref, b_ref, c_ref, d_ref, ends_ref, held):
     gather_ring(where_ref, (a_ref, b_ref, c_ref, d_ref), held)
-    z, core = where_ref[0], where_ref[1]
-    for part in range(2):
-        held[4, part, half_of(core), :] = far_ref[part]
-        held[4, part, half_of(1 - core), :] = far_other_ref[part]
-    re, im = held[z, 0], held[z, 1]
-    for i in range(1, 5):
-        re, im = complex_mm(re, im, held[(z + i) % 5, 0], held[(z + i) % 5, 1])
-        re, im = re.astype(BF16), im.astype(BF16)
-    m_ref[0] = re
-    m_ref[1] = im
+    z = where_ref[0]
+    ends_ref[0] = held[z]
+    ends_ref[1, 0] = (iota((BOND, BOND), 0) == iota((BOND, BOND), 1)).astype(BF16)
+    ends_ref[1, 1] = jnp.zeros((BOND, BOND), BF16)
+    for i in range(1, 4):
+        end = jnp.where(z + i < 4, 0, 1)
+        spot = (z + i) % 4
+        re, im = rounded(complex_mm(ends_ref[end, 0], ends_ref[end, 1], held[spot, 0], held[spot, 1]))
+        ends_ref[end, 0] = re
+        ends_ref[end, 1] = im
 
 
 def vmem():
@@ -260,9 +264,14 @@
         in_specs=ins,
         out_specs=jax.tree.map(lambda _: vmem(), out),
         scratch_shapes=scratch,
-        cost_estimate=pl.CostEstimate(flops=flops, bytes_accessed=moved, transcendentals=0),
+        cost_estimate=pl.CostEstimate(flops=1024, bytes_accessed=1024, transcendentals=0),
         compiler_params=pltpu.CompilerParams(vmem_limit_bytes=room * 2**20),
     )
+
+
+def shared(value):
+    with jax.named_scope("shared"):
+        return swap(value)
 
 
 def after(value, *others):
@@ -273,47 +282,43 @@
     stem, leaf, core = (lax.axis_index(name) for name in AXES)
     where = jnp.stack([stem % 4, core, leaf // 2, leaf % 2]).astype(jnp.int32)
     matrix = jax.ShapeDtypeStruct((2, BOND, BOND), BF16)
-    half = jax.ShapeDtypeStruct((2, BOND // 2, BOND), BF16)
 
     own = lax.optimization_barrier(jnp.concatenate([node_first, node_second], axis=0))
+    with jax.named_scope("side"):
+        side = along_x(own)
     with jax.named_scope("sibling"):
         sibling = swap(own)
-    with jax.named_scope("side"):
-        side = along_x(own)
     stem_own = stem_tensors[0]
     with jax.named_scope("stem_other"):
         stem_other = swap(stem_own)
-    own_later, sibling = lax.optimization_barrier((own, sibling))
+    own_later, sibling_later = lax.optimization_barrier((own, sibling))[:2]
     with jax.named_scope("side_far"):
-        side_far = along_x(sibling)
+        side_far = along_x(sibling_later)
     with jax.named_scope("turned"):
         turned = along_y(own_later)
-
     product = call(pair_kernel, matrix, [smem(), vmem(), vmem()],
                    [pltpu.VMEM((2, 2, BOND, BOND), BF16)], 2**28, 2**20)(after(where, sibling), stem_own, stem_other)
+    with jax.named_scope("side_turned"):
+        side_turned = along_y(after(side, product, turned))
+    with jax.named_scope("across"):
+        across = along_x(after(side, product, turned))
     with jax.named_scope("near"):
         near = along_z(product)
     with jax.named_scope("opposite"):
         opposite = across_z(product)
-
-    hbm = pl.BlockSpec(memory_space=pltpu.HBM)
-    parents = jnp.concatenate([first_parent.reshape(1, ROWS), second_parent.reshape(1, ROWS)], axis=0)
-    side_later = after(side, product, turned)
-    with jax.named_scope("side_turned"):
-        side_turned = along_y(side_later)
-    with jax.named_scope("across"):
-        across = along_x(side_later)
     with jax.named_scope("near_other"):
         near_other = swap(near)
     with jax.named_scope("side_far_turned"):
         side_far_turned = along_y(after(side_far, product))
+    with jax.named_scope("across_turned"):
+        across_turned = along_x(side_turned)
     ring = (product, near, near_other, opposite)
-    total = call(ring_kernel, half, [smem()] + [vmem()] * 4,
+    total = call(ring_kernel, matrix, [smem()] + [vmem()] * 4,
                  [pltpu.VMEM((4, 2, BOND, BOND), BF16)], 2**29, 2**20)(where, *ring)
     with jax.named_scope("far"):
         far = across_y(total)
-    with jax.named_scope("across_turned"):
-        across_turned = along_y(after(across, total))
+    hbm = pl.BlockSpec(memory_space=pltpu.HBM)
+    parents = jnp.concatenate([first_parent.reshape(1, ROWS), second_parent.reshape(1, ROWS)], axis=0)
     x1, goes, place, table = call(
         prepare_kernel,
         (
@@ -329,29 +334,39 @@
             pltpu.SemaphoreType.DMA,
         ],
         2**31, 2**22,
-    )(after(where, across, total), parents, branch_rows)
+    )(after(where, total, across), parents, branch_rows)
     to2, back = call(
         select_kernel,
         (jax.ShapeDtypeStruct((SORTED, SORTED), BF16), jax.ShapeDtypeStruct((ROWS, SORTED), BF16)),
         [vmem(), vmem()], [], 2**30, 2**22,
     )(after(goes, side_turned), place)
-    with jax.named_scope("far_other"):
-        far_other = swap(far)
-    loop = call(loop_kernel, matrix, [smem()] + [vmem()] * 6,
-                [pltpu.VMEM((5, 2, BOND, BOND), BF16)], 2**29, 2**20)(where, *ring, far, far_other)
-
-    slots = [own, sibling]
-    for value in (side, turned, side_far, side_turned, across, side_far_turned, across_turned):
-        with jax.named_scope("shared"):
-            slots += [value, swap(after(value, to2))]
-
+    ends = call(ends_kernel, jax.ShapeDtypeStruct((2, 2, BOND, BOND), BF16), [smem()] + [vmem()] * 4,
+                [pltpu.VMEM((4, 2, BOND, BOND), BF16)], 2**29, 2**20)(after(where, table), *ring)
+
+    side_shared = shared(after(side, table))
+    turned_shared = shared(after(turned, table))
+    side_far_shared = shared(after(side_far, table))
+    side_turned_shared = shared(after(side_turned, table))
+    across_shared = shared(after(across, table))
+    side_far_turned_shared = shared(after(side_far_turned, table))
+    across_turned_shared = shared(after(across_turned, to2, ends))
+    pairs = (
+        (own, sibling), (side, side_shared), (turned, turned_shared), (side_far, side_far_shared),
+        (side_turned, side_turned_shared), (across, across_shared),
+        (side_far_turned, side_far_turned_shared), (across_turned, across_turned_shared),
+    )
+    slots = [value for pair in pairs for value in pair]
+
+    second = call(
+        nodes_kernel,
+        jax.ShapeDtypeStruct((2, ROOM, BOND), BF16),
+        [smem()] + [vmem()] * (2 + NODES),
+        [pltpu.VMEM((2, ROOM, BOND), BF16)] * 2,
+        2**33, 2**24,
+    )(table, x1, to2, *slots)
     return call(
-        rows_kernel,
-        jax.ShapeDtypeStruct((ROWS, 2, BOND), BF16),
-        [smem()] + [vmem()] * (4 + NODES),
-        [pltpu.VMEM((2, ROOM, BOND), BF16)] * 3,
-        2**33, 2**24,
-    )(table, x1, to2, back, loop, *slots)
+        stem_kernel, jax.ShapeDtypeStruct((ROWS, 2, BOND), BF16), [vmem()] * 4, [], 2**32, 2**23
+    )(second, back, ends, after(far, second))
 
 
 def solution(mesh):

time: 60 us -> 54.1 us (0.902)
  waiting for transfers between devices: 9.14 us -> 3.78 us
  starting transfers between devices: 26.9 us -> 26 us
    ppermute x21 -> x20, waiting for transfers between devices: 9.14 us -> 3.78 us  [routed(): return lax.ppermute(value, AXES, pairs)]
    ppermute x21 -> x20, starting transfers between devices: 26.9 us -> 26 us  [routed(): return lax.ppermute(value, AXES, pairs)]
    pallas_call x3 -> x4, Pallas kernels: 14 us -> 14.6 us  [the longest x1 6.3 us: body(): call(nodes_kernel, jax.ShapeDtypeStruct((2, ROOM, BOND), BF16), [smem()]...]
  transfers between devices with their start and end apart: 21 -> 20, of which waited for: 6 -> 4; matrix products, arithmetic and copies ran while one was open for 1% -> 1% of each run, Pallas kernels for 15% -> 29%
where the time goes in v3:
time: 54.1 us; the launch traced here: 53.7 us
  starting transfers between devices  26 us (48%)
  Pallas kernels  20.9 us (39%)
  waiting for transfers between devices  3.78 us (7%)
  other arithmetic  1.96 us (4%)
  local copies, waits for them, and re-layouts  0.95 us (2%)
    ppermute x20, starting transfers between devices, routed(): return lax.ppermute(value, AXES, pairs)  26 us
    pallas_call x1, Pallas kernels, body(): call(nodes_kernel, jax.ShapeDtypeStruct((2, ROOM, BOND), BF16), [smem()]...  6.3 us
    pallas_call x1, Pallas kernels, body(): call(stem_kernel, jax.ShapeDtypeStruct((ROWS, 2, BOND), BF16), [vmem()] *...  5.54 us
    ppermute x20, waiting for transfers between devices, routed(): return lax.ppermute(value, AXES, pairs)  3.78 us
    pallas_call x1, Pallas kernels, body(): call(prepare_kernel, (jax.ShapeDtypeStruct((2, ROOM, BOND), BF16), jax.Sh...  3.77 us
    pallas_call x1, Pallas kernels, body(): call(select_kernel, (jax.ShapeDtypeStruct((SORTED, SORTED), BF16), jax.Sh...  1.65 us
    pallas_call x1, Pallas kernels, body(): call(ends_kernel, jax.ShapeDtypeStruct((2, 2, BOND, BOND), BF16), [smem()...  1.43 us
    pallas_call x1, Pallas kernels, body(): call(ring_kernel, matrix, [smem()] + [vmem()] * 4, [pltpu.VMEM((4, 2, BON...  1.35 us
  transfers between devices with their start and end apart: 20, of which 4 were waited for; matrix products, arithmetic and copies ran while one was open for 1% of the time, Pallas kernels for 29%

profile of v3, /device:TPU:1, one launch (start us, length us, event | category | flops | bytes accessed | tf_op | source)
XLA Modules:
  0.0 53.7 jit_solution(16386739121535500904)
XLA Ops:
  0.0 1.2 %pad_maximum_fusion.refs_3_ = bf16[2,2,256,256]{3,2,1,0:T(8,128)(2,1)S(1)} fusion(bf16[1,2,256,256]{3,2,1,0:T(8,128)(2,1)} %param.10, bf16[1,2,256,256]{3,2,1,0:T(8,128)(2,1)} %param.9), kind=kLoop, calls=%fused_computation | loop fusion | flops 262144 | bytes 1048576 | tf_op jit(solution)/shard_map/concatenate | solution.py:286
  1.2 1.5 %collective-permute-start = (bf16[2,2,256,256]{3,2,1,0:T(8,128)(2,1)S(1)}, bf16[2,2,256,256]{3,2,1,0:T(8,128)(2,1)S(1)}, u32[]{:S(2)}, u32[]{:S(2)}) collective-permute-start(bf16[2,2,256,256]{3,2,1,0:T(8,128)(2,1)S(1)} %pad_maximum_fusion.refs_3_), channel_id=1, source_target_pairs={{0,1},{1,0},{16,17},{17,16},{32,33},{33,32},{48,49},{49,48},{2,3},... | collective-permute-start | bytes 1572872 | tf_op jit(solution)/shard_map/sibling/ppermute | solution.py:33
  2.7 2.6 %collective-permute-start.5 = (bf16[2,2,256,256]{3,2,1,0:T(8,128)(2,1)S(1)}, bf16[2,2,256,256]{3,2,1,0:T(8,128)(2,1)S(1)}, u32[]{:S(2)}, u32[]{:S(2)}) collective-permute-start(bf16[2,2,256,256]{3,2,1,0:T(8,128)(2,1)S(1)} %pad_maximum_fusion.refs_3_), channel_id=1, source_target_pairs={{0,4},{1,13},{16,20},{17,29},{32,36},{33,45},{48,52},{49,61},{2,6}... | collective-permute-start | bytes 1572872 | tf_op jit(solution)/shard_map/side/ppermute | solution.py:33
  5.2 2.7 %collective-permute-start.6 = (bf16[2,2,256,256]{3,2,1,0:T(8,128)(2,1)S(1)}, bf16[2,2,256,256]{3,2,1,0:T(8,128)(2,1)S(1)}, u32[]{:S(2)}, u32[]{:S(2)}) collective-permute-start(bf16[2,2,256,256]{3,2,1,0:T(8,128)(2,1)S(1)} %pad_maximum_fusion.refs_3_), channel_id=1, source_target_pairs={{0,2},{1,67},{16,18},{17,83},{32,34},{33,99},{48,50},{49,115},{2,6... | collective-permute-start | bytes 1572872 | tf_op jit(solution)/shard_map/turned/ppermute | solution.py:33
  8.0 1.5 %collective-permute-start.11 = (bf16[2,2,256,256]{3,2,1,0:T(8,128)(2,1)S(1)}, bf16[2,2,256,256]{3,2,1,0:T(8,128)(2,1)S(1)}, u32[]{:S(2)}, u32[]{:S(2)}) collective-permute-start(bf16[2,2,256,256]{3,2,1,0:T(8,128)(2,1)S(1)} %collective-permute-done.refs_4_), channel_id=1, source_target_pairs={{0,4},{1,13},{16,20},{17,29},{32,36},{33,45},{48,52},{49,61},{2,6}... | collective-permute-start | bytes 1572872 | tf_op jit(solution)/shard_map/side_far/ppermute | solution.py:33
  9.7 0.9 %copy-done.1 = bf16[1,2,2,128,256]{4,3,2,1,0:T(8,128)(2,1)S(1)} copy-done((bf16[1,2,2,128,256]{4,3,2,1,0:T(8,128)(2,1)S(1)}, bf16[1,2,2,128,256]{4,3,2,1,0:T(8,128)(2,1)}, u32[]{:S(2)}) %copy-start.1) | copy-done | bytes 262168
  10.7 0.9 %shard_map.64.a_ref = bf16[2,256,256]{2,1,0:T(8,128)(2,1)S(1)} custom-call(s32[4]{0:T(128)S(1)} %pad_add_fusion.1.where_ref, bf16[2,2,128,256]{3,2,1,0:T(8,128)(2,1)S(1)} %bitcast.8, bf16[2,2,128,256]{3,2,1,0:T(8,128)(2,1)S(1)} %collective-permute-done.1.other_ref), custom_call_target="tpu_custom_call" | custom-call | flops 1024 | bytes 1024 | tf_op jit(solution)/shard_map/pallas_call | solution.py:299
  11.6 3.8 %collective-permute-start.2 = (bf16[2,256,256]{2,1,0:T(8,128)(2,1)S(1)}, bf16[2,256,256]{2,1,0:T(8,128)(2,1)S(1)}, u32[]{:S(2)}, u32[]{:S(2)}) collective-permute-start(bf16[2,256,256]{2,1,0:T(8,128)(2,1)S(1)} %shard_map.64.a_ref), channel_id=1, source_target_pairs={{0,16},{1,49},{16,32},{17,1},{32,48},{33,17},{48,0},{49,33},{2,18}... | collective-permute-start | bytes 786440 | tf_op jit(solution)/shard_map/near/ppermute | solution.py:33
  15.4 1.5 %collective-permute-start.7 = (bf16[2,2,256,256]{3,2,1,0:T(8,128)(2,1)S(1)}, bf16[2,2,256,256]{3,2,1,0:T(8,128)(2,1)S(1)}, u32[]{:S(2)}, u32[]{:S(2)}) collective-permute-start(bf16[2,2,256,256]{3,2,1,0:T(8,128)(2,1)S(1)} %collective-permute-done.5.refs_5_), channel_id=1, source_target_pairs={{0,4},{1,13},{16,20},{17,29},{32,36},{33,45},{48,52},{49,61},{2,6}... | collective-permute-start | bytes 1572872 | tf_op jit(solution)/shard_map/across/ppermute | solution.py:33
  16.9 1.8 %collective-permute-start.8 = (bf16[2,2,256,256]{3,2,1,0:T(8,128)(2,1)S(1)}, bf16[2,2,256,256]{3,2,1,0:T(8,128)(2,1)S(1)}, u32[]{:S(2)}, u32[]{:S(2)}) collective-permute-start(bf16[2,2,256,256]{3,2,1,0:T(8,128)(2,1)S(1)} %collective-permute-done.5.refs_5_), channel_id=1, source_target_pairs={{0,2},{1,67},{16,18},{17,83},{32,34},{33,99},{48,50},{49,115},{2,6... | collective-permute-start | bytes 1572872 | tf_op jit(solution)/shard_map/side_turned/ppermute | solution.py:33
  18.8 3.6 %collective-permute-start.4 = (bf16[2,256,256]{2,1,0:T(8,128)(2,1)S(1)}, bf16[2,256,256]{2,1,0:T(8,128)(2,1)S(1)}, u32[]{:S(2)}, u32[]{:S(2)}) collective-permute-start(bf16[2,256,256]{2,1,0:T(8,128)(2,1)S(1)} %shard_map.64.a_ref), channel_id=1, source_target_pairs={{0,32},{1,33},{16,48},{17,49},{32,0},{33,1},{48,16},{49,17},{2,34}... | collective-permute-start | bytes 786440 | tf_op jit(solution)/shard_map/opposite/ppermute | solution.py:33
  22.4 1.0 %collective-permute-start.15 = (bf16[2,2,256,256]{3,2,1,0:T(8,128)(2,1)S(1)}, bf16[2,2,256,256]{3,2,1,0:T(8,128)(2,1)S(1)}, u32[]{:S(2)}, u32[]{:S(2)}) collective-permute-start(bf16[2,2,256,256]{3,2,1,0:T(8,128)(2,1)S(1)} %collective-permute-done.11.refs_9_), channel_id=1, source_target_pairs={{0,2},{1,67},{16,18},{17,83},{32,34},{33,99},{48,50},{49,115},{2,6... | collective-permute-start | bytes 1572872 | tf_op jit(solution)/shard_map/side_far_turned/ppermute | solution.py:33
  23.4 0.7 %pad_add_fusion.parents_ref = s32[2,1024]{1,0:T(2,128)S(1)} fusion(s32[1,1024]{1,0:T(1,128)} %bitcast.9, s32[1,1024]{1,0:T(1,128)} %bitcast.10), kind=kLoop, calls=%fused_computation.1 | loop fusion | flops 2048 | bytes 16384 | tf_op jit(solution)/shard_map/concatenate | solution.py:321
  24.1 3.2 %collective-permute-done.4.d_ref = bf16[2,256,256]{2,1,0:T(8,128)(2,1)S(1)} collective-permute-done((bf16[2,256,256]{2,1,0:T(8,128)(2,1)S(1)}, bf16[2,256,256]{2,1,0:T(8,128)(2,1)S(1)}, u32[]{:S(2)}, u32[]{:S(2)}) %collective-permute-start.4) | collective-permute-done | bytes 262176 | tf_op jit(solution)/shard_map/opposite/ppermute | solution.py:33
  27.3 1.4 %shard_map.65 = bf16[2,256,256]{2,1,0:T(8,128)(2,1)S(1)} custom-call(s32[4]{0:T(128)S(1)} %pad_add_fusion.1.where_ref, bf16[2,256,256]{2,1,0:T(8,128)(2,1)S(1)} %shard_map.64.a_ref, bf16[2,256,256]{2,1,0:T(8,128)(2,1)S(1)} %collective-permute-done.2.b_ref, bf16[2,256,256]{2,1,0:T(8,128)(2,1)S(1)} %collective-permute-done.3.c_ref, ...), custom_call_target="tpu_custom_call" | custom-call | flops 1024 | bytes 1024 | tf_op jit(solution)/shard_map/pallas_call | solution.py:316
  28.6 1.5 %collective-permute-start.17 = (bf16[2,2,256,256]{3,2,1,0:T(8,128)(2,1)S(1)}, bf16[2,2,256,256]{3,2,1,0:T(8,128)(2,1)S(1)}, u32[]{:S(2)}, u32[]{:S(2)}) collective-permute-start(bf16[2,2,256,256]{3,2,1,0:T(8,128)(2,1)S(1)} %collective-permute-done.8.refs_11_), channel_id=1, source_target_pairs={{0,4},{1,13},{16,20},{17,29},{32,36},{33,45},{48,52},{49,61},{2,6}... | collective-permute-start | bytes 1572872 | tf_op jit(solution)/shard_map/across_turned/ppermute | solution.py:33
  30.2 3.8 %shard_map.66 = (bf16[2,1440,256]{2,1,0:T(8,128)(2,1)S(1)}, s32[8,1280]{1,0:T(8,128)S(1)}, f32[8,1024]{1,0:T(8,128)S(1)}, s32[8,16]{1,0:T(8,128)S(1)}) custom-call(s32[4]{0:T(128)S(1)} %pad_add_fusion.1.where_ref, s32[2,1024]{1,0:T(2,128)S(1)} %pad_add_fusion.parents_ref, bf16[1024,2,256]{2,1,0:T(2,128)(2,1)S(1)} %copy-done), custom_call_target="tpu_custom_call" | custom-call | flops 1024 | bytes 1024 | tf_op jit(solution)/shard_map/pallas_call | solution.py:322
  34.7 0.4 collective-permute-start.13
  35.1 1.7 %shard_map.67 = (bf16[1280,1280]{1,0:T(8,128)(2,1)S(1)}, bf16[1024,1280]{1,0:T(8,128)(2,1)S(1)}) custom-call(s32[8,1280]{1,0:T(8,128)S(1)} %get-tuple-element.34.goes_ref, f32[8,1024]{1,0:T(8,128)S(1)} %get-tuple-element.35.place_ref), custom_call_target="tpu_custom_call" | custom-call | flops 1024 | bytes 1024 | tf_op jit(solution)/shard_map/pallas_call | solution.py:338
  36.7 1.4 %shard_map.68.ends_ref = bf16[2,2,256,256]{3,2,1,0:T(8,128)(2,1)S(1)} custom-call(s32[4]{0:T(128)S(1)} %pad_add_fusion.1.where_ref, bf16[2,256,256]{2,1,0:T(8,128)(2,1)S(1)} %shard_map.64.a_ref, bf16[2,256,256]{2,1,0:T(8,128)(2,1)S(1)} %collective-permute-done.2.b_ref, bf16[2,256,256]{2,1,0:T(8,128)(2,1)S(1)} %collective-permute-done.3.c_ref, ...), custom_call_target="tpu_custom_call" | custom-call | flops 1024 | bytes 1024 | tf_op jit(solution)/shard_map/pallas_call | solution.py:343
  38.4 0.4 collective-permute-start.16
  38.9 2.6 %collective-permute-start.19 = (bf16[2,256,256]{2,1,0:T(8,128)(2,1)S(1)}, bf16[2,256,256]{2,1,0:T(8,128)(2,1)S(1)}, u32[]{:S(2)}, u32[]{:S(2)}) collective-permute-start(bf16[2,256,256]{2,1,0:T(8,128)(2,1)S(1)} %shard_map.65), channel_id=1, source_target_pairs={{0,64},{1,65},{16,80},{17,81},{32,96},{33,97},{48,112},{49,113},{2... | collective-permute-start | bytes 786440 | tf_op jit(solution)/shard_map/far/ppermute | solution.py:33
  41.7 6.3 %shard_map.69.second = bf16[2,1440,256]{2,1,0:T(8,128)(2,1)S(1)} custom-call(s32[8,16]{1,0:T(8,128)S(1)} %get-tuple-element.31.refs_0_, bf16[2,1440,256]{2,1,0:T(8,128)(2,1)S(1)} %get-tuple-element.32.refs_1_, bf16[1280,1280]{1,0:T(8,128)(2,1)S(1)} %get-tuple-element.36.refs_2_, bf16[2,2,256,256]{3,2,1,0:T(8,128)(2,1)S(1)} %pad_maximum_fusion.refs_3_, ...), custom_call_target="tpu_custom_call" | custom-call | flops 1024 | bytes 1024 | tf_op jit(solution)/shard_map/pallas_call | solution.py:360
  48.2 5.5 %shard_map.70 = bf16[1024,2,256]{2,1,0:T(2,128)(2,1)} custom-call(bf16[2,1440,256]{2,1,0:T(8,128)(2,1)S(1)} %shard_map.69.second, bf16[1024,1280]{1,0:T(8,128)(2,1)S(1)} %get-tuple-element.47.back_ref, bf16[2,2,256,256]{3,2,1,0:T(8,128)(2,1)S(1)} %shard_map.68.ends_ref, bf16[2,256,256]{2,1,0:T(8,128)(2,1)S(1)} %collective-permute-done.19.far_ref), custom_call_target="tpu_custom_call" | custom-call | flops 1024 | bytes 1024 | tf_op jit(solution)/shard_map/pallas_call | solution.py:367
  (30 shorter events, 1.7 us)
Async XLA Ops:
  0.0 30.2 %copy-start = (bf16[1024,2,256]{2,1,0:T(2,128)(2,1)S(1)}, bf16[1024,2,256]{2,1,0:T(2,128)(2,1)}, u32[]{:S(2)}) copy-start(bf16[1024,2,256]{2,1,0:T(2,128)(2,1)} %rows_hbm.1) | copy-start | bytes 3145732
  1.2 4.1 %collective-permute-start = (bf16[2,2,256,256]{3,2,1,0:T(8,128)(2,1)S(1)}, bf16[2,2,256,256]{3,2,1,0:T(8,128)(2,1)S(1)}, u32[]{:S(2)}, u32[]{:S(2)}) collective-permute-start(bf16[2,2,256,256]{3,2,1,0:T(8,128)(2,1)S(1)} %pad_maximum_fusion.refs_3_), channel_id=1, source_target_pairs={{0,1},{1,0},{16,17},{17,16},{32,33},{33,32},{48,49},{49,48},{2,3},... | collective-permute-start | bytes 1572872 | tf_op jit(solution)/shard_map/sibling/ppermute | solution.py:33
  2.7 12.7 %collective-permute-start.5 = (bf16[2,2,256,256]{3,2,1,0:T(8,128)(2,1)S(1)}, bf16[2,2,256,256]{3,2,1,0:T(8,128)(2,1)S(1)}, u32[]{:S(2)}, u32[]{:S(2)}) collective-permute-start(bf16[2,2,256,256]{3,2,1,0:T(8,128)(2,1)S(1)} %pad_maximum_fusion.refs_3_), channel_id=1, source_target_pairs={{0,4},{1,13},{16,20},{17,29},{32,36},{33,45},{48,52},{49,61},{2,6}... | collective-permute-start | bytes 1572872 | tf_op jit(solution)/shard_map/side/ppermute | solution.py:33
  5.2 10.1 %collective-permute-start.6 = (bf16[2,2,256,256]{3,2,1,0:T(8,128)(2,1)S(1)}, bf16[2,2,256,256]{3,2,1,0:T(8,128)(2,1)S(1)}, u32[]{:S(2)}, u32[]{:S(2)}) collective-permute-start(bf16[2,2,256,256]{3,2,1,0:T(8,128)(2,1)S(1)} %pad_maximum_fusion.refs_3_), channel_id=1, source_target_pairs={{0,2},{1,67},{16,18},{17,83},{32,34},{33,99},{48,50},{49,115},{2,6... | collective-permute-start | bytes 1572872 | tf_op jit(solution)/shard_map/turned/ppermute | solution.py:33
  8.0 1.7 %collective-permute-start.1 = (bf16[2,2,128,256]{3,2,1,0:T(8,128)(2,1)}, bf16[2,2,128,256]{3,2,1,0:T(8,128)(2,1)S(1)}, u32[]{:S(2)}, u32[]{:S(2)}) collective-permute-start(bf16[2,2,128,256]{3,2,1,0:T(8,128)(2,1)} %bitcast.7), channel_id=1, source_target_pairs={{0,1},{1,0},{16,17},{17,16},{32,33},{33,32},{48,49},{49,48},{2,3},... | collective-permute-start | bytes 786440 | tf_op jit(solution)/shard_map/stem_other/ppermute | solution.py:33
  8.0 14.4 %collective-permute-start.11 = (bf16[2,2,256,256]{3,2,1,0:T(8,128)(2,1)S(1)}, bf16[2,2,256,256]{3,2,1,0:T(8,128)(2,1)S(1)}, u32[]{:S(2)}, u32[]{:S(2)}) collective-permute-start(bf16[2,2,256,256]{3,2,1,0:T(8,128)(2,1)S(1)} %collective-permute-done.refs_4_), channel_id=1, source_target_pairs={{0,4},{1,13},{16,20},{17,29},{32,36},{33,45},{48,52},{49,61},{2,6}... | collective-permute-start | bytes 1572872 | tf_op jit(solution)/shard_map/side_far/ppermute | solution.py:33
  9.7 1.0 %copy-start.1 = (bf16[1,2,2,128,256]{4,3,2,1,0:T(8,128)(2,1)S(1)}, bf16[1,2,2,128,256]{4,3,2,1,0:T(8,128)(2,1)}, u32[]{:S(2)}) copy-start(bf16[1,2,2,128,256]{4,3,2,1,0:T(8,128)(2,1)} %param.11) | copy-start | bytes 786436
  11.6 10.8 %collective-permute-start.2 = (bf16[2,256,256]{2,1,0:T(8,128)(2,1)S(1)}, bf16[2,256,256]{2,1,0:T(8,128)(2,1)S(1)}, u32[]{:S(2)}, u32[]{:S(2)}) collective-permute-start(bf16[2,256,256]{2,1,0:T(8,128)(2,1)S(1)} %shard_map.64.a_ref), channel_id=1, source_target_pairs={{0,16},{1,49},{16,32},{17,1},{32,48},{33,17},{48,0},{49,33},{2,18}... | collective-permute-start | bytes 786440 | tf_op jit(solution)/shard_map/near/ppermute | solution.py:33
  15.4 13.2 %collective-permute-start.7 = (bf16[2,2,256,256]{3,2,1,0:T(8,128)(2,1)S(1)}, bf16[2,2,256,256]{3,2,1,0:T(8,128)(2,1)S(1)}, u32[]{:S(2)}, u32[]{:S(2)}) collective-permute-start(bf16[2,2,256,256]{3,2,1,0:T(8,128)(2,1)S(1)} %collective-permute-done.5.refs_5_), channel_id=1, source_target_pairs={{0,4},{1,13},{16,20},{17,29},{32,36},{33,45},{48,52},{49,61},{2,6}... | collective-permute-start | bytes 1572872 | tf_op jit(solution)/shard_map/across/ppermute | solution.py:33
  16.9 11.7 %collective-permute-start.8 = (bf16[2,2,256,256]{3,2,1,0:T(8,128)(2,1)S(1)}, bf16[2,2,256,256]{3,2,1,0:T(8,128)(2,1)S(1)}, u32[]{:S(2)}, u32[]{:S(2)}) collective-permute-start(bf16[2,2,256,256]{3,2,1,0:T(8,128)(2,1)S(1)} %collective-permute-done.5.refs_5_), channel_id=1, source_target_pairs={{0,2},{1,67},{16,18},{17,83},{32,34},{33,99},{48,50},{49,115},{2,6... | collective-permute-start | bytes 1572872 | tf_op jit(solution)/shard_map/side_turned/ppermute | solution.py:33
  18.8 8.5 %collective-permute-start.4 = (bf16[2,256,256]{2,1,0:T(8,128)(2,1)S(1)}, bf16[2,256,256]{2,1,0:T(8,128)(2,1)S(1)}, u32[]{:S(2)}, u32[]{:S(2)}) collective-permute-start(bf16[2,256,256]{2,1,0:T(8,128)(2,1)S(1)} %shard_map.64.a_ref), channel_id=1, source_target_pairs={{0,32},{1,33},{16,48},{17,49},{32,0},{33,1},{48,16},{49,17},{2,34}... | collective-permute-start | bytes 786440 | tf_op jit(solution)/shard_map/opposite/ppermute | solution.py:33
  22.4 4.9 %collective-permute-start.3 = (bf16[2,256,256]{2,1,0:T(8,128)(2,1)S(1)}, bf16[2,256,256]{2,1,0:T(8,128)(2,1)S(1)}, u32[]{:S(2)}, u32[]{:S(2)}) collective-permute-start(bf16[2,256,256]{2,1,0:T(8,128)(2,1)S(1)} %collective-permute-done.2.b_ref), channel_id=1, source_target_pairs={{0,1},{1,0},{16,17},{17,16},{32,33},{33,32},{48,49},{49,48},{2,3},... | collective-permute-start | bytes 786440 | tf_op jit(solution)/shard_map/near_other/ppermute | solution.py:33
  22.4 12.3 %collective-permute-start.15 = (bf16[2,2,256,256]{3,2,1,0:T(8,128)(2,1)S(1)}, bf16[2,2,256,256]{3,2,1,0:T(8,128)(2,1)S(1)}, u32[]{:S(2)}, u32[]{:S(2)}) collective-permute-start(bf16[2,2,256,256]{3,2,1,0:T(8,128)(2,1)S(1)} %collective-permute-done.11.refs_9_), channel_id=1, source_target_pairs={{0,2},{1,67},{16,18},{17,83},{32,34},{33,99},{48,50},{49,115},{2,6... | collective-permute-start | bytes 1572872 | tf_op jit(solution)/shard_map/side_far_turned/ppermute | solution.py:33
  28.6 9.5 %collective-permute-start.17 = (bf16[2,2,256,256]{3,2,1,0:T(8,128)(2,1)S(1)}, bf16[2,2,256,256]{3,2,1,0:T(8,128)(2,1)S(1)}, u32[]{:S(2)}, u32[]{:S(2)}) collective-permute-start(bf16[2,2,256,256]{3,2,1,0:T(8,128)(2,1)S(1)} %collective-permute-done.8.refs_11_), channel_id=1, source_target_pairs={{0,4},{1,13},{16,20},{17,29},{32,36},{33,45},{48,52},{49,61},{2,6}... | collective-permute-start | bytes 1572872 | tf_op jit(solution)/shard_map/across_turned/ppermute | solution.py:33
  34.0 4.4 %collective-permute-start.9 = (bf16[2,2,256,256]{3,2,1,0:T(8,128)(2,1)S(1)}, bf16[2,2,256,256]{3,2,1,0:T(8,128)(2,1)S(1)}, u32[]{:S(2)}, u32[]{:S(2)}) collective-permute-start(bf16[2,2,256,256]{3,2,1,0:T(8,128)(2,1)S(1)} %collective-permute-done.5.refs_5_), channel_id=1, source_target_pairs={{0,1},{1,0},{16,17},{17,16},{32,33},{33,32},{48,49},{49,48},{2,3},... | collective-permute-start | bytes 1572872 | tf_op jit(solution)/shard_map/shared/ppermute | solution.py:33
  34.1 4.6 %collective-permute-start.10 = (bf16[2,2,256,256]{3,2,1,0:T(8,128)(2,1)S(1)}, bf16[2,2,256,256]{3,2,1,0:T(8,128)(2,1)S(1)}, u32[]{:S(2)}, u32[]{:S(2)}) collective-permute-start(bf16[2,2,256,256]{3,2,1,0:T(8,128)(2,1)S(1)} %collective-permute-done.6.refs_7_), channel_id=1, source_target_pairs={{0,1},{1,0},{16,17},{17,16},{32,33},{33,32},{48,49},{49,48},{2,3},... | collective-permute-start | bytes 1572872 | tf_op jit(solution)/shard_map/shared/ppermute | solution.py:33
  34.5 4.3 %collective-permute-start.12 = (bf16[2,2,256,256]{3,2,1,0:T(8,128)(2,1)S(1)}, bf16[2,2,256,256]{3,2,1,0:T(8,128)(2,1)S(1)}, u32[]{:S(2)}, u32[]{:S(2)}) collective-permute-start(bf16[2,2,256,256]{3,2,1,0:T(8,128)(2,1)S(1)} %collective-permute-done.11.refs_9_), channel_id=1, source_target_pairs={{0,1},{1,0},{16,17},{17,16},{32,33},{33,32},{48,49},{49,48},{2,3},... | collective-permute-start | bytes 1572872 | tf_op jit(solution)/shard_map/shared/ppermute | solution.py:33
  34.7 6.8 %collective-permute-start.13 = (bf16[2,2,256,256]{3,2,1,0:T(8,128)(2,1)S(1)}, bf16[2,2,256,256]{3,2,1,0:T(8,128)(2,1)S(1)}, u32[]{:S(2)}, u32[]{:S(2)}) collective-permute-start(bf16[2,2,256,256]{3,2,1,0:T(8,128)(2,1)S(1)} %collective-permute-done.8.refs_11_), channel_id=1, source_target_pairs={{0,1},{1,0},{16,17},{17,16},{32,33},{33,32},{48,49},{49,48},{2,3},... | collective-permute-start | bytes 1572872 | tf_op jit(solution)/shard_map/shared/ppermute | solution.py:33
  38.2 3.3 %collective-permute-start.14 = (bf16[2,2,256,256]{3,2,1,0:T(8,128)(2,1)S(1)}, bf16[2,2,256,256]{3,2,1,0:T(8,128)(2,1)S(1)}, u32[]{:S(2)}, u32[]{:S(2)}) collective-permute-start(bf16[2,2,256,256]{3,2,1,0:T(8,128)(2,1)S(1)} %collective-permute-done.7.refs_13_), channel_id=1, source_target_pairs={{0,1},{1,0},{16,17},{17,16},{32,33},{33,32},{48,49},{49,48},{2,3},... | collective-permute-start | bytes 1572872 | tf_op jit(solution)/shard_map/shared/ppermute | solution.py:33
  38.4 3.1 %collective-permute-start.16 = (bf16[2,2,256,256]{3,2,1,0:T(8,128)(2,1)S(1)}, bf16[2,2,256,256]{3,2,1,0:T(8,128)(2,1)S(1)}, u32[]{:S(2)}, u32[]{:S(2)}) collective-permute-start(bf16[2,2,256,256]{3,2,1,0:T(8,128)(2,1)S(1)} %collective-permute-done.15.refs_15_), channel_id=1, source_target_pairs={{0,1},{1,0},{16,17},{17,16},{32,33},{33,32},{48,49},{49,48},{2,3},... | collective-permute-start | bytes 1572872 | tf_op jit(solution)/shard_map/shared/ppermute | solution.py:33
  38.8 2.9 %collective-permute-start.18 = (bf16[2,2,256,256]{3,2,1,0:T(8,128)(2,1)S(1)}, bf16[2,2,256,256]{3,2,1,0:T(8,128)(2,1)S(1)}, u32[]{:S(2)}, u32[]{:S(2)}) collective-permute-start(bf16[2,2,256,256]{3,2,1,0:T(8,128)(2,1)S(1)} %collective-permute-done.17.refs_17_), channel_id=1, source_target_pairs={{0,1},{1,0},{16,17},{17,16},{32,33},{33,32},{48,49},{49,48},{2,3},... | collective-permute-start | bytes 1572872 | tf_op jit(solution)/shard_map/shared/ppermute | solution.py:33
  38.9 9.3 %collective-permute-start.19 = (bf16[2,256,256]{2,1,0:T(8,128)(2,1)S(1)}, bf16[2,256,256]{2,1,0:T(8,128)(2,1)S(1)}, u32[]{:S(2)}, u32[]{:S(2)}) collective-permute-start(bf16[2,256,256]{2,1,0:T(8,128)(2,1)S(1)} %shard_map.65), channel_id=1, source_target_pairs={{0,64},{1,65},{16,80},{17,81},{32,96},{33,97},{48,112},{49,113},{2... | collective-permute-start | bytes 786440 | tf_op jit(solution)/shard_map/far/ppermute | solution.py:33

commit v4 on v3

--- a/solution.py
+++ b/solution.py
@@ -11,8 +11,8 @@
 NODES = 16
 PAD = 16
 SORTED = 1280
-WINDOW = 80
-ROOM = SORTED + 2 * WINDOW
+CAP = 160
+ROOM = SORTED + CAP
 TAIL = ROOM - 928
 F32 = jnp.float32
 BF16 = jnp.bfloat16
@@ -161,19 +161,15 @@
 
 
 def window(x_ref, out_ref, slot, which, begin):
-    spot = pl.ds(pl.multiple_of(begin, PAD), WINDOW)
-    pair = x_ref[:, spot, :].reshape(2 * WINDOW, BOND)
+    spot = pl.ds(pl.multiple_of(begin, PAD), CAP)
+    pair = x_ref[:, spot, :].reshape(2 * CAP, BOND)
     by_re, by_im = mm(pair, slot[which, 0]), mm(pair, slot[which, 1])
-    out_ref[0, spot, :] = (by_re[:WINDOW] - by_im[WINDOW:]).astype(BF16)
-    out_ref[1, spot, :] = (by_im[:WINDOW] + by_re[WINDOW:]).astype(BF16)
+    out_ref[0, spot, :] = (by_re[:CAP] - by_im[CAP:]).astype(BF16)
+    out_ref[1, spot, :] = (by_im[:CAP] + by_re[CAP:]).astype(BF16)
 
 
 def level(x_ref, out_ref, table_ref, row, slots, which):
     out_ref[:, pl.ds(ROOM - TAIL, TAIL), :] = jnp.zeros((2, TAIL, BOND), BF16)
-    for k, slot in enumerate(slots):
-        @pl.when(table_ref[row + 1, k] > WINDOW)
-        def _(k=k, slot=slot):
-            window(x_ref, out_ref, slot, which, table_ref[row, k] + WINDOW)
     for k, slot in enumerate(slots):
         window(x_ref, out_ref, slot, which, table_ref[row, k])
 

time: 54.1 us -> 54.1 us (level)
  transfers between devices with their start and end apart: 20 -> 20, of which waited for: 4 -> 4; matrix products, arithmetic and copies ran while one was open for 1% -> 1% of each run, Pallas kernels for 29% -> 28%
where the time goes in v4:
time: 54.1 us; the launch traced here: 53.7 us
  starting transfers between devices  26 us (48%)
  Pallas kernels  20.5 us (38%)
  waiting for transfers between devices  4.24 us (8%)
  other arithmetic  1.96 us (4%)
  local copies, waits for them, and re-layouts  0.95 us (2%)
    ppermute x20, starting transfers between devices, routed(): return lax.ppermute(value, AXES, pairs)  26 us
    pallas_call x1, Pallas kernels, body(): call(nodes_kernel, jax.ShapeDtypeStruct((2, ROOM, BOND), BF16), [smem()]...  5.84 us
    pallas_call x1, Pallas kernels, body(): call(stem_kernel, jax.ShapeDtypeStruct((ROWS, 2, BOND), BF16), [vmem()] *...  5.54 us
    ppermute x20, waiting for transfers between devices, routed(): return lax.ppermute(value, AXES, pairs)  4.24 us
    pallas_call x1, Pallas kernels, body(): call(prepare_kernel, (jax.ShapeDtypeStruct((2, ROOM, BOND), BF16), jax.Sh...  3.77 us
    pallas_call x1, Pallas kernels, body(): call(select_kernel, (jax.ShapeDtypeStruct((SORTED, SORTED), BF16), jax.Sh...  1.65 us
    pallas_call x1, Pallas kernels, body(): call(ends_kernel, jax.ShapeDtypeStruct((2, 2, BOND, BOND), BF16), [smem()...  1.43 us
    pallas_call x1, Pallas kernels, body(): call(ring_kernel, matrix, [smem()] + [vmem()] * 4, [pltpu.VMEM((4, 2, BON...  1.35 us
  transfers between devices with their start and end apart: 20, of which 4 were waited for; matrix products, arithmetic and copies ran while one was open for 1% of the time, Pallas kernels for 28%

profile of v4, /device:TPU:1, one launch (start us, length us, event | category | flops | bytes accessed | tf_op | source)
XLA Modules:
  0.0 53.7 jit_solution(5705370825950088093)
XLA Ops:
  0.0 1.2 %pad_maximum_fusion.refs_3_ = bf16[2,2,256,256]{3,2,1,0:T(8,128)(2,1)S(1)} fusion(bf16[1,2,256,256]{3,2,1,0:T(8,128)(2,1)} %param.10, bf16[1,2,256,256]{3,2,1,0:T(8,128)(2,1)} %param.9), kind=kLoop, calls=%fused_computation | loop fusion | flops 262144 | bytes 1048576 | tf_op jit(solution)/shard_map/concatenate | solution.py:282
  1.2 1.5 %collective-permute-start = (bf16[2,2,256,256]{3,2,1,0:T(8,128)(2,1)S(1)}, bf16[2,2,256,256]{3,2,1,0:T(8,128)(2,1)S(1)}, u32[]{:S(2)}, u32[]{:S(2)}) collective-permute-start(bf16[2,2,256,256]{3,2,1,0:T(8,128)(2,1)S(1)} %pad_maximum_fusion.refs_3_), channel_id=1, source_target_pairs={{0,1},{1,0},{16,17},{17,16},{32,33},{33,32},{48,49},{49,48},{2,3},... | collective-permute-start | bytes 1572872 | tf_op jit(solution)/shard_map/sibling/ppermute | solution.py:33
  2.7 2.6 %collective-permute-start.5 = (bf16[2,2,256,256]{3,2,1,0:T(8,128)(2,1)S(1)}, bf16[2,2,256,256]{3,2,1,0:T(8,128)(2,1)S(1)}, u32[]{:S(2)}, u32[]{:S(2)}) collective-permute-start(bf16[2,2,256,256]{3,2,1,0:T(8,128)(2,1)S(1)} %pad_maximum_fusion.refs_3_), channel_id=1, source_target_pairs={{0,4},{1,13},{16,20},{17,29},{32,36},{33,45},{48,52},{49,61},{2,6}... | collective-permute-start | bytes 1572872 | tf_op jit(solution)/shard_map/side/ppermute | solution.py:33
  5.2 2.7 %collective-permute-start.6 = (bf16[2,2,256,256]{3,2,1,0:T(8,128)(2,1)S(1)}, bf16[2,2,256,256]{3,2,1,0:T(8,128)(2,1)S(1)}, u32[]{:S(2)}, u32[]{:S(2)}) collective-permute-start(bf16[2,2,256,256]{3,2,1,0:T(8,128)(2,1)S(1)} %pad_maximum_fusion.refs_3_), channel_id=1, source_target_pairs={{0,2},{1,67},{16,18},{17,83},{32,34},{33,99},{48,50},{49,115},{2,6... | collective-permute-start | bytes 1572872 | tf_op jit(solution)/shard_map/turned/ppermute | solution.py:33
  8.0 1.5 %collective-permute-start.11 = (bf16[2,2,256,256]{3,2,1,0:T(8,128)(2,1)S(1)}, bf16[2,2,256,256]{3,2,1,0:T(8,128)(2,1)S(1)}, u32[]{:S(2)}, u32[]{:S(2)}) collective-permute-start(bf16[2,2,256,256]{3,2,1,0:T(8,128)(2,1)S(1)} %collective-permute-done.refs_4_), channel_id=1, source_target_pairs={{0,4},{1,13},{16,20},{17,29},{32,36},{33,45},{48,52},{49,61},{2,6}... | collective-permute-start | bytes 1572872 | tf_op jit(solution)/shard_map/side_far/ppermute | solution.py:33
  9.7 0.9 %copy-done.1 = bf16[1,2,2,128,256]{4,3,2,1,0:T(8,128)(2,1)S(1)} copy-done((bf16[1,2,2,128,256]{4,3,2,1,0:T(8,128)(2,1)S(1)}, bf16[1,2,2,128,256]{4,3,2,1,0:T(8,128)(2,1)}, u32[]{:S(2)}) %copy-start.1) | copy-done | bytes 262168
  10.7 0.9 %shard_map.64.a_ref = bf16[2,256,256]{2,1,0:T(8,128)(2,1)S(1)} custom-call(s32[4]{0:T(128)S(1)} %pad_add_fusion.1.where_ref, bf16[2,2,128,256]{3,2,1,0:T(8,128)(2,1)S(1)} %bitcast.8, bf16[2,2,128,256]{3,2,1,0:T(8,128)(2,1)S(1)} %collective-permute-done.1.other_ref), custom_call_target="tpu_custom_call" | custom-call | flops 1024 | bytes 1024 | tf_op jit(solution)/shard_map/pallas_call | solution.py:295
  11.6 3.8 %collective-permute-start.2 = (bf16[2,256,256]{2,1,0:T(8,128)(2,1)S(1)}, bf16[2,256,256]{2,1,0:T(8,128)(2,1)S(1)}, u32[]{:S(2)}, u32[]{:S(2)}) collective-permute-start(bf16[2,256,256]{2,1,0:T(8,128)(2,1)S(1)} %shard_map.64.a_ref), channel_id=1, source_target_pairs={{0,16},{1,49},{16,32},{17,1},{32,48},{33,17},{48,0},{49,33},{2,18}... | collective-permute-start | bytes 786440 | tf_op jit(solution)/shard_map/near/ppermute | solution.py:33
  15.4 1.5 %collective-permute-start.7 = (bf16[2,2,256,256]{3,2,1,0:T(8,128)(2,1)S(1)}, bf16[2,2,256,256]{3,2,1,0:T(8,128)(2,1)S(1)}, u32[]{:S(2)}, u32[]{:S(2)}) collective-permute-start(bf16[2,2,256,256]{3,2,1,0:T(8,128)(2,1)S(1)} %collective-permute-done.5.refs_5_), channel_id=1, source_target_pairs={{0,4},{1,13},{16,20},{17,29},{32,36},{33,45},{48,52},{49,61},{2,6}... | collective-permute-start | bytes 1572872 | tf_op jit(solution)/shard_map/across/ppermute | solution.py:33
  16.9 1.8 %collective-permute-start.8 = (bf16[2,2,256,256]{3,2,1,0:T(8,128)(2,1)S(1)}, bf16[2,2,256,256]{3,2,1,0:T(8,128)(2,1)S(1)}, u32[]{:S(2)}, u32[]{:S(2)}) collective-permute-start(bf16[2,2,256,256]{3,2,1,0:T(8,128)(2,1)S(1)} %collective-permute-done.5.refs_5_), channel_id=1, source_target_pairs={{0,2},{1,67},{16,18},{17,83},{32,34},{33,99},{48,50},{49,115},{2,6... | collective-permute-start | bytes 1572872 | tf_op jit(solution)/shard_map/side_turned/ppermute | solution.py:33
  18.8 3.6 %collective-permute-start.4 = (bf16[2,256,256]{2,1,0:T(8,128)(2,1)S(1)}, bf16[2,256,256]{2,1,0:T(8,128)(2,1)S(1)}, u32[]{:S(2)}, u32[]{:S(2)}) collective-permute-start(bf16[2,256,256]{2,1,0:T(8,128)(2,1)S(1)} %shard_map.64.a_ref), channel_id=1, source_target_pairs={{0,32},{1,33},{16,48},{17,49},{32,0},{33,1},{48,16},{49,17},{2,34}... | collective-permute-start | bytes 786440 | tf_op jit(solution)/shard_map/opposite/ppermute | solution.py:33
  22.4 1.0 %collective-permute-start.15 = (bf16[2,2,256,256]{3,2,1,0:T(8,128)(2,1)S(1)}, bf16[2,2,256,256]{3,2,1,0:T(8,128)(2,1)S(1)}, u32[]{:S(2)}, u32[]{:S(2)}) collective-permute-start(bf16[2,2,256,256]{3,2,1,0:T(8,128)(2,1)S(1)} %collective-permute-done.11.refs_9_), channel_id=1, source_target_pairs={{0,2},{1,67},{16,18},{17,83},{32,34},{33,99},{48,50},{49,115},{2,6... | collective-permute-start | bytes 1572872 | tf_op jit(solution)/shard_map/side_far_turned/ppermute | solution.py:33
  23.4 0.7 %pad_add_fusion.parents_ref = s32[2,1024]{1,0:T(2,128)S(1)} fusion(s32[1,1024]{1,0:T(1,128)} %bitcast.9, s32[1,1024]{1,0:T(1,128)} %bitcast.10), kind=kLoop, calls=%fused_computation.1 | loop fusion | flops 2048 | bytes 16384 | tf_op jit(solution)/shard_map/concatenate | solution.py:317
  24.1 3.2 %collective-permute-done.4.d_ref = bf16[2,256,256]{2,1,0:T(8,128)(2,1)S(1)} collective-permute-done((bf16[2,256,256]{2,1,0:T(8,128)(2,1)S(1)}, bf16[2,256,256]{2,1,0:T(8,128)(2,1)S(1)}, u32[]{:S(2)}, u32[]{:S(2)}) %collective-permute-start.4) | collective-permute-done | bytes 262176 | tf_op jit(solution)/shard_map/opposite/ppermute | solution.py:33
  27.3 1.4 %shard_map.65 = bf16[2,256,256]{2,1,0:T(8,128)(2,1)S(1)} custom-call(s32[4]{0:T(128)S(1)} %pad_add_fusion.1.where_ref, bf16[2,256,256]{2,1,0:T(8,128)(2,1)S(1)} %shard_map.64.a_ref, bf16[2,256,256]{2,1,0:T(8,128)(2,1)S(1)} %collective-permute-done.2.b_ref, bf16[2,256,256]{2,1,0:T(8,128)(2,1)S(1)} %collective-permute-done.3.c_ref, ...), custom_call_target="tpu_custom_call" | custom-call | flops 1024 | bytes 1024 | tf_op jit(solution)/shard_map/pallas_call | solution.py:312
  28.6 1.5 %collective-permute-start.17 = (bf16[2,2,256,256]{3,2,1,0:T(8,128)(2,1)S(1)}, bf16[2,2,256,256]{3,2,1,0:T(8,128)(2,1)S(1)}, u32[]{:S(2)}, u32[]{:S(2)}) collective-permute-start(bf16[2,2,256,256]{3,2,1,0:T(8,128)(2,1)S(1)} %collective-permute-done.8.refs_11_), channel_id=1, source_target_pairs={{0,4},{1,13},{16,20},{17,29},{32,36},{33,45},{48,52},{49,61},{2,6}... | collective-permute-start | bytes 1572872 | tf_op jit(solution)/shard_map/across_turned/ppermute | solution.py:33
  30.2 3.8 %shard_map.66 = (bf16[2,1440,256]{2,1,0:T(8,128)(2,1)S(1)}, s32[8,1280]{1,0:T(8,128)S(1)}, f32[8,1024]{1,0:T(8,128)S(1)}, s32[8,16]{1,0:T(8,128)S(1)}) custom-call(s32[4]{0:T(128)S(1)} %pad_add_fusion.1.where_ref, s32[2,1024]{1,0:T(2,128)S(1)} %pad_add_fusion.parents_ref, bf16[1024,2,256]{2,1,0:T(2,128)(2,1)S(1)} %copy-done), custom_call_target="tpu_custom_call" | custom-call | flops 1024 | bytes 1024 | tf_op jit(solution)/shard_map/pallas_call | solution.py:318
  34.7 0.4 collective-permute-start.13
  35.1 1.7 %shard_map.67 = (bf16[1280,1280]{1,0:T(8,128)(2,1)S(1)}, bf16[1024,1280]{1,0:T(8,128)(2,1)S(1)}) custom-call(s32[8,1280]{1,0:T(8,128)S(1)} %get-tuple-element.34.goes_ref, f32[8,1024]{1,0:T(8,128)S(1)} %get-tuple-element.35.place_ref), custom_call_target="tpu_custom_call" | custom-call | flops 1024 | bytes 1024 | tf_op jit(solution)/shard_map/pallas_call | solution.py:334
  36.7 1.4 %shard_map.68.ends_ref = bf16[2,2,256,256]{3,2,1,0:T(8,128)(2,1)S(1)} custom-call(s32[4]{0:T(128)S(1)} %pad_add_fusion.1.where_ref, bf16[2,256,256]{2,1,0:T(8,128)(2,1)S(1)} %shard_map.64.a_ref, bf16[2,256,256]{2,1,0:T(8,128)(2,1)S(1)} %collective-permute-done.2.b_ref, bf16[2,256,256]{2,1,0:T(8,128)(2,1)S(1)} %collective-permute-done.3.c_ref, ...), custom_call_target="tpu_custom_call" | custom-call | flops 1024 | bytes 1024 | tf_op jit(solution)/shard_map/pallas_call | solution.py:339
  38.9 2.6 %collective-permute-start.19 = (bf16[2,256,256]{2,1,0:T(8,128)(2,1)S(1)}, bf16[2,256,256]{2,1,0:T(8,128)(2,1)S(1)}, u32[]{:S(2)}, u32[]{:S(2)}) collective-permute-start(bf16[2,256,256]{2,1,0:T(8,128)(2,1)S(1)} %shard_map.65), channel_id=1, source_target_pairs={{0,64},{1,65},{16,80},{17,81},{32,96},{33,97},{48,112},{49,113},{2... | collective-permute-start | bytes 786440 | tf_op jit(solution)/shard_map/far/ppermute | solution.py:33
  41.7 5.8 %shard_map.69.second = bf16[2,1440,256]{2,1,0:T(8,128)(2,1)S(1)} custom-call(s32[8,16]{1,0:T(8,128)S(1)} %get-tuple-element.31.refs_0_, bf16[2,1440,256]{2,1,0:T(8,128)(2,1)S(1)} %get-tuple-element.32.refs_1_, bf16[1280,1280]{1,0:T(8,128)(2,1)S(1)} %get-tuple-element.36.refs_2_, bf16[2,2,256,256]{3,2,1,0:T(8,128)(2,1)S(1)} %pad_maximum_fusion.refs_3_, ...), custom_call_target="tpu_custom_call" | custom-call | flops 1024 | bytes 1024 | tf_op jit(solution)/shard_map/pallas_call | solution.py:356
  47.5 0.7 %collective-permute-done.19.far_ref = bf16[2,256,256]{2,1,0:T(8,128)(2,1)S(1)} collective-permute-done((bf16[2,256,256]{2,1,0:T(8,128)(2,1)S(1)}, bf16[2,256,256]{2,1,0:T(8,128)(2,1)S(1)}, u32[]{:S(2)}, u32[]{:S(2)}) %collective-permute-start.19) | collective-permute-done | bytes 262176 | tf_op jit(solution)/shard_map/far/ppermute | solution.py:33
  48.2 5.5 %shard_map.70 = bf16[1024,2,256]{2,1,0:T(2,128)(2,1)} custom-call(bf16[2,1440,256]{2,1,0:T(8,128)(2,1)S(1)} %shard_map.69.second, bf16[1024,1280]{1,0:T(8,128)(2,1)S(1)} %get-tuple-element.47.back_ref, bf16[2,2,256,256]{3,2,1,0:T(8,128)(2,1)S(1)} %shard_map.68.ends_ref, bf16[2,256,256]{2,1,0:T(8,128)(2,1)S(1)} %collective-permute-done.19.far_ref), custom_call_target="tpu_custom_call" | custom-call | flops 1024 | bytes 1024 | tf_op jit(solution)/shard_map/pallas_call | solution.py:363
  (30 shorter events, 1.9 us)
Async XLA Ops:
  0.0 30.2 %copy-start = (bf16[1024,2,256]{2,1,0:T(2,128)(2,1)S(1)}, bf16[1024,2,256]{2,1,0:T(2,128)(2,1)}, u32[]{:S(2)}) copy-start(bf16[1024,2,256]{2,1,0:T(2,128)(2,1)} %rows_hbm.1) | copy-start | bytes 3145732
  1.2 4.1 %collective-permute-start = (bf16[2,2,256,256]{3,2,1,0:T(8,128)(2,1)S(1)}, bf16[2,2,256,256]{3,2,1,0:T(8,128)(2,1)S(1)}, u32[]{:S(2)}, u32[]{:S(2)}) collective-permute-start(bf16[2,2,256,256]{3,2,1,0:T(8,128)(2,1)S(1)} %pad_maximum_fusion.refs_3_), channel_id=1, source_target_pairs={{0,1},{1,0},{16,17},{17,16},{32,33},{33,32},{48,49},{49,48},{2,3},... | collective-permute-start | bytes 1572872 | tf_op jit(solution)/shard_map/sibling/ppermute | solution.py:33
  2.7 12.7 %collective-permute-start.5 = (bf16[2,2,256,256]{3,2,1,0:T(8,128)(2,1)S(1)}, bf16[2,2,256,256]{3,2,1,0:T(8,128)(2,1)S(1)}, u32[]{:S(2)}, u32[]{:S(2)}) collective-permute-start(bf16[2,2,256,256]{3,2,1,0:T(8,128)(2,1)S(1)} %pad_maximum_fusion.refs_3_), channel_id=1, source_target_pairs={{0,4},{1,13},{16,20},{17,29},{32,36},{33,45},{48,52},{49,61},{2,6}... | collective-permute-start | bytes 1572872 | tf_op jit(solution)/shard_map/side/ppermute | solution.py:33
  5.2 10.1 %collective-permute-start.6 = (bf16[2,2,256,256]{3,2,1,0:T(8,128)(2,1)S(1)}, bf16[2,2,256,256]{3,2,1,0:T(8,128)(2,1)S(1)}, u32[]{:S(2)}, u32[]{:S(2)}) collective-permute-start(bf16[2,2,256,256]{3,2,1,0:T(8,128)(2,1)S(1)} %pad_maximum_fusion.refs_3_), channel_id=1, source_target_pairs={{0,2},{1,67},{16,18},{17,83},{32,34},{33,99},{48,50},{49,115},{2,6... | collective-permute-start | bytes 1572872 | tf_op jit(solution)/shard_map/turned/ppermute | solution.py:33
  8.0 1.7 %collective-permute-start.1 = (bf16[2,2,128,256]{3,2,1,0:T(8,128)(2,1)}, bf16[2,2,128,256]{3,2,1,0:T(8,128)(2,1)S(1)}, u32[]{:S(2)}, u32[]{:S(2)}) collective-permute-start(bf16[2,2,128,256]{3,2,1,0:T(8,128)(2,1)} %bitcast.7), channel_id=1, source_target_pairs={{0,1},{1,0},{16,17},{17,16},{32,33},{33,32},{48,49},{49,48},{2,3},... | collective-permute-start | bytes 786440 | tf_op jit(solution)/shard_map/stem_other/ppermute | solution.py:33
  8.0 14.4 %collective-permute-start.11 = (bf16[2,2,256,256]{3,2,1,0:T(8,128)(2,1)S(1)}, bf16[2,2,256,256]{3,2,1,0:T(8,128)(2,1)S(1)}, u32[]{:S(2)}, u32[]{:S(2)}) collective-permute-start(bf16[2,2,256,256]{3,2,1,0:T(8,128)(2,1)S(1)} %collective-permute-done.refs_4_), channel_id=1, source_target_pairs={{0,4},{1,13},{16,20},{17,29},{32,36},{33,45},{48,52},{49,61},{2,6}... | collective-permute-start | bytes 1572872 | tf_op jit(solution)/shard_map/side_far/ppermute | solution.py:33
  9.7 1.0 %copy-start.1 = (bf16[1,2,2,128,256]{4,3,2,1,0:T(8,128)(2,1)S(1)}, bf16[1,2,2,128,256]{4,3,2,1,0:T(8,128)(2,1)}, u32[]{:S(2)}) copy-start(bf16[1,2,2,128,256]{4,3,2,1,0:T(8,128)(2,1)} %param.11) | copy-start | bytes 786436
  11.6 10.8 %collective-permute-start.2 = (bf16[2,256,256]{2,1,0:T(8,128)(2,1)S(1)}, bf16[2,256,256]{2,1,0:T(8,128)(2,1)S(1)}, u32[]{:S(2)}, u32[]{:S(2)}) collective-permute-start(bf16[2,256,256]{2,1,0:T(8,128)(2,1)S(1)} %shard_map.64.a_ref), channel_id=1, source_target_pairs={{0,16},{1,49},{16,32},{17,1},{32,48},{33,17},{48,0},{49,33},{2,18}... | collective-permute-start | bytes 786440 | tf_op jit(solution)/shard_map/near/ppermute | solution.py:33
  15.4 13.2 %collective-permute-start.7 = (bf16[2,2,256,256]{3,2,1,0:T(8,128)(2,1)S(1)}, bf16[2,2,256,256]{3,2,1,0:T(8,128)(2,1)S(1)}, u32[]{:S(2)}, u32[]{:S(2)}) collective-permute-start(bf16[2,2,256,256]{3,2,1,0:T(8,128)(2,1)S(1)} %collective-permute-done.5.refs_5_), channel_id=1, source_target_pairs={{0,4},{1,13},{16,20},{17,29},{32,36},{33,45},{48,52},{49,61},{2,6}... | collective-permute-start | bytes 1572872 | tf_op jit(solution)/shard_map/across/ppermute | solution.py:33
  16.9 11.7 %collective-permute-start.8 = (bf16[2,2,256,256]{3,2,1,0:T(8,128)(2,1)S(1)}, bf16[2,2,256,256]{3,2,1,0:T(8,128)(2,1)S(1)}, u32[]{:S(2)}, u32[]{:S(2)}) collective-permute-start(bf16[2,2,256,256]{3,2,1,0:T(8,128)(2,1)S(1)} %collective-permute-done.5.refs_5_), channel_id=1, source_target_pairs={{0,2},{1,67},{16,18},{17,83},{32,34},{33,99},{48,50},{49,115},{2,6... | collective-permute-start | bytes 1572872 | tf_op jit(solution)/shard_map/side_turned/ppermute | solution.py:33
  18.8 8.5 %collective-permute-start.4 = (bf16[2,256,256]{2,1,0:T(8,128)(2,1)S(1)}, bf16[2,256,256]{2,1,0:T(8,128)(2,1)S(1)}, u32[]{:S(2)}, u32[]{:S(2)}) collective-permute-start(bf16[2,256,256]{2,1,0:T(8,128)(2,1)S(1)} %shard_map.64.a_ref), channel_id=1, source_target_pairs={{0,32},{1,33},{16,48},{17,49},{32,0},{33,1},{48,16},{49,17},{2,34}... | collective-permute-start | bytes 786440 | tf_op jit(solution)/shard_map/opposite/ppermute | solution.py:33
  22.4 4.9 %collective-permute-start.3 = (bf16[2,256,256]{2,1,0:T(8,128)(2,1)S(1)}, bf16[2,256,256]{2,1,0:T(8,128)(2,1)S(1)}, u32[]{:S(2)}, u32[]{:S(2)}) collective-permute-start(bf16[2,256,256]{2,1,0:T(8,128)(2,1)S(1)} %collective-permute-done.2.b_ref), channel_id=1, source_target_pairs={{0,1},{1,0},{16,17},{17,16},{32,33},{33,32},{48,49},{49,48},{2,3},... | collective-permute-start | bytes 786440 | tf_op jit(solution)/shard_map/near_other/ppermute | solution.py:33
  22.4 12.3 %collective-permute-start.15 = (bf16[2,2,256,256]{3,2,1,0:T(8,128)(2,1)S(1)}, bf16[2,2,256,256]{3,2,1,0:T(8,128)(2,1)S(1)}, u32[]{:S(2)}, u32[]{:S(2)}) collective-permute-start(bf16[2,2,256,256]{3,2,1,0:T(8,128)(2,1)S(1)} %collective-permute-done.11.refs_9_), channel_id=1, source_target_pairs={{0,2},{1,67},{16,18},{17,83},{32,34},{33,99},{48,50},{49,115},{2,6... | collective-permute-start | bytes 1572872 | tf_op jit(solution)/shard_map/side_far_turned/ppermute | solution.py:33
  28.6 9.5 %collective-permute-start.17 = (bf16[2,2,256,256]{3,2,1,0:T(8,128)(2,1)S(1)}, bf16[2,2,256,256]{3,2,1,0:T(8,128)(2,1)S(1)}, u32[]{:S(2)}, u32[]{:S(2)}) collective-permute-start(bf16[2,2,256,256]{3,2,1,0:T(8,128)(2,1)S(1)} %collective-permute-done.8.refs_11_), channel_id=1, source_target_pairs={{0,4},{1,13},{16,20},{17,29},{32,36},{33,45},{48,52},{49,61},{2,6}... | collective-permute-start | bytes 1572872 | tf_op jit(solution)/shard_map/across_turned/ppermute | solution.py:33
  34.0 4.4 %collective-permute-start.9 = (bf16[2,2,256,256]{3,2,1,0:T(8,128)(2,1)S(1)}, bf16[2,2,256,256]{3,2,1,0:T(8,128)(2,1)S(1)}, u32[]{:S(2)}, u32[]{:S(2)}) collective-permute-start(bf16[2,2,256,256]{3,2,1,0:T(8,128)(2,1)S(1)} %collective-permute-done.5.refs_5_), channel_id=1, source_target_pairs={{0,1},{1,0},{16,17},{17,16},{32,33},{33,32},{48,49},{49,48},{2,3},... | collective-permute-start | bytes 1572872 | tf_op jit(solution)/shard_map/shared/ppermute | solution.py:33
  34.1 4.6 %collective-permute-start.10 = (bf16[2,2,256,256]{3,2,1,0:T(8,128)(2,1)S(1)}, bf16[2,2,256,256]{3,2,1,0:T(8,128)(2,1)S(1)}, u32[]{:S(2)}, u32[]{:S(2)}) collective-permute-start(bf16[2,2,256,256]{3,2,1,0:T(8,128)(2,1)S(1)} %collective-permute-done.6.refs_7_), channel_id=1, source_target_pairs={{0,1},{1,0},{16,17},{17,16},{32,33},{33,32},{48,49},{49,48},{2,3},... | collective-permute-start | bytes 1572872 | tf_op jit(solution)/shard_map/shared/ppermute | solution.py:33
  34.5 4.3 %collective-permute-start.12 = (bf16[2,2,256,256]{3,2,1,0:T(8,128)(2,1)S(1)}, bf16[2,2,256,256]{3,2,1,0:T(8,128)(2,1)S(1)}, u32[]{:S(2)}, u32[]{:S(2)}) collective-permute-start(bf16[2,2,256,256]{3,2,1,0:T(8,128)(2,1)S(1)} %collective-permute-done.11.refs_9_), channel_id=1, source_target_pairs={{0,1},{1,0},{16,17},{17,16},{32,33},{33,32},{48,49},{49,48},{2,3},... | collective-permute-start | bytes 1572872 | tf_op jit(solution)/shard_map/shared/ppermute | solution.py:33
  34.7 6.8 %collective-permute-start.13 = (bf16[2,2,256,256]{3,2,1,0:T(8,128)(2,1)S(1)}, bf16[2,2,256,256]{3,2,1,0:T(8,128)(2,1)S(1)}, u32[]{:S(2)}, u32[]{:S(2)}) collective-permute-start(bf16[2,2,256,256]{3,2,1,0:T(8,128)(2,1)S(1)} %collective-permute-done.8.refs_11_), channel_id=1, source_target_pairs={{0,1},{1,0},{16,17},{17,16},{32,33},{33,32},{48,49},{49,48},{2,3},... | collective-permute-start | bytes 1572872 | tf_op jit(solution)/shard_map/shared/ppermute | solution.py:33
  38.2 3.3 %collective-permute-start.14 = (bf16[2,2,256,256]{3,2,1,0:T(8,128)(2,1)S(1)}, bf16[2,2,256,256]{3,2,1,0:T(8,128)(2,1)S(1)}, u32[]{:S(2)}, u32[]{:S(2)}) collective-permute-start(bf16[2,2,256,256]{3,2,1,0:T(8,128)(2,1)S(1)} %collective-permute-done.7.refs_13_), channel_id=1, source_target_pairs={{0,1},{1,0},{16,17},{17,16},{32,33},{33,32},{48,49},{49,48},{2,3},... | collective-permute-start | bytes 1572872 | tf_op jit(solution)/shard_map/shared/ppermute | solution.py:33
  38.4 3.1 %collective-permute-start.16 = (bf16[2,2,256,256]{3,2,1,0:T(8,128)(2,1)S(1)}, bf16[2,2,256,256]{3,2,1,0:T(8,128)(2,1)S(1)}, u32[]{:S(2)}, u32[]{:S(2)}) collective-permute-start(bf16[2,2,256,256]{3,2,1,0:T(8,128)(2,1)S(1)} %collective-permute-done.15.refs_15_), channel_id=1, source_target_pairs={{0,1},{1,0},{16,17},{17,16},{32,33},{33,32},{48,49},{49,48},{2,3},... | collective-permute-start | bytes 1572872 | tf_op jit(solution)/shard_map/shared/ppermute | solution.py:33
  38.8 2.9 %collective-permute-start.18 = (bf16[2,2,256,256]{3,2,1,0:T(8,128)(2,1)S(1)}, bf16[2,2,256,256]{3,2,1,0:T(8,128)(2,1)S(1)}, u32[]{:S(2)}, u32[]{:S(2)}) collective-permute-start(bf16[2,2,256,256]{3,2,1,0:T(8,128)(2,1)S(1)} %collective-permute-done.17.refs_17_), channel_id=1, source_target_pairs={{0,1},{1,0},{16,17},{17,16},{32,33},{33,32},{48,49},{49,48},{2,3},... | collective-permute-start | bytes 1572872 | tf_op jit(solution)/shard_map/shared/ppermute | solution.py:33
  38.9 9.3 %collective-permute-start.19 = (bf16[2,256,256]{2,1,0:T(8,128)(2,1)S(1)}, bf16[2,256,256]{2,1,0:T(8,128)(2,1)S(1)}, u32[]{:S(2)}, u32[]{:S(2)}) collective-permute-start(bf16[2,256,256]{2,1,0:T(8,128)(2,1)S(1)} %shard_map.65), channel_id=1, source_target_pairs={{0,64},{1,65},{16,80},{17,81},{32,96},{33,97},{48,112},{49,113},{2... | collective-permute-start | bytes 786440 | tf_op jit(solution)/shard_map/far/ppermute | solution.py:33

commit v5 on v3

--- a/solution.py
+++ b/solution.py
@@ -94,7 +94,8 @@
     copy = pltpu.make_async_copy(rows_hbm, rows_ref, sem)
     copy.start()
     x, p, c = where_ref[2], where_ref[3], where_ref[1]
-    triangle = (iota((ROWS, ROWS), 0) < iota((ROWS, ROWS), 1)).astype(BF16)
+    step = 256
+    triangle = (iota((step, step), 0) < iota((step, step), 1)).astype(BF16)
     node = iota((NODES, ROWS), 0)
     match = jnp.concatenate(
         [
@@ -103,8 +104,13 @@
         ],
         axis=0,
     )
-    before = mm(match.astype(BF16), triangle)
-    total = round_up(jnp.sum(match, axis=1, keepdims=True))
+    before, passed = [], jnp.zeros((2 * NODES, 1), F32)
+    for block in range(ROWS // step):
+        piece = match[:, block * step : (block + 1) * step]
+        before.append(mm(piece.astype(BF16), triangle) + passed)
+        passed = passed + jnp.sum(piece, axis=1, keepdims=True)
+    before = jnp.concatenate(before, axis=1)
+    total = round_up(passed)
     lower = (iota((NODES, NODES), 1) < iota((NODES, NODES), 0)).astype(BF16)
     upper = (iota((NODES, NODES), 0) < iota((NODES, NODES), 1)).astype(BF16)
     places, rows_of_table = [], []

time: 54.1 us -> 54.1 us (level)
  transfers between devices with their start and end apart: 20 -> 20, of which waited for: 4 -> 4; matrix products, arithmetic and copies ran while one was open for 1% -> 1% of each run, Pallas kernels for 29% -> 28%
where the time goes in v5:
time: 54.1 us; the launch traced here: 53.7 us
  starting transfers between devices  26.1 us (48%)
  Pallas kernels  20.7 us (38%)
  waiting for transfers between devices  3.91 us (7%)
  other arithmetic  1.96 us (4%)
  local copies, waits for them, and re-layouts  0.95 us (2%)
    ppermute x20, starting transfers between devices, routed(): return lax.ppermute(value, AXES, pairs)  26.1 us
    pallas_call x1, Pallas kernels, body(): call(nodes_kernel, jax.ShapeDtypeStruct((2, ROOM, BOND), BF16), [smem()]...  6.11 us
    pallas_call x1, Pallas kernels, body(): call(stem_kernel, jax.ShapeDtypeStruct((ROWS, 2, BOND), BF16), [vmem()] *...  5.54 us
    ppermute x20, waiting for transfers between devices, routed(): return lax.ppermute(value, AXES, pairs)  3.91 us
    pallas_call x1, Pallas kernels, body(): call(prepare_kernel, (jax.ShapeDtypeStruct((2, ROOM, BOND), BF16), jax.Sh...  3.72 us
    pallas_call x1, Pallas kernels, body(): call(select_kernel, (jax.ShapeDtypeStruct((SORTED, SORTED), BF16), jax.Sh...  1.65 us
    pallas_call x1, Pallas kernels, body(): call(ends_kernel, jax.ShapeDtypeStruct((2, 2, BOND, BOND), BF16), [smem()...  1.43 us
    pallas_call x1, Pallas kernels, body(): call(ring_kernel, matrix, [smem()] + [vmem()] * 4, [pltpu.VMEM((4, 2, BON...  1.35 us
  transfers between devices with their start and end apart: 20, of which 4 were waited for; matrix products, arithmetic and copies ran while one was open for 1% of the time, Pallas kernels for 28%

profile of v5, /device:TPU:1, one launch (start us, length us, event | category | flops | bytes accessed | tf_op | source)
XLA Modules:
  0.0 53.7 jit_solution(2768527993479309036)
XLA Ops:
  0.0 1.2 %pad_maximum_fusion.refs_3_ = bf16[2,2,256,256]{3,2,1,0:T(8,128)(2,1)S(1)} fusion(bf16[1,2,256,256]{3,2,1,0:T(8,128)(2,1)} %param.10, bf16[1,2,256,256]{3,2,1,0:T(8,128)(2,1)} %param.9), kind=kLoop, calls=%fused_computation | loop fusion | flops 262144 | bytes 1048576 | tf_op jit(solution)/shard_map/concatenate | solution.py:292
  1.2 1.5 %collective-permute-start = (bf16[2,2,256,256]{3,2,1,0:T(8,128)(2,1)S(1)}, bf16[2,2,256,256]{3,2,1,0:T(8,128)(2,1)S(1)}, u32[]{:S(2)}, u32[]{:S(2)}) collective-permute-start(bf16[2,2,256,256]{3,2,1,0:T(8,128)(2,1)S(1)} %pad_maximum_fusion.refs_3_), channel_id=1, source_target_pairs={{0,1},{1,0},{16,17},{17,16},{32,33},{33,32},{48,49},{49,48},{2,3},... | collective-permute-start | bytes 1572872 | tf_op jit(solution)/shard_map/sibling/ppermute | solution.py:33
  2.7 2.6 %collective-permute-start.5 = (bf16[2,2,256,256]{3,2,1,0:T(8,128)(2,1)S(1)}, bf16[2,2,256,256]{3,2,1,0:T(8,128)(2,1)S(1)}, u32[]{:S(2)}, u32[]{:S(2)}) collective-permute-start(bf16[2,2,256,256]{3,2,1,0:T(8,128)(2,1)S(1)} %pad_maximum_fusion.refs_3_), channel_id=1, source_target_pairs={{0,4},{1,13},{16,20},{17,29},{32,36},{33,45},{48,52},{49,61},{2,6}... | collective-permute-start | bytes 1572872 | tf_op jit(solution)/shard_map/side/ppermute | solution.py:33
  5.2 2.7 %collective-permute-start.6 = (bf16[2,2,256,256]{3,2,1,0:T(8,128)(2,1)S(1)}, bf16[2,2,256,256]{3,2,1,0:T(8,128)(2,1)S(1)}, u32[]{:S(2)}, u32[]{:S(2)}) collective-permute-start(bf16[2,2,256,256]{3,2,1,0:T(8,128)(2,1)S(1)} %pad_maximum_fusion.refs_3_), channel_id=1, source_target_pairs={{0,2},{1,67},{16,18},{17,83},{32,34},{33,99},{48,50},{49,115},{2,6... | collective-permute-start | bytes 1572872 | tf_op jit(solution)/shard_map/turned/ppermute | solution.py:33
  8.0 1.5 %collective-permute-start.11 = (bf16[2,2,256,256]{3,2,1,0:T(8,128)(2,1)S(1)}, bf16[2,2,256,256]{3,2,1,0:T(8,128)(2,1)S(1)}, u32[]{:S(2)}, u32[]{:S(2)}) collective-permute-start(bf16[2,2,256,256]{3,2,1,0:T(8,128)(2,1)S(1)} %collective-permute-done.refs_4_), channel_id=1, source_target_pairs={{0,4},{1,13},{16,20},{17,29},{32,36},{33,45},{48,52},{49,61},{2,6}... | collective-permute-start | bytes 1572872 | tf_op jit(solution)/shard_map/side_far/ppermute | solution.py:33
  9.7 0.9 %copy-done.1 = bf16[1,2,2,128,256]{4,3,2,1,0:T(8,128)(2,1)S(1)} copy-done((bf16[1,2,2,128,256]{4,3,2,1,0:T(8,128)(2,1)S(1)}, bf16[1,2,2,128,256]{4,3,2,1,0:T(8,128)(2,1)}, u32[]{:S(2)}) %copy-start.1) | copy-done | bytes 262168
  10.7 0.9 %shard_map.64.a_ref = bf16[2,256,256]{2,1,0:T(8,128)(2,1)S(1)} custom-call(s32[4]{0:T(128)S(1)} %pad_add_fusion.1.where_ref, bf16[2,2,128,256]{3,2,1,0:T(8,128)(2,1)S(1)} %bitcast.8, bf16[2,2,128,256]{3,2,1,0:T(8,128)(2,1)S(1)} %collective-permute-done.1.other_ref), custom_call_target="tpu_custom_call" | custom-call | flops 1024 | bytes 1024 | tf_op jit(solution)/shard_map/pallas_call | solution.py:305
  11.6 3.8 %collective-permute-start.2 = (bf16[2,256,256]{2,1,0:T(8,128)(2,1)S(1)}, bf16[2,256,256]{2,1,0:T(8,128)(2,1)S(1)}, u32[]{:S(2)}, u32[]{:S(2)}) collective-permute-start(bf16[2,256,256]{2,1,0:T(8,128)(2,1)S(1)} %shard_map.64.a_ref), channel_id=1, source_target_pairs={{0,16},{1,49},{16,32},{17,1},{32,48},{33,17},{48,0},{49,33},{2,18}... | collective-permute-start | bytes 786440 | tf_op jit(solution)/shard_map/near/ppermute | solution.py:33
  15.4 1.5 %collective-permute-start.7 = (bf16[2,2,256,256]{3,2,1,0:T(8,128)(2,1)S(1)}, bf16[2,2,256,256]{3,2,1,0:T(8,128)(2,1)S(1)}, u32[]{:S(2)}, u32[]{:S(2)}) collective-permute-start(bf16[2,2,256,256]{3,2,1,0:T(8,128)(2,1)S(1)} %collective-permute-done.5.refs_5_), channel_id=1, source_target_pairs={{0,4},{1,13},{16,20},{17,29},{32,36},{33,45},{48,52},{49,61},{2,6}... | collective-permute-start | bytes 1572872 | tf_op jit(solution)/shard_map/across/ppermute | solution.py:33
  16.9 1.8 %collective-permute-start.8 = (bf16[2,2,256,256]{3,2,1,0:T(8,128)(2,1)S(1)}, bf16[2,2,256,256]{3,2,1,0:T(8,128)(2,1)S(1)}, u32[]{:S(2)}, u32[]{:S(2)}) collective-permute-start(bf16[2,2,256,256]{3,2,1,0:T(8,128)(2,1)S(1)} %collective-permute-done.5.refs_5_), channel_id=1, source_target_pairs={{0,2},{1,67},{16,18},{17,83},{32,34},{33,99},{48,50},{49,115},{2,6... | collective-permute-start | bytes 1572872 | tf_op jit(solution)/shard_map/side_turned/ppermute | solution.py:33
  18.8 3.6 %collective-permute-start.4 = (bf16[2,256,256]{2,1,0:T(8,128)(2,1)S(1)}, bf16[2,256,256]{2,1,0:T(8,128)(2,1)S(1)}, u32[]{:S(2)}, u32[]{:S(2)}) collective-permute-start(bf16[2,256,256]{2,1,0:T(8,128)(2,1)S(1)} %shard_map.64.a_ref), channel_id=1, source_target_pairs={{0,32},{1,33},{16,48},{17,49},{32,0},{33,1},{48,16},{49,17},{2,34}... | collective-permute-start | bytes 786440 | tf_op jit(solution)/shard_map/opposite/ppermute | solution.py:33
  22.4 1.0 %collective-permute-start.15 = (bf16[2,2,256,256]{3,2,1,0:T(8,128)(2,1)S(1)}, bf16[2,2,256,256]{3,2,1,0:T(8,128)(2,1)S(1)}, u32[]{:S(2)}, u32[]{:S(2)}) collective-permute-start(bf16[2,2,256,256]{3,2,1,0:T(8,128)(2,1)S(1)} %collective-permute-done.11.refs_9_), channel_id=1, source_target_pairs={{0,2},{1,67},{16,18},{17,83},{32,34},{33,99},{48,50},{49,115},{2,6... | collective-permute-start | bytes 1572872 | tf_op jit(solution)/shard_map/side_far_turned/ppermute | solution.py:33
  23.4 0.7 %pad_add_fusion.parents_ref = s32[2,1024]{1,0:T(2,128)S(1)} fusion(s32[1,1024]{1,0:T(1,128)} %bitcast.9, s32[1,1024]{1,0:T(1,128)} %bitcast.10), kind=kLoop, calls=%fused_computation.1 | loop fusion | flops 2048 | bytes 16384 | tf_op jit(solution)/shard_map/concatenate | solution.py:327
  24.1 3.2 %collective-permute-done.4.d_ref = bf16[2,256,256]{2,1,0:T(8,128)(2,1)S(1)} collective-permute-done((bf16[2,256,256]{2,1,0:T(8,128)(2,1)S(1)}, bf16[2,256,256]{2,1,0:T(8,128)(2,1)S(1)}, u32[]{:S(2)}, u32[]{:S(2)}) %collective-permute-start.4) | collective-permute-done | bytes 262176 | tf_op jit(solution)/shard_map/opposite/ppermute | solution.py:33
  27.3 1.4 %shard_map.65 = bf16[2,256,256]{2,1,0:T(8,128)(2,1)S(1)} custom-call(s32[4]{0:T(128)S(1)} %pad_add_fusion.1.where_ref, bf16[2,256,256]{2,1,0:T(8,128)(2,1)S(1)} %shard_map.64.a_ref, bf16[2,256,256]{2,1,0:T(8,128)(2,1)S(1)} %collective-permute-done.2.b_ref, bf16[2,256,256]{2,1,0:T(8,128)(2,1)S(1)} %collective-permute-done.3.c_ref, ...), custom_call_target="tpu_custom_call" | custom-call | flops 1024 | bytes 1024 | tf_op jit(solution)/shard_map/pallas_call | solution.py:322
  28.6 1.5 %collective-permute-start.17 = (bf16[2,2,256,256]{3,2,1,0:T(8,128)(2,1)S(1)}, bf16[2,2,256,256]{3,2,1,0:T(8,128)(2,1)S(1)}, u32[]{:S(2)}, u32[]{:S(2)}) collective-permute-start(bf16[2,2,256,256]{3,2,1,0:T(8,128)(2,1)S(1)} %collective-permute-done.8.refs_11_), channel_id=1, source_target_pairs={{0,4},{1,13},{16,20},{17,29},{32,36},{33,45},{48,52},{49,61},{2,6}... | collective-permute-start | bytes 1572872 | tf_op jit(solution)/shard_map/across_turned/ppermute | solution.py:33
  30.2 3.7 %shard_map.66 = (bf16[2,1440,256]{2,1,0:T(8,128)(2,1)S(1)}, s32[8,1280]{1,0:T(8,128)S(1)}, f32[8,1024]{1,0:T(8,128)S(1)}, s32[8,16]{1,0:T(8,128)S(1)}) custom-call(s32[4]{0:T(128)S(1)} %pad_add_fusion.1.where_ref, s32[2,1024]{1,0:T(2,128)S(1)} %pad_add_fusion.parents_ref, bf16[1024,2,256]{2,1,0:T(2,128)(2,1)S(1)} %copy-done), custom_call_target="tpu_custom_call" | custom-call | flops 1024 | bytes 1024 | tf_op jit(solution)/shard_map/pallas_call | solution.py:328
  34.6 0.4 collective-permute-start.13
  35.0 1.7 %shard_map.67 = (bf16[1280,1280]{1,0:T(8,128)(2,1)S(1)}, bf16[1024,1280]{1,0:T(8,128)(2,1)S(1)}) custom-call(s32[8,1280]{1,0:T(8,128)S(1)} %get-tuple-element.34.goes_ref, f32[8,1024]{1,0:T(8,128)S(1)} %get-tuple-element.35.place_ref), custom_call_target="tpu_custom_call" | custom-call | flops 1024 | bytes 1024 | tf_op jit(solution)/shard_map/pallas_call | solution.py:344
  36.7 1.4 %shard_map.68.ends_ref = bf16[2,2,256,256]{3,2,1,0:T(8,128)(2,1)S(1)} custom-call(s32[4]{0:T(128)S(1)} %pad_add_fusion.1.where_ref, bf16[2,256,256]{2,1,0:T(8,128)(2,1)S(1)} %shard_map.64.a_ref, bf16[2,256,256]{2,1,0:T(8,128)(2,1)S(1)} %collective-permute-done.2.b_ref, bf16[2,256,256]{2,1,0:T(8,128)(2,1)S(1)} %collective-permute-done.3.c_ref, ...), custom_call_target="tpu_custom_call" | custom-call | flops 1024 | bytes 1024 | tf_op jit(solution)/shard_map/pallas_call | solution.py:349
  38.8 2.6 %collective-permute-start.19 = (bf16[2,256,256]{2,1,0:T(8,128)(2,1)S(1)}, bf16[2,256,256]{2,1,0:T(8,128)(2,1)S(1)}, u32[]{:S(2)}, u32[]{:S(2)}) collective-permute-start(bf16[2,256,256]{2,1,0:T(8,128)(2,1)S(1)} %shard_map.65), channel_id=1, source_target_pairs={{0,64},{1,65},{16,80},{17,81},{32,96},{33,97},{48,112},{49,113},{2... | collective-permute-start | bytes 786440 | tf_op jit(solution)/shard_map/far/ppermute | solution.py:33
  41.6 6.1 %shard_map.69.second = bf16[2,1440,256]{2,1,0:T(8,128)(2,1)S(1)} custom-call(s32[8,16]{1,0:T(8,128)S(1)} %get-tuple-element.31.refs_0_, bf16[2,1440,256]{2,1,0:T(8,128)(2,1)S(1)} %get-tuple-element.32.refs_1_, bf16[1280,1280]{1,0:T(8,128)(2,1)S(1)} %get-tuple-element.36.refs_2_, bf16[2,2,256,256]{3,2,1,0:T(8,128)(2,1)S(1)} %pad_maximum_fusion.refs_3_, ...), custom_call_target="tpu_custom_call" | custom-call | flops 1024 | bytes 1024 | tf_op jit(solution)/shard_map/pallas_call | solution.py:366
  47.7 0.4 collective-permute-done.19.far_ref
  48.1 5.5 %shard_map.70 = bf16[1024,2,256]{2,1,0:T(2,128)(2,1)} custom-call(bf16[2,1440,256]{2,1,0:T(8,128)(2,1)S(1)} %shard_map.69.second, bf16[1024,1280]{1,0:T(8,128)(2,1)S(1)} %get-tuple-element.47.back_ref, bf16[2,2,256,256]{3,2,1,0:T(8,128)(2,1)S(1)} %shard_map.68.ends_ref, bf16[2,256,256]{2,1,0:T(8,128)(2,1)S(1)} %collective-permute-done.19.far_ref), custom_call_target="tpu_custom_call" | custom-call | flops 1024 | bytes 1024 | tf_op jit(solution)/shard_map/pallas_call | solution.py:373
  (30 shorter events, 1.8 us)
Async XLA Ops:
  0.0 30.2 %copy-start = (bf16[1024,2,256]{2,1,0:T(2,128)(2,1)S(1)}, bf16[1024,2,256]{2,1,0:T(2,128)(2,1)}, u32[]{:S(2)}) copy-start(bf16[1024,2,256]{2,1,0:T(2,128)(2,1)} %rows_hbm.1) | copy-start | bytes 3145732
  1.2 4.1 %collective-permute-start = (bf16[2,2,256,256]{3,2,1,0:T(8,128)(2,1)S(1)}, bf16[2,2,256,256]{3,2,1,0:T(8,128)(2,1)S(1)}, u32[]{:S(2)}, u32[]{:S(2)}) collective-permute-start(bf16[2,2,256,256]{3,2,1,0:T(8,128)(2,1)S(1)} %pad_maximum_fusion.refs_3_), channel_id=1, source_target_pairs={{0,1},{1,0},{16,17},{17,16},{32,33},{33,32},{48,49},{49,48},{2,3},... | collective-permute-start | bytes 1572872 | tf_op jit(solution)/shard_map/sibling/ppermute | solution.py:33
  2.7 12.7 %collective-permute-start.5 = (bf16[2,2,256,256]{3,2,1,0:T(8,128)(2,1)S(1)}, bf16[2,2,256,256]{3,2,1,0:T(8,128)(2,1)S(1)}, u32[]{:S(2)}, u32[]{:S(2)}) collective-permute-start(bf16[2,2,256,256]{3,2,1,0:T(8,128)(2,1)S(1)} %pad_maximum_fusion.refs_3_), channel_id=1, source_target_pairs={{0,4},{1,13},{16,20},{17,29},{32,36},{33,45},{48,52},{49,61},{2,6}... | collective-permute-start | bytes 1572872 | tf_op jit(solution)/shard_map/side/ppermute | solution.py:33
  5.2 10.1 %collective-permute-start.6 = (bf16[2,2,256,256]{3,2,1,0:T(8,128)(2,1)S(1)}, bf16[2,2,256,256]{3,2,1,0:T(8,128)(2,1)S(1)}, u32[]{:S(2)}, u32[]{:S(2)}) collective-permute-start(bf16[2,2,256,256]{3,2,1,0:T(8,128)(2,1)S(1)} %pad_maximum_fusion.refs_3_), channel_id=1, source_target_pairs={{0,2},{1,67},{16,18},{17,83},{32,34},{33,99},{48,50},{49,115},{2,6... | collective-permute-start | bytes 1572872 | tf_op jit(solution)/shard_map/turned/ppermute | solution.py:33
  8.0 1.7 %collective-permute-start.1 = (bf16[2,2,128,256]{3,2,1,0:T(8,128)(2,1)}, bf16[2,2,128,256]{3,2,1,0:T(8,128)(2,1)S(1)}, u32[]{:S(2)}, u32[]{:S(2)}) collective-permute-start(bf16[2,2,128,256]{3,2,1,0:T(8,128)(2,1)} %bitcast.7), channel_id=1, source_target_pairs={{0,1},{1,0},{16,17},{17,16},{32,33},{33,32},{48,49},{49,48},{2,3},... | collective-permute-start | bytes 786440 | tf_op jit(solution)/shard_map/stem_other/ppermute | solution.py:33
  8.0 14.4 %collective-permute-start.11 = (bf16[2,2,256,256]{3,2,1,0:T(8,128)(2,1)S(1)}, bf16[2,2,256,256]{3,2,1,0:T(8,128)(2,1)S(1)}, u32[]{:S(2)}, u32[]{:S(2)}) collective-permute-start(bf16[2,2,256,256]{3,2,1,0:T(8,128)(2,1)S(1)} %collective-permute-done.refs_4_), channel_id=1, source_target_pairs={{0,4},{1,13},{16,20},{17,29},{32,36},{33,45},{48,52},{49,61},{2,6}... | collective-permute-start | bytes 1572872 | tf_op jit(solution)/shard_map/side_far/ppermute | solution.py:33
  9.7 1.0 %copy-start.1 = (bf16[1,2,2,128,256]{4,3,2,1,0:T(8,128)(2,1)S(1)}, bf16[1,2,2,128,256]{4,3,2,1,0:T(8,128)(2,1)}, u32[]{:S(2)}) copy-start(bf16[1,2,2,128,256]{4,3,2,1,0:T(8,128)(2,1)} %param.11) | copy-start | bytes 786436
  11.6 10.8 %collective-permute-start.2 = (bf16[2,256,256]{2,1,0:T(8,128)(2,1)S(1)}, bf16[2,256,256]{2,1,0:T(8,128)(2,1)S(1)}, u32[]{:S(2)}, u32[]{:S(2)}) collective-permute-start(bf16[2,256,256]{2,1,0:T(8,128)(2,1)S(1)} %shard_map.64.a_ref), channel_id=1, source_target_pairs={{0,16},{1,49},{16,32},{17,1},{32,48},{33,17},{48,0},{49,33},{2,18}... | collective-permute-start | bytes 786440 | tf_op jit(solution)/shard_map/near/ppermute | solution.py:33
  15.4 13.2 %collective-permute-start.7 = (bf16[2,2,256,256]{3,2,1,0:T(8,128)(2,1)S(1)}, bf16[2,2,256,256]{3,2,1,0:T(8,128)(2,1)S(1)}, u32[]{:S(2)}, u32[]{:S(2)}) collective-permute-start(bf16[2,2,256,256]{3,2,1,0:T(8,128)(2,1)S(1)} %collective-permute-done.5.refs_5_), channel_id=1, source_target_pairs={{0,4},{1,13},{16,20},{17,29},{32,36},{33,45},{48,52},{49,61},{2,6}... | collective-permute-start | bytes 1572872 | tf_op jit(solution)/shard_map/across/ppermute | solution.py:33
  16.9 11.7 %collective-permute-start.8 = (bf16[2,2,256,256]{3,2,1,0:T(8,128)(2,1)S(1)}, bf16[2,2,256,256]{3,2,1,0:T(8,128)(2,1)S(1)}, u32[]{:S(2)}, u32[]{:S(2)}) collective-permute-start(bf16[2,2,256,256]{3,2,1,0:T(8,128)(2,1)S(1)} %collective-permute-done.5.refs_5_), channel_id=1, source_target_pairs={{0,2},{1,67},{16,18},{17,83},{32,34},{33,99},{48,50},{49,115},{2,6... | collective-permute-start | bytes 1572872 | tf_op jit(solution)/shard_map/side_turned/ppermute | solution.py:33
  18.8 8.5 %collective-permute-start.4 = (bf16[2,256,256]{2,1,0:T(8,128)(2,1)S(1)}, bf16[2,256,256]{2,1,0:T(8,128)(2,1)S(1)}, u32[]{:S(2)}, u32[]{:S(2)}) collective-permute-start(bf16[2,256,256]{2,1,0:T(8,128)(2,1)S(1)} %shard_map.64.a_ref), channel_id=1, source_target_pairs={{0,32},{1,33},{16,48},{17,49},{32,0},{33,1},{48,16},{49,17},{2,34}... | collective-permute-start | bytes 786440 | tf_op jit(solution)/shard_map/opposite/ppermute | solution.py:33
  22.4 4.9 %collective-permute-start.3 = (bf16[2,256,256]{2,1,0:T(8,128)(2,1)S(1)}, bf16[2,256,256]{2,1,0:T(8,128)(2,1)S(1)}, u32[]{:S(2)}, u32[]{:S(2)}) collective-permute-start(bf16[2,256,256]{2,1,0:T(8,128)(2,1)S(1)} %collective-permute-done.2.b_ref), channel_id=1, source_target_pairs={{0,1},{1,0},{16,17},{17,16},{32,33},{33,32},{48,49},{49,48},{2,3},... | collective-permute-start | bytes 786440 | tf_op jit(solution)/shard_map/near_other/ppermute | solution.py:33
  22.4 12.2 %collective-permute-start.15 = (bf16[2,2,256,256]{3,2,1,0:T(8,128)(2,1)S(1)}, bf16[2,2,256,256]{3,2,1,0:T(8,128)(2,1)S(1)}, u32[]{:S(2)}, u32[]{:S(2)}) collective-permute-start(bf16[2,2,256,256]{3,2,1,0:T(8,128)(2,1)S(1)} %collective-permute-done.11.refs_9_), channel_id=1, source_target_pairs={{0,2},{1,67},{16,18},{17,83},{32,34},{33,99},{48,50},{49,115},{2,6... | collective-permute-start | bytes 1572872 | tf_op jit(solution)/shard_map/side_far_turned/ppermute | solution.py:33
  28.6 9.5 %collective-permute-start.17 = (bf16[2,2,256,256]{3,2,1,0:T(8,128)(2,1)S(1)}, bf16[2,2,256,256]{3,2,1,0:T(8,128)(2,1)S(1)}, u32[]{:S(2)}, u32[]{:S(2)}) collective-permute-start(bf16[2,2,256,256]{3,2,1,0:T(8,128)(2,1)S(1)} %collective-permute-done.8.refs_11_), channel_id=1, source_target_pairs={{0,4},{1,13},{16,20},{17,29},{32,36},{33,45},{48,52},{49,61},{2,6}... | collective-permute-start | bytes 1572872 | tf_op jit(solution)/shard_map/across_turned/ppermute | solution.py:33
  33.9 4.4 %collective-permute-start.9 = (bf16[2,2,256,256]{3,2,1,0:T(8,128)(2,1)S(1)}, bf16[2,2,256,256]{3,2,1,0:T(8,128)(2,1)S(1)}, u32[]{:S(2)}, u32[]{:S(2)}) collective-permute-start(bf16[2,2,256,256]{3,2,1,0:T(8,128)(2,1)S(1)} %collective-permute-done.5.refs_5_), channel_id=1, source_target_pairs={{0,1},{1,0},{16,17},{17,16},{32,33},{33,32},{48,49},{49,48},{2,3},... | collective-permute-start | bytes 1572872 | tf_op jit(solution)/shard_map/shared/ppermute | solution.py:33
  34.1 4.6 %collective-permute-start.10 = (bf16[2,2,256,256]{3,2,1,0:T(8,128)(2,1)S(1)}, bf16[2,2,256,256]{3,2,1,0:T(8,128)(2,1)S(1)}, u32[]{:S(2)}, u32[]{:S(2)}) collective-permute-start(bf16[2,2,256,256]{3,2,1,0:T(8,128)(2,1)S(1)} %collective-permute-done.6.refs_7_), channel_id=1, source_target_pairs={{0,1},{1,0},{16,17},{17,16},{32,33},{33,32},{48,49},{49,48},{2,3},... | collective-permute-start | bytes 1572872 | tf_op jit(solution)/shard_map/shared/ppermute | solution.py:33
  34.5 4.3 %collective-permute-start.12 = (bf16[2,2,256,256]{3,2,1,0:T(8,128)(2,1)S(1)}, bf16[2,2,256,256]{3,2,1,0:T(8,128)(2,1)S(1)}, u32[]{:S(2)}, u32[]{:S(2)}) collective-permute-start(bf16[2,2,256,256]{3,2,1,0:T(8,128)(2,1)S(1)} %collective-permute-done.11.refs_9_), channel_id=1, source_target_pairs={{0,1},{1,0},{16,17},{17,16},{32,33},{33,32},{48,49},{49,48},{2,3},... | collective-permute-start | bytes 1572872 | tf_op jit(solution)/shard_map/shared/ppermute | solution.py:33
  34.6 6.8 %collective-permute-start.13 = (bf16[2,2,256,256]{3,2,1,0:T(8,128)(2,1)S(1)}, bf16[2,2,256,256]{3,2,1,0:T(8,128)(2,1)S(1)}, u32[]{:S(2)}, u32[]{:S(2)}) collective-permute-start(bf16[2,2,256,256]{3,2,1,0:T(8,128)(2,1)S(1)} %collective-permute-done.8.refs_11_), channel_id=1, source_target_pairs={{0,1},{1,0},{16,17},{17,16},{32,33},{33,32},{48,49},{49,48},{2,3},... | collective-permute-start | bytes 1572872 | tf_op jit(solution)/shard_map/shared/ppermute | solution.py:33
  38.1 3.3 %collective-permute-start.14 = (bf16[2,2,256,256]{3,2,1,0:T(8,128)(2,1)S(1)}, bf16[2,2,256,256]{3,2,1,0:T(8,128)(2,1)S(1)}, u32[]{:S(2)}, u32[]{:S(2)}) collective-permute-start(bf16[2,2,256,256]{3,2,1,0:T(8,128)(2,1)S(1)} %collective-permute-done.7.refs_13_), channel_id=1, source_target_pairs={{0,1},{1,0},{16,17},{17,16},{32,33},{33,32},{48,49},{49,48},{2,3},... | collective-permute-start | bytes 1572872 | tf_op jit(solution)/shard_map/shared/ppermute | solution.py:33
  38.3 3.1 %collective-permute-start.16 = (bf16[2,2,256,256]{3,2,1,0:T(8,128)(2,1)S(1)}, bf16[2,2,256,256]{3,2,1,0:T(8,128)(2,1)S(1)}, u32[]{:S(2)}, u32[]{:S(2)}) collective-permute-start(bf16[2,2,256,256]{3,2,1,0:T(8,128)(2,1)S(1)} %collective-permute-done.15.refs_15_), channel_id=1, source_target_pairs={{0,1},{1,0},{16,17},{17,16},{32,33},{33,32},{48,49},{49,48},{2,3},... | collective-permute-start | bytes 1572872 | tf_op jit(solution)/shard_map/shared/ppermute | solution.py:33
  38.7 2.9 %collective-permute-start.18 = (bf16[2,2,256,256]{3,2,1,0:T(8,128)(2,1)S(1)}, bf16[2,2,256,256]{3,2,1,0:T(8,128)(2,1)S(1)}, u32[]{:S(2)}, u32[]{:S(2)}) collective-permute-start(bf16[2,2,256,256]{3,2,1,0:T(8,128)(2,1)S(1)} %collective-permute-done.17.refs_17_), channel_id=1, source_target_pairs={{0,1},{1,0},{16,17},{17,16},{32,33},{33,32},{48,49},{49,48},{2,3},... | collective-permute-start | bytes 1572872 | tf_op jit(solution)/shard_map/shared/ppermute | solution.py:33
  38.8 9.3 %collective-permute-start.19 = (bf16[2,256,256]{2,1,0:T(8,128)(2,1)S(1)}, bf16[2,256,256]{2,1,0:T(8,128)(2,1)S(1)}, u32[]{:S(2)}, u32[]{:S(2)}) collective-permute-start(bf16[2,256,256]{2,1,0:T(8,128)(2,1)S(1)} %shard_map.65), channel_id=1, source_target_pairs={{0,64},{1,65},{16,80},{17,81},{32,96},{33,97},{48,112},{49,113},{2... | collective-permute-start | bytes 786440 | tf_op jit(solution)/shard_map/far/ppermute | solution.py:33
